TPU v7x, 32 devices: a whole 2x2x4 slice. The times are simulated.
32 devices in a mesh: grp: 2 (over y), frm: 4 (over z), head: 2 (over x), pos: 2 (over core).
Axes of the slice: x: 2, y: 2, z: 4, core: 2. Of those that a mesh axis runs over, the one named last changes fastest.
Arguments:
- queries: float32 [32, 128, 3072], P(('grp', 'frm'), 'pos', 'head'), parts along dimension 0, may hold values from -120 to 120
- key_states: float32 [32, 128, 3072], P(('grp', 'frm'), 'pos', 'head'), parts along dimension 0, may hold values from -4 to 4
- value_states: float32 [32, 128, 3072], P(('grp', 'frm'), 'pos', 'head'), parts along dimension 0, may hold values from -6 to 6
- windows: int32 [24], P('head'), may hold values from 1 to 2, as said below
- strides: int32 [24], P('head'), may hold values from 4 to 8, as said below
- cutoffs: int32 [24], P('head'), may hold values from 1 to 2, as said below
Outputs:
- blended: float32 [32, 128, 3072], P(('grp', 'frm'), 'pos', 'head'), parts along dimension 0
There are 2 independent parts, one for each index of `grp`. A program takes and returns all parts, laid end to end along the dimension named above; an argument that names none is the same for every part. Nothing has to cross between parts.
Inputs may be any that keep to these rules, and one draw needn't show every extreme that they name: `windows`: some head has exactly 2. `strides`: each is 4 or 8, and both occur. `cutoffs`: some head has exactly 2.
All inputs are finite; a program needn't handle non-finite values.
Results may differ from a plain program's by a relative error of at most 0.0003.
Values sent between devices are 32-bit elements; how exact they have to be, the bound alone decides.
No kernel may reach another device: no remote copies, remote signals or barrier semaphores. Data moves between devices by JAX's collectives and lax.ppermute only.
A program may use at most 128 MiB of HBM per device.

v0:
```python
import functools
import math

import jax
import jax.numpy as jnp
import numpy as np
from jax import lax
from jax.experimental import pallas as pl
from jax.experimental.pallas import tpu as pltpu
from jax.sharding import PartitionSpec as P


DH = 128
KSTRIDE = 4
WMAX = 2
MASKED = -1e30


def lowpass_table(frames):
    cutoff = np.arange(frames // 2 + 1)
    freq = np.arange(frames)
    keep = (np.minimum(freq, frames - freq)[None, :] <= cutoff[:, None]).astype(np.float64)
    waves = np.cos(2.0 * np.pi / frames * (np.outer(freq, freq) % frames))
    return (keep @ waves / frames).astype(np.float32)


def pack_kernel(slot, parts, per_part, *refs):
    sources, outs = refs[:3], refs[3 : 3 + parts]
    held, load_sem, store_sem = refs[3 + parts :]
    me = lax.axis_index("frm")
    order = [*range(1, parts), 0]
    loads, stores = {}, {}
    for hop in order:
        owner = lax.rem(me + hop, parts)
        columns = pl.ds(pl.multiple_of((owner * per_part + slot) * DH, DH), DH)
        for at in range(3):
            loads[hop, at] = pltpu.make_async_copy(
                sources[at].at[:, :, columns], held.at[hop, at], load_sem.at[hop, at]
            )
            loads[hop, at].start()
    for hop in order:
        for at in range(3):
            loads[hop, at].wait()
        stores[hop] = pltpu.make_async_copy(held.at[hop], outs[hop], store_sem.at[hop])
        stores[hop].start()
    for hop in order:
        stores[hop].wait()


def pack(slot, parts, queries, key_states, value_states):
    frames_dev, rows, channels = queries.shape
    piece = (3, frames_dev, rows, DH)
    moved = parts * math.prod(piece) * 4
    return pl.pallas_call(
        functools.partial(pack_kernel, slot, parts, channels // DH // parts),
        out_shape=[jax.ShapeDtypeStruct(piece, jnp.float32)] * parts,
        in_specs=[pl.BlockSpec(memory_space=pl.ANY)] * 3,
        out_specs=[pl.BlockSpec(memory_space=pl.ANY)] * parts,
        scratch_shapes=[
            pltpu.VMEM((parts, *piece), jnp.float32),
            pltpu.SemaphoreType.DMA((parts, 3)),
            pltpu.SemaphoreType.DMA((parts,)),
        ],
        cost_estimate=pl.CostEstimate(flops=0, bytes_accessed=2 * moved, transcendentals=0),
    )(queries, key_states, value_states)


def split(value):
    high = value.astype(jnp.bfloat16)
    return high, (value - high.astype(jnp.float32)).astype(jnp.bfloat16)


def weighted(scores, values):
    highest = jnp.max(scores, axis=1, keepdims=True)
    weights = jnp.exp(scores - highest)
    total = jnp.sum(weights, axis=1, keepdims=True)
    high, low = split(weights)
    wide = jnp.dot(high, values, preferred_element_type=jnp.float32)
    rest = jnp.dot(low, values[:, :DH], preferred_element_type=jnp.float32)
    return (wide[:, :DH] + wide[:, DH:] + rest) / total


def attend_kernel(slot, parts, per_part, *refs):
    windows, strides, cutoffs, table = refs[:4]
    mine, theirs = refs[4 : 4 + parts], refs[4 + parts : 4 + 2 * parts]
    outs = refs[4 + 2 * parts : 4 + 3 * parts]
    (q_in, k_in, v_in, q_cat, k_cat, v_cat, kg_cat, vg_cat, local, diff, load_sem, store_sem) = refs[
        4 + 3 * parts :
    ]
    frames, rows, _ = q_in.shape
    tokens = k_in.shape[1]
    frames_dev = frames // parts
    me = lax.axis_index("frm")
    head = me * per_part + slot
    window, stride, cutoff = windows[head], strides[head], cutoffs[head]

    loads = []
    for hop in range(parts):
        owner = lax.rem(me + parts - hop, parts)
        span = pl.ds(owner * frames_dev, frames_dev)
        near, far = pl.ds(0, rows), pl.ds(rows, rows)
        for at, (source, target) in enumerate(
            (
                (mine[hop].at[0], q_in.at[span]),
                (mine[hop].at[1], k_in.at[span, near]),
                (mine[hop].at[2], v_in.at[span, near]),
                (theirs[hop].at[1], k_in.at[span, far]),
                (theirs[hop].at[2], v_in.at[span, far]),
            )
        ):
            copy = pltpu.make_async_copy(source, target, load_sem.at[hop, at])
            copy.start()
            loads.append(copy)
    for copy in loads:
        copy.wait()

    score_scale = DH ** (-0.5)

    def prepare(frame, carry):
        q_at = pl.ds(pl.multiple_of(frame * rows, rows), rows)
        k_at = pl.ds(pl.multiple_of(frame * tokens, tokens), tokens)
        high, low = split(q_in[frame] * score_scale)
        q_cat[q_at, 0:DH] = high
        q_cat[q_at, DH : 2 * DH] = low
        q_cat[q_at, 2 * DH : 3 * DH] = high
        k_high, k_low = split(k_in[frame])
        k_cat[k_at, 0:DH] = k_high
        k_cat[k_at, DH : 2 * DH] = k_high
        k_cat[k_at, 2 * DH : 3 * DH] = k_low
        v_high, v_low = split(v_in[frame])
        v_cat[k_at, 0:DH] = v_high
        v_cat[k_at, DH : 2 * DH] = v_low
        return carry

    lax.fori_loop(0, frames, prepare, 0)
    key_frames = frames // KSTRIDE
    for at in range(key_frames):
        source = pl.ds(at * KSTRIDE * tokens, tokens)
        target = pl.ds(at * tokens, tokens)
        kg_cat[target, :] = k_cat[source, :]
        vg_cat[target, :] = v_cat[source, :]

    def scores_of(query_rows, key_rows):
        return lax.dot_general(
            query_rows, key_rows, (((1,), (1,)), ((), ())), preferred_element_type=jnp.float32
        )

    pair = 2
    reach = min(2 * WMAX + pair, frames)
    pair_rows = pair * rows
    key_frame = lax.broadcasted_iota(jnp.int32, (1, key_frames * tokens), 1) // tokens * KSTRIDE
    global_bias = jnp.where(lax.rem(key_frame, stride) == 0, 0.0, MASKED)

    def per_pair(step, carry):
        first = step * pair
        start = jnp.clip(first - WMAX, 0, frames - reach)
        q_part = q_cat[pl.ds(pl.multiple_of(first * rows, pair_rows), pair_rows), :]
        k_at = pl.ds(pl.multiple_of(start * tokens, tokens), reach * tokens)
        near_frame = start + lax.broadcasted_iota(jnp.int32, (pair_rows, reach * tokens), 1) // tokens
        query_frame = first + lax.broadcasted_iota(jnp.int32, (pair_rows, reach * tokens), 0) // rows
        scores = scores_of(q_part, k_cat[k_at, :])
        scores = jnp.where(jnp.abs(near_frame - query_frame) <= window, scores, MASKED)
        local_part = weighted(scores, v_cat[k_at, :])
        global_part = weighted(scores_of(q_part, kg_cat[...]) + global_bias, vg_cat[...])
        difference = global_part - local_part
        for at in range(pair):
            local[first + at] = local_part[at * rows : (at + 1) * rows]
            diff[first + at] = difference[at * rows : (at + 1) * rows]
        return carry

    lax.fori_loop(0, frames // pair, per_pair, 0)

    kept = jnp.clip(cutoff, 0, frames // 2)

    def blend(frame, carry):
        total = local[frame]
        for other in range(frames):
            total += table[kept, lax.rem(frame + frames - other, frames)] * diff[other]
        q_in[frame] = total
        return carry

    lax.fori_loop(0, frames, blend, 0)
    stores = []
    for hop in range(parts):
        owner = lax.rem(me + hop, parts)
        stores.append(
            pltpu.make_async_copy(
                q_in.at[pl.ds(owner * frames_dev, frames_dev)], outs[hop], store_sem.at[hop]
            )
        )
        stores[-1].start()
    for copy in stores:
        copy.wait()


def attend_head(slot, parts, scalars, table, mine, theirs):
    _, frames_dev, rows, _ = mine[0].shape
    frames, tokens = frames_dev * parts, 2 * rows
    per_part = scalars[0].shape[0] // parts
    key_frames = frames // KSTRIDE
    flops = 12 * frames * rows * (5 + key_frames) * tokens * DH
    return pl.pallas_call(
        functools.partial(attend_kernel, slot, parts, per_part),
        out_shape=[jax.ShapeDtypeStruct((frames_dev, rows, DH), jnp.float32)] * parts,
        in_specs=[pl.BlockSpec(memory_space=pltpu.SMEM)] * 4
        + [pl.BlockSpec(memory_space=pl.ANY)] * (2 * parts),
        out_specs=[pl.BlockSpec(memory_space=pl.ANY)] * parts,
        scratch_shapes=[
            pltpu.VMEM((frames, rows, DH), jnp.float32),
            pltpu.VMEM((frames, tokens, DH), jnp.float32),
            pltpu.VMEM((frames, tokens, DH), jnp.float32),
            pltpu.VMEM((frames * rows, 3 * DH), jnp.bfloat16),
            pltpu.VMEM((frames * tokens, 3 * DH), jnp.bfloat16),
            pltpu.VMEM((frames * tokens, 2 * DH), jnp.bfloat16),
            pltpu.VMEM((key_frames * tokens, 3 * DH), jnp.bfloat16),
            pltpu.VMEM((key_frames * tokens, 2 * DH), jnp.bfloat16),
            pltpu.VMEM((frames, rows, DH), jnp.float32),
            pltpu.VMEM((frames, rows, DH), jnp.float32),
            pltpu.SemaphoreType.DMA((parts, 5)),
            pltpu.SemaphoreType.DMA((parts,)),
        ],
        cost_estimate=pl.CostEstimate(
            flops=flops,
            bytes_accessed=6 * frames * rows * DH * 4,
            transcendentals=frames * rows * (5 + key_frames) * tokens,
        ),
    )(*scalars, table, *mine, *theirs)


def unpack_kernel(parts, per_part, *refs):
    count = parts * per_part
    pieces, out = refs[:count], refs[count]
    held, load_sem, store_sem = refs[count + 1 :]
    me = lax.axis_index("frm")
    loads, stores = [], []
    for at in range(count):
        loads.append(pltpu.make_async_copy(pieces[at], held.at[at], load_sem.at[at]))
        loads[-1].start()
    for at in range(count):
        slot, hop = at // parts, at % parts
        owner = lax.rem(me + parts - hop, parts)
        columns = pl.ds(pl.multiple_of((owner * per_part + slot) * DH, DH), DH)
        loads[at].wait()
        stores.append(pltpu.make_async_copy(held.at[at], out.at[:, :, columns], store_sem.at[at]))
        stores[-1].start()
    for copy in stores:
        copy.wait()


def unpack(parts, pieces):
    frames_dev, rows, _ = pieces[0].shape
    count = len(pieces)
    return pl.pallas_call(
        functools.partial(unpack_kernel, parts, count // parts),
        out_shape=jax.ShapeDtypeStruct((frames_dev, rows, count * DH), jnp.float32),
        in_specs=[pl.BlockSpec(memory_space=pl.ANY)] * count,
        out_specs=pl.BlockSpec(memory_space=pl.ANY),
        scratch_shapes=[
            pltpu.VMEM((count, frames_dev, rows, DH), jnp.float32),
            pltpu.SemaphoreType.DMA((count,)),
            pltpu.SemaphoreType.DMA((count,)),
        ],
        name="unpack",
    )(*pieces)


def around(value, hop):
    size = lax.axis_size("frm")
    return lax.ppermute(value, "frm", [(i, (i + hop) % size) for i in range(size)])


def swap(value):
    size = lax.axis_size("pos")
    return lax.ppermute(value, "pos", [(i, size - 1 - i) for i in range(size)])


def by_heads(queries, key_states, value_states, windows, strides, cutoffs):
    parts = lax.axis_size("frm")
    per_part = queries.shape[2] // DH // parts
    frames = queries.shape[0] * parts
    table = jnp.asarray(lowpass_table(frames))
    scalars = (windows, strides, cutoffs)
    packed, sources, moved, pieces = [], (queries, key_states, value_states), [], []
    for slot in range(per_part):
        packed.append(pack(slot, parts, *sources))
        packed[-1], sources = lax.optimization_barrier((packed[-1], sources))
        moved.append([packed[-1][0]])
        for hop in range(1, parts):
            moved[-1].append(around(packed[-1][hop], hop))
    for slot, mine in enumerate(moved):
        theirs = []
        for hop in range(parts):
            theirs.append(swap(mine[hop]))
        done = attend_head(slot, parts, scalars, table, mine, theirs)
        pieces.append(done[0])
        for hop in range(1, parts):
            pieces.append(around(done[hop], hop))
    return unpack(parts, pieces)


def with_halo(value, sides, width):
    for axis, dim in sides:
        size, length = (lax.axis_size(axis), value.shape[dim])
        up = [(i, (i + 1) % size) for i in range(size - 1)]
        down = [(j, i) for i, j in up]
        last = lax.slice_in_dim(value, length - width, length, axis=dim)
        first = lax.slice_in_dim(value, 0, width, axis=dim)
        before = lax.ppermute(last, axis, up)
        after = lax.ppermute(first, axis, down)
        value = jnp.concatenate([before, value, after], axis=dim)
    return value


def attend(query_rows, key_rows, value_rows, allowed, score_scale):
    scores = (
        jnp.einsum("qhd,khd->hqk", query_rows, key_rows, precision=lax.Precision.HIGHEST)
        * score_scale
    )
    highest = jnp.max(jnp.where(allowed, scores, -1e30), axis=2, keepdims=True)
    weights = jnp.where(allowed, jnp.exp(scores - highest), 0.0)
    row_total = jnp.sum(weights, axis=2, keepdims=True)
    return jnp.einsum(
        "hqk,khd->qhd", weights / row_total, value_rows, precision=lax.Precision.HIGHEST
    )


def by_frames(queries, key_states, value_states, windows, strides, cutoffs):
    frames_dev, half_tokens, channels = queries.shape
    heads_local = channels // DH
    frame_groups = lax.axis_size("frm")
    pos_count = lax.axis_size("pos")
    total_frames = frames_dev * frame_groups
    halo_frames = frames_dev // 2
    score_scale = DH ** (-0.5)
    query_count = frames_dev * half_tokens
    query_rows = queries.reshape(query_count, heads_local, DH)
    query_blocks = queries.reshape(frames_dev, half_tokens, heads_local, DH)
    first_frame = lax.axis_index("frm") * frames_dev
    key_full, value_full = (
        lax.all_gather(key_states, "pos", axis=1, tiled=True),
        lax.all_gather(value_states, "pos", axis=1, tiled=True),
    )
    full_tokens = key_full.shape[1]
    stacked = jnp.stack([key_full, value_full])
    padded = with_halo(stacked, (("frm", 1),), halo_frames)
    window_span = 2 * halo_frames + 1
    span_rows = window_span * full_tokens
    span_offsets = jnp.arange(span_rows, dtype=jnp.int32) // full_tokens - halo_frames

    def local_frame(frame_local):
        query_part = lax.dynamic_index_in_dim(query_blocks, frame_local, 0, keepdims=False)
        block = lax.dynamic_slice_in_dim(padded, frame_local, window_span, 1)
        near_keys = block[0].reshape(span_rows, heads_local, DH)
        near_values = block[1].reshape(span_rows, heads_local, DH)
        near_frames = first_frame + frame_local + span_offsets
        inside = (near_frames >= 0) & (near_frames < total_frames)
        allowed = inside[None, None, :] & (
            jnp.abs(span_offsets)[None, None, :] <= windows[:, None, None]
        )
        return attend(query_part, near_keys, near_values, allowed, score_scale)

    local_out = lax.map(local_frame, jnp.arange(frames_dev, dtype=jnp.int32)).reshape(
        query_count, heads_local, DH
    )
    frame_keys = key_states[::KSTRIDE].reshape(-1, heads_local, DH)
    frame_values = value_states[::KSTRIDE].reshape(-1, heads_local, DH)
    rows_dev = frame_keys.shape[0]
    key_part = lax.all_gather(frame_keys, ("frm", "pos"), axis=0, tiled=True)
    value_part = lax.all_gather(frame_values, ("frm", "pos"), axis=0, tiled=True)
    row_count = key_part.shape[0]
    row_ids = jnp.arange(row_count, dtype=jnp.int32)
    frame_ids = (
        row_ids // rows_dev // pos_count * frames_dev + row_ids % rows_dev // half_tokens * KSTRIDE
    )
    allowed = (frame_ids[None, :] % strides[:, None] == 0)[:, None, :]
    scores = (
        jnp.einsum("qhd,khd->hqk", query_rows, key_part, precision=lax.Precision.HIGHEST)
        * score_scale
    )
    top_old = jnp.full((heads_local, query_count), -1e30, jnp.float32)
    top_new = jnp.maximum(top_old, jnp.max(jnp.where(allowed, scores, -1e30), axis=2))
    weights = jnp.where(allowed, jnp.exp(scores - top_new[:, :, None]), 0.0)
    total_new = jnp.sum(weights, axis=2)
    accum_new = jnp.einsum("hqk,khd->hqd", weights, value_part, precision=lax.Precision.HIGHEST)
    final_state = (top_new, total_new, accum_new)
    _, total_final, accum_final = final_state
    global_out = jnp.transpose(accum_final / total_final[:, :, None], (1, 0, 2))
    frequency = jnp.arange(total_frames, dtype=jnp.int32)
    phase_index = frequency[:, None] * frequency[None, :] % total_frames
    phases = 2.0 * math.pi / total_frames * phase_index.astype(jnp.float32)
    cos_table = jnp.cos(phases)
    sin_table = jnp.sin(phases)
    distance_freq = jnp.minimum(frequency, total_frames - frequency)
    low_keep = (distance_freq[None, :] <= cutoffs[:, None]).astype(jnp.float32)
    lowpass = (
        jnp.einsum("kf,hk,kg->hfg", cos_table, low_keep, cos_table, precision=lax.Precision.HIGHEST)
        + jnp.einsum(
            "kf,hk,kg->hfg", sin_table, low_keep, sin_table, precision=lax.Precision.HIGHEST
        )
    ) / total_frames
    group_items = half_tokens // frame_groups
    local_grid = local_out.reshape(frames_dev, frame_groups, group_items, channels)
    global_grid = global_out.reshape(frames_dev, frame_groups, group_items, channels)
    frame_block = lax.all_to_all(
        global_grid - local_grid, "frm", split_axis=1, concat_axis=0, tiled=True
    )
    frames_all = frame_block.shape[0]
    item_count = frame_block.shape[2]
    shaped = frame_block.reshape(frames_all, item_count, heads_local, DH)
    filtered_block = jnp.einsum(
        "hfg,gihd->fihd", lowpass, shaped, precision=lax.Precision.HIGHEST
    ).reshape(frame_block.shape)
    filtered = lax.all_to_all(filtered_block, "frm", split_axis=0, concat_axis=1, tiled=True)
    blended = local_grid + filtered
    return blended.reshape(frames_dev, half_tokens, channels)


def splits_by_heads(heads_local, parts, pos_count):
    return heads_local % parts == 0 and pos_count == 2


def shards(queries, key_states, value_states, windows, strides, cutoffs):
    heads_local = queries.shape[2] // DH
    if splits_by_heads(heads_local, lax.axis_size("frm"), lax.axis_size("pos")):
        return by_heads(queries, key_states, value_states, windows, strides, cutoffs)
    return by_frames(queries, key_states, value_states, windows, strides, cutoffs)


def solution(mesh):
    in_specs = (
        P(("grp", "frm"), "pos", "head"),
        P(("grp", "frm"), "pos", "head"),
        P(("grp", "frm"), "pos", "head"),
        P("head"),
        P("head"),
        P("head"),
    )
    out_specs = P(("grp", "frm"), "pos", "head")
    return jax.shard_map(
        shards, mesh=mesh, in_specs=in_specs, out_specs=out_specs, check_vma=False
    )
```

profile of v0, /device:TPU:0, one launch (start us, length us, event | category | flops | bytes accessed | tf_op | source)
XLA Modules:
  0.0 180.0 jit_solution(6959417726630432810)
XLA Ops:
  0.0 2.4 %shard_map.73 = (f32[3,4,64,128]{3,2,1,0:T(8,128)}, f32[3,4,64,128]{3,2,1,0:T(8,128)}, f32[3,4,64,128]{3,2,1,0:T(8,128)}, f32[3,4,64,128]{3,2,1,0:T(8,128)}) custom-call(f32[4,64,1536]{2,1,0:T(8,128)} %refs_0_.8, f32[4,64,1536]{2,1,0:T(8,128)} %refs_1_.8, f32[4,64,1536]{2,1,0:T(8,128)} %refs_2_.8), custom_call_target="tpu_custom_call" | custom-call | bytes 3145728 | tf_op jit(solution)/shard_map/pallas_call | solution.py:54
  2.4 3.1 %collective-permute-start = (f32[3,4,64,128]{3,2,1,0:T(8,128)}, f32[3,4,64,128]{3,2,1,0:T(8,128)S(1)}, u32[]{:S(2)}, u32[]{:S(2)}) collective-permute-start(f32[3,4,64,128]{3,2,1,0:T(8,128)} %get-tuple-element.52), channel_id=1, source_target_pairs={{0,4},{4,8},{8,12},{12,0},{1,5},{5,9},{9,13},{13,1},{2,6},{6,10},{... | collective-permute-start | bytes 1179656 | tf_op jit(solution)/shard_map/ppermute | solution.py:269
  5.5 2.6 %collective-permute-start.1 = (f32[3,4,64,128]{3,2,1,0:T(8,128)}, f32[3,4,64,128]{3,2,1,0:T(8,128)S(1)}, u32[]{:S(2)}, u32[]{:S(2)}) collective-permute-start(f32[3,4,64,128]{3,2,1,0:T(8,128)} %get-tuple-element.53), channel_id=1, source_target_pairs={{0,8},{4,12},{8,0},{12,4},{1,9},{5,13},{9,1},{13,5},{2,10},{6,14},... | collective-permute-start | bytes 1179656 | tf_op jit(solution)/shard_map/ppermute | solution.py:269
  8.1 1.3 collective-permute-start.2
  9.4 0.0 collective-permute-start.3
  9.4 2.4 %shard_map.75 = (f32[3,4,64,128]{3,2,1,0:T(8,128)}, f32[3,4,64,128]{3,2,1,0:T(8,128)}, f32[3,4,64,128]{3,2,1,0:T(8,128)}, f32[3,4,64,128]{3,2,1,0:T(8,128)}) custom-call(f32[4,64,1536]{2,1,0:T(8,128)} %refs_0_.8, f32[4,64,1536]{2,1,0:T(8,128)} %refs_1_.8, f32[4,64,1536]{2,1,0:T(8,128)} %refs_2_.8), custom_call_target="tpu_custom_call" | custom-call | bytes 3145728 | tf_op jit(solution)/shard_map/pallas_call | solution.py:54
  11.9 0.7 collective-permute-start.10
  12.6 5.2 %collective-permute-done.refs_5_ = f32[3,4,64,128]{3,2,1,0:T(8,128)S(1)} collective-permute-done((f32[3,4,64,128]{3,2,1,0:T(8,128)}, f32[3,4,64,128]{3,2,1,0:T(8,128)S(1)}, u32[]{:S(2)}, u32[]{:S(2)}) %collective-permute-start) | collective-permute-done | bytes 393248 | tf_op jit(solution)/shard_map/ppermute | solution.py:269
  17.8 17.8 %collective-permute-start.11 = (f32[3,4,64,128]{3,2,1,0:T(8,128)}, f32[3,4,64,128]{3,2,1,0:T(8,128)}, u32[]{:S(2)}, u32[]{:S(2)}) collective-permute-start(f32[3,4,64,128]{3,2,1,0:T(8,128)} %get-tuple-element.68), channel_id=1, source_target_pairs={{0,8},{4,12},{8,0},{12,4},{1,9},{5,13},{9,1},{13,5},{2,10},{6,14},... | collective-permute-start | bytes 1179656 | tf_op jit(solution)/shard_map/ppermute | solution.py:269
  35.6 0.0 collective-permute-done.1.refs_6_
  35.6 22.0 %collective-permute-start.12 = (f32[3,4,64,128]{3,2,1,0:T(8,128)}, f32[3,4,64,128]{3,2,1,0:T(8,128)}, u32[]{:S(2)}, u32[]{:S(2)}) collective-permute-start(f32[3,4,64,128]{3,2,1,0:T(8,128)} %get-tuple-element.69), channel_id=1, source_target_pairs={{0,12},{4,0},{8,4},{12,8},{1,13},{5,1},{9,5},{13,9},{2,14},{6,2},{... | collective-permute-start | bytes 1179656 | tf_op jit(solution)/shard_map/ppermute | solution.py:269
  57.5 2.4 %shard_map.77 = (f32[3,4,64,128]{3,2,1,0:T(8,128)}, f32[3,4,64,128]{3,2,1,0:T(8,128)}, f32[3,4,64,128]{3,2,1,0:T(8,128)}, f32[3,4,64,128]{3,2,1,0:T(8,128)}) custom-call(f32[4,64,1536]{2,1,0:T(8,128)} %refs_0_.8, f32[4,64,1536]{2,1,0:T(8,128)} %refs_1_.8, f32[4,64,1536]{2,1,0:T(8,128)} %refs_2_.8), custom_call_target="tpu_custom_call" | custom-call | bytes 3145728 | tf_op jit(solution)/shard_map/pallas_call | solution.py:54
  59.9 0.0 collective-permute-done.2.refs_7_
  60.0 0.1 collective-permute-start.13
  60.1 0.1 collective-permute-start.20
  60.1 0.0 collective-permute-done.10.refs_5_
  60.1 9.1 %collective-permute-start.21 = (f32[3,4,64,128]{3,2,1,0:T(8,128)}, f32[3,4,64,128]{3,2,1,0:T(8,128)S(1)}, u32[]{:S(2)}, u32[]{:S(2)}) collective-permute-start(f32[3,4,64,128]{3,2,1,0:T(8,128)} %get-tuple-element.83), channel_id=1, source_target_pairs={{0,8},{4,12},{8,0},{12,4},{1,9},{5,13},{9,1},{13,5},{2,10},{6,14},... | collective-permute-start | bytes 1179656 | tf_op jit(solution)/shard_map/ppermute | solution.py:269
  69.3 15.2 %collective-permute-done.11.refs_6_ = f32[3,4,64,128]{3,2,1,0:T(8,128)} collective-permute-done((f32[3,4,64,128]{3,2,1,0:T(8,128)}, f32[3,4,64,128]{3,2,1,0:T(8,128)}, u32[]{:S(2)}, u32[]{:S(2)}) %collective-permute-start.11) | collective-permute-done | bytes 393248 | tf_op jit(solution)/shard_map/ppermute | solution.py:269
  84.5 2.6 %collective-permute-start.22 = (f32[3,4,64,128]{3,2,1,0:T(8,128)}, f32[3,4,64,128]{3,2,1,0:T(8,128)}, u32[]{:S(2)}, u32[]{:S(2)}) collective-permute-start(f32[3,4,64,128]{3,2,1,0:T(8,128)} %get-tuple-element.84), channel_id=1, source_target_pairs={{0,12},{4,0},{8,4},{12,8},{1,13},{5,1},{9,5},{13,9},{2,14},{6,2},{... | collective-permute-start | bytes 1179656 | tf_op jit(solution)/shard_map/ppermute | solution.py:269
  87.2 0.5 collective-permute-start.5
  87.7 0.1 collective-permute-start.6
  87.8 13.5 %collective-permute-done.21.refs_6_ = f32[3,4,64,128]{3,2,1,0:T(8,128)S(1)} collective-permute-done((f32[3,4,64,128]{3,2,1,0:T(8,128)}, f32[3,4,64,128]{3,2,1,0:T(8,128)S(1)}, u32[]{:S(2)}, u32[]{:S(2)}) %collective-permute-start.21) | collective-permute-done | bytes 393248 | tf_op jit(solution)/shard_map/ppermute | solution.py:269
  101.3 2.9 %collective-permute-done.22.refs_7_ = f32[3,4,64,128]{3,2,1,0:T(8,128)} collective-permute-done((f32[3,4,64,128]{3,2,1,0:T(8,128)}, f32[3,4,64,128]{3,2,1,0:T(8,128)}, u32[]{:S(2)}, u32[]{:S(2)}) %collective-permute-start.22) | collective-permute-done | bytes 393248 | tf_op jit(solution)/shard_map/ppermute | solution.py:269
  104.2 0.5 collective-permute-start.16
  104.7 0.1 collective-permute-start.23
  104.8 0.4 collective-permute-start.24
  105.3 0.1 collective-permute-start.25
  105.4 0.7 collective-permute-done.15.refs_10_
  106.1 0.7 copy-done.23
  106.9 0.1 collective-permute-start.26
  107.0 14.2 %shard_map.74 = (f32[4,64,128]{2,1,0:T(8,128)}, f32[4,64,128]{2,1,0:T(8,128)}, f32[4,64,128]{2,1,0:T(8,128)}, f32[4,64,128]{2,1,0:T(8,128)}) custom-call(s32[12]{0:T(128)} %refs_0_.9, s32[12]{0:T(128)} %refs_1_.9, s32[12]{0:T(128)} %refs_2_.9, f32[9,16]{1,0:T(8,128)} %constant.2.clone.refs_3_, f32[3,4,64,128]{3,2,1,0:T(8,128)} %get-tuple-element.51.refs_4_, ...), custom_call_target="tpu_custom_call" | custom-call | flops 1811939328 | bytes 3145728 | tf_op jit(solution)/shard_map/pallas_call | solution.py:202
  121.3 6.2 %collective-permute-start.7 = (f32[4,64,128]{2,1,0:T(8,128)}, f32[4,64,128]{2,1,0:T(8,128)S(1)}, u32[]{:S(2)}, u32[]{:S(2)}) collective-permute-start(f32[4,64,128]{2,1,0:T(8,128)} %get-tuple-element.56), channel_id=1, source_target_pairs={{0,4},{4,8},{8,12},{12,0},{1,5},{5,9},{9,13},{13,1},{2,6},{6,10},{... | collective-permute-start | bytes 393224 | tf_op jit(solution)/shard_map/ppermute | solution.py:269
  127.5 14.2 %shard_map.76 = (f32[4,64,128]{2,1,0:T(8,128)}, f32[4,64,128]{2,1,0:T(8,128)}, f32[4,64,128]{2,1,0:T(8,128)}, f32[4,64,128]{2,1,0:T(8,128)}) custom-call(s32[12]{0:T(128)} %refs_0_.9, s32[12]{0:T(128)} %refs_1_.9, s32[12]{0:T(128)} %refs_2_.9, f32[9,16]{1,0:T(8,128)} %constant.2.clone.refs_3_, f32[3,4,64,128]{3,2,1,0:T(8,128)} %get-tuple-element.66.refs_4_, ...), custom_call_target="tpu_custom_call" | custom-call | flops 1811939328 | bytes 3145728 | tf_op jit(solution)/shard_map/pallas_call | solution.py:202
  141.7 0.0 copy-start.18
  141.7 1.9 %collective-permute-start.8 = (f32[4,64,128]{2,1,0:T(8,128)S(1)}, f32[4,64,128]{2,1,0:T(8,128)S(1)}, u32[]{:S(2)}, u32[]{:S(2)}) collective-permute-start(f32[4,64,128]{2,1,0:T(8,128)S(1)} %copy-done.27), channel_id=1, source_target_pairs={{0,8},{4,12},{8,0},{12,4},{1,9},{5,13},{9,1},{13,5},{2,10},{6,14},... | collective-permute-start | bytes 393224 | tf_op jit(solution)/shard_map/ppermute | solution.py:269
  143.6 0.8 collective-permute-start.9
  144.3 1.3 collective-permute-start.17
  145.6 1.1 collective-permute-start.18
  146.8 14.2 %shard_map.78 = (f32[4,64,128]{2,1,0:T(8,128)}, f32[4,64,128]{2,1,0:T(8,128)}, f32[4,64,128]{2,1,0:T(8,128)}, f32[4,64,128]{2,1,0:T(8,128)}) custom-call(s32[12]{0:T(128)} %refs_0_.9, s32[12]{0:T(128)} %refs_1_.9, s32[12]{0:T(128)} %refs_2_.9, f32[9,16]{1,0:T(8,128)} %constant.2.clone.refs_3_, f32[3,4,64,128]{3,2,1,0:T(8,128)} %get-tuple-element.81.refs_4_, ...), custom_call_target="tpu_custom_call" | custom-call | flops 1811939328 | bytes 3145728 | tf_op jit(solution)/shard_map/pallas_call | solution.py:202
  161.0 1.6 collective-permute-start.19
  162.6 0.5 collective-permute-start.27
  163.1 1.8 %collective-permute-start.28 = (f32[4,64,128]{2,1,0:T(8,128)}, f32[4,64,128]{2,1,0:T(8,128)S(1)}, u32[]{:S(2)}, u32[]{:S(2)}) collective-permute-start(f32[4,64,128]{2,1,0:T(8,128)} %get-tuple-element.87), channel_id=1, source_target_pairs={{0,8},{4,12},{8,0},{12,4},{1,9},{5,13},{9,1},{13,5},{2,10},{6,14},... | collective-permute-start | bytes 393224 | tf_op jit(solution)/shard_map/ppermute | solution.py:269
  164.9 2.5 %collective-permute-start.29 = (f32[4,64,128]{2,1,0:T(8,128)}, f32[4,64,128]{2,1,0:T(8,128)S(1)}, u32[]{:S(2)}, u32[]{:S(2)}) collective-permute-start(f32[4,64,128]{2,1,0:T(8,128)} %get-tuple-element.88), channel_id=1, source_target_pairs={{0,12},{4,0},{8,4},{12,8},{1,13},{5,1},{9,5},{13,9},{2,14},{6,2},{... | collective-permute-start | bytes 393224 | tf_op jit(solution)/shard_map/ppermute | solution.py:269
  167.4 3.7 %collective-permute-done.27.refs_9_ = f32[4,64,128]{2,1,0:T(8,128)S(1)} collective-permute-done((f32[4,64,128]{2,1,0:T(8,128)}, f32[4,64,128]{2,1,0:T(8,128)S(1)}, u32[]{:S(2)}, u32[]{:S(2)}) %collective-permute-start.27) | collective-permute-done | bytes 131104 | tf_op jit(solution)/shard_map/ppermute | solution.py:269
  171.1 5.9 %collective-permute-done.28.refs_10_ = f32[4,64,128]{2,1,0:T(8,128)S(1)} collective-permute-done((f32[4,64,128]{2,1,0:T(8,128)}, f32[4,64,128]{2,1,0:T(8,128)S(1)}, u32[]{:S(2)}, u32[]{:S(2)}) %collective-permute-start.28) | collective-permute-done | bytes 131104 | tf_op jit(solution)/shard_map/ppermute | solution.py:269
  177.1 0.6 copy-done.7
  177.6 0.1 copy-done.8
  177.7 2.3 %unpack.1 = f32[4,64,1536]{2,1,0:T(8,128)} custom-call(f32[4,64,128]{2,1,0:T(8,128)} %get-tuple-element.55.refs_0_, f32[4,64,128]{2,1,0:T(8,128)} %copy-done, f32[4,64,128]{2,1,0:T(8,128)} %copy-done.1, f32[4,64,128]{2,1,0:T(8,128)} %copy-done.2, f32[4,64,128]{2,1,0:T(8,128)} %get-tuple-element.70.refs_4_, f32[4,64,128]{2,1,0:T(8,128)} %copy-done.3, ...), custom_call_target="tpu_custom_call" | custom-call | tf_op jit(solution)/shard_map/unpack/pallas_call | solution.py:253
  (75 shorter events, 0.2 us)
Async XLA Ops:
  2.4 15.4 %collective-permute-start = (f32[3,4,64,128]{3,2,1,0:T(8,128)}, f32[3,4,64,128]{3,2,1,0:T(8,128)S(1)}, u32[]{:S(2)}, u32[]{:S(2)}) collective-permute-start(f32[3,4,64,128]{3,2,1,0:T(8,128)} %get-tuple-element.52), channel_id=1, source_target_pairs={{0,4},{4,8},{8,12},{12,0},{1,5},{5,9},{9,13},{13,1},{2,6},{6,10},{... | collective-permute-start | bytes 1179656 | tf_op jit(solution)/shard_map/ppermute | solution.py:269
  5.5 30.1 %collective-permute-start.1 = (f32[3,4,64,128]{3,2,1,0:T(8,128)}, f32[3,4,64,128]{3,2,1,0:T(8,128)S(1)}, u32[]{:S(2)}, u32[]{:S(2)}) collective-permute-start(f32[3,4,64,128]{3,2,1,0:T(8,128)} %get-tuple-element.53), channel_id=1, source_target_pairs={{0,8},{4,12},{8,0},{12,4},{1,9},{5,13},{9,1},{13,5},{2,10},{6,14},... | collective-permute-start | bytes 1179656 | tf_op jit(solution)/shard_map/ppermute | solution.py:269
  8.1 51.9 %collective-permute-start.2 = (f32[3,4,64,128]{3,2,1,0:T(8,128)}, f32[3,4,64,128]{3,2,1,0:T(8,128)S(1)}, u32[]{:S(2)}, u32[]{:S(2)}) collective-permute-start(f32[3,4,64,128]{3,2,1,0:T(8,128)} %get-tuple-element.54), channel_id=1, source_target_pairs={{0,12},{4,0},{8,4},{12,8},{1,13},{5,1},{9,5},{13,9},{2,14},{6,2},{... | collective-permute-start | bytes 1179656 | tf_op jit(solution)/shard_map/ppermute | solution.py:269
  9.4 50.6 %collective-permute-start.3 = (f32[3,4,64,128]{3,2,1,0:T(8,128)}, f32[3,4,64,128]{3,2,1,0:T(8,128)S(1)}, u32[]{:S(2)}, u32[]{:S(2)}) collective-permute-start(f32[3,4,64,128]{3,2,1,0:T(8,128)} %get-tuple-element.51.refs_4_), channel_id=1, source_target_pairs={{0,1},{1,0},{2,3},{3,2},{4,5},{5,4},{6,7},{7,6},{8,9},{9,8},{10,11... | collective-permute-start | bytes 1179656 | tf_op jit(solution)/shard_map/ppermute | solution.py:274
  11.9 48.1 %copy-start.10 = (f32[3,4,64,128]{3,2,1,0:T(8,128)S(1)}, f32[3,4,64,128]{3,2,1,0:T(8,128)}, u32[]{:S(2)}) copy-start(f32[3,4,64,128]{3,2,1,0:T(8,128)} %get-tuple-element.66.refs_4_) | copy-start | bytes 1179652
  11.9 48.3 %collective-permute-start.10 = (f32[3,4,64,128]{3,2,1,0:T(8,128)}, f32[3,4,64,128]{3,2,1,0:T(8,128)S(1)}, u32[]{:S(2)}, u32[]{:S(2)}) collective-permute-start(f32[3,4,64,128]{3,2,1,0:T(8,128)} %get-tuple-element.67), channel_id=1, source_target_pairs={{0,4},{4,8},{8,12},{12,0},{1,5},{5,9},{9,13},{13,1},{2,6},{6,10},{... | collective-permute-start | bytes 1179656 | tf_op jit(solution)/shard_map/ppermute | solution.py:269
  17.8 69.3 %copy-start.11 = (f32[3,4,64,128]{3,2,1,0:T(8,128)}, f32[3,4,64,128]{3,2,1,0:T(8,128)S(1)}, u32[]{:S(2)}) copy-start(f32[3,4,64,128]{3,2,1,0:T(8,128)S(1)} %collective-permute-done.refs_5_) | copy-start | bytes 1179652
  17.8 66.7 %collective-permute-start.11 = (f32[3,4,64,128]{3,2,1,0:T(8,128)}, f32[3,4,64,128]{3,2,1,0:T(8,128)}, u32[]{:S(2)}, u32[]{:S(2)}) collective-permute-start(f32[3,4,64,128]{3,2,1,0:T(8,128)} %get-tuple-element.68), channel_id=1, source_target_pairs={{0,8},{4,12},{8,0},{12,4},{1,9},{5,13},{9,1},{13,5},{2,10},{6,14},... | collective-permute-start | bytes 1179656 | tf_op jit(solution)/shard_map/ppermute | solution.py:269
  35.6 51.6 %copy-start.13 = (f32[3,4,64,128]{3,2,1,0:T(8,128)}, f32[3,4,64,128]{3,2,1,0:T(8,128)S(1)}, u32[]{:S(2)}) copy-start(f32[3,4,64,128]{3,2,1,0:T(8,128)S(1)} %collective-permute-done.1.refs_6_) | copy-start | bytes 1179652
  35.6 51.6 %collective-permute-start.12 = (f32[3,4,64,128]{3,2,1,0:T(8,128)}, f32[3,4,64,128]{3,2,1,0:T(8,128)}, u32[]{:S(2)}, u32[]{:S(2)}) collective-permute-start(f32[3,4,64,128]{3,2,1,0:T(8,128)} %get-tuple-element.69), channel_id=1, source_target_pairs={{0,12},{4,0},{8,4},{12,8},{1,13},{5,1},{9,5},{13,9},{2,14},{6,2},{... | collective-permute-start | bytes 1179656 | tf_op jit(solution)/shard_map/ppermute | solution.py:269
  59.9 47.1 %copy-start.15 = (f32[3,4,64,128]{3,2,1,0:T(8,128)}, f32[3,4,64,128]{3,2,1,0:T(8,128)S(1)}, u32[]{:S(2)}) copy-start(f32[3,4,64,128]{3,2,1,0:T(8,128)S(1)} %collective-permute-done.2.refs_7_) | copy-start | bytes 1179652
  60.0 27.2 %collective-permute-start.13 = (f32[3,4,64,128]{3,2,1,0:T(8,128)S(1)}, f32[3,4,64,128]{3,2,1,0:T(8,128)S(1)}, u32[]{:S(2)}, u32[]{:S(2)}) collective-permute-start(f32[3,4,64,128]{3,2,1,0:T(8,128)S(1)} %copy-done.10), channel_id=1, source_target_pairs={{0,1},{1,0},{2,3},{3,2},{4,5},{5,4},{6,7},{7,6},{8,9},{9,8},{10,11... | collective-permute-start | bytes 1179656 | tf_op jit(solution)/shard_map/ppermute | solution.py:274
  60.0 47.0 %copy-start.16 = (f32[3,4,64,128]{3,2,1,0:T(8,128)}, f32[3,4,64,128]{3,2,1,0:T(8,128)S(1)}, u32[]{:S(2)}) copy-start(f32[3,4,64,128]{3,2,1,0:T(8,128)S(1)} %collective-permute-done.3.refs_8_) | copy-start | bytes 1179652
  60.1 27.7 %collective-permute-start.20 = (f32[3,4,64,128]{3,2,1,0:T(8,128)}, f32[3,4,64,128]{3,2,1,0:T(8,128)S(1)}, u32[]{:S(2)}, u32[]{:S(2)}) collective-permute-start(f32[3,4,64,128]{3,2,1,0:T(8,128)} %get-tuple-element.82), channel_id=1, source_target_pairs={{0,4},{4,8},{8,12},{12,0},{1,5},{5,9},{9,13},{13,1},{2,6},{6,10},{... | collective-permute-start | bytes 1179656 | tf_op jit(solution)/shard_map/ppermute | solution.py:269
  60.1 61.1 %copy-start.12 = (f32[3,4,64,128]{3,2,1,0:T(8,128)}, f32[3,4,64,128]{3,2,1,0:T(8,128)S(1)}, u32[]{:S(2)}) copy-start(f32[3,4,64,128]{3,2,1,0:T(8,128)S(1)} %collective-permute-done.10.refs_5_) | copy-start | bytes 1179652
  60.1 41.2 %collective-permute-start.21 = (f32[3,4,64,128]{3,2,1,0:T(8,128)}, f32[3,4,64,128]{3,2,1,0:T(8,128)S(1)}, u32[]{:S(2)}, u32[]{:S(2)}) collective-permute-start(f32[3,4,64,128]{3,2,1,0:T(8,128)} %get-tuple-element.83), channel_id=1, source_target_pairs={{0,8},{4,12},{8,0},{12,4},{1,9},{5,13},{9,1},{13,5},{2,10},{6,14},... | collective-permute-start | bytes 1179656 | tf_op jit(solution)/shard_map/ppermute | solution.py:269
  84.5 19.7 %collective-permute-start.22 = (f32[3,4,64,128]{3,2,1,0:T(8,128)}, f32[3,4,64,128]{3,2,1,0:T(8,128)}, u32[]{:S(2)}, u32[]{:S(2)}) collective-permute-start(f32[3,4,64,128]{3,2,1,0:T(8,128)} %get-tuple-element.84), channel_id=1, source_target_pairs={{0,12},{4,0},{8,4},{12,8},{1,13},{5,1},{9,5},{13,9},{2,14},{6,2},{... | collective-permute-start | bytes 1179656 | tf_op jit(solution)/shard_map/ppermute | solution.py:269
  87.1 17.1 %collective-permute-start.4 = (f32[3,4,64,128]{3,2,1,0:T(8,128)S(1)}, f32[3,4,64,128]{3,2,1,0:T(8,128)S(1)}, u32[]{:S(2)}, u32[]{:S(2)}) collective-permute-start(f32[3,4,64,128]{3,2,1,0:T(8,128)S(1)} %collective-permute-done.refs_5_), channel_id=1, source_target_pairs={{0,1},{1,0},{2,3},{3,2},{4,5},{5,4},{6,7},{7,6},{8,9},{9,8},{10,11... | collective-permute-start | bytes 1179656 | tf_op jit(solution)/shard_map/ppermute | solution.py:274
  87.2 18.1 %copy-start.17 = (f32[3,4,64,128]{3,2,1,0:T(8,128)}, f32[3,4,64,128]{3,2,1,0:T(8,128)S(1)}, u32[]{:S(2)}) copy-start(f32[3,4,64,128]{3,2,1,0:T(8,128)S(1)} %collective-permute-done.13.refs_8_) | copy-start | bytes 1179652
  87.2 17.5 %collective-permute-start.5 = (f32[3,4,64,128]{3,2,1,0:T(8,128)S(1)}, f32[3,4,64,128]{3,2,1,0:T(8,128)S(1)}, u32[]{:S(2)}, u32[]{:S(2)}) collective-permute-start(f32[3,4,64,128]{3,2,1,0:T(8,128)S(1)} %collective-permute-done.1.refs_6_), channel_id=1, source_target_pairs={{0,1},{1,0},{2,3},{3,2},{4,5},{5,4},{6,7},{7,6},{8,9},{9,8},{10,11... | collective-permute-start | bytes 1179656 | tf_op jit(solution)/shard_map/ppermute | solution.py:274
  87.7 33.5 %copy-start.9 = (f32[3,4,64,128]{3,2,1,0:T(8,128)}, f32[3,4,64,128]{3,2,1,0:T(8,128)S(1)}, u32[]{:S(2)}) copy-start(f32[3,4,64,128]{3,2,1,0:T(8,128)S(1)} %collective-permute-done.20.refs_5_) | copy-start | bytes 1179652
  87.7 17.1 %collective-permute-start.6 = (f32[3,4,64,128]{3,2,1,0:T(8,128)S(1)}, f32[3,4,64,128]{3,2,1,0:T(8,128)S(1)}, u32[]{:S(2)}, u32[]{:S(2)}) collective-permute-start(f32[3,4,64,128]{3,2,1,0:T(8,128)S(1)} %collective-permute-done.2.refs_7_), channel_id=1, source_target_pairs={{0,1},{1,0},{2,3},{3,2},{4,5},{5,4},{6,7},{7,6},{8,9},{9,8},{10,11... | collective-permute-start | bytes 1179656 | tf_op jit(solution)/shard_map/ppermute | solution.py:274
  101.3 19.9 %copy-start.14 = (f32[3,4,64,128]{3,2,1,0:T(8,128)}, f32[3,4,64,128]{3,2,1,0:T(8,128)S(1)}, u32[]{:S(2)}) copy-start(f32[3,4,64,128]{3,2,1,0:T(8,128)S(1)} %collective-permute-done.21.refs_6_) | copy-start | bytes 1179652
  101.3 3.9 %collective-permute-start.14 = (f32[3,4,64,128]{3,2,1,0:T(8,128)S(1)}, f32[3,4,64,128]{3,2,1,0:T(8,128)S(1)}, u32[]{:S(2)}, u32[]{:S(2)}) collective-permute-start(f32[3,4,64,128]{3,2,1,0:T(8,128)S(1)} %collective-permute-done.10.refs_5_), channel_id=1, source_target_pairs={{0,1},{1,0},{2,3},{3,2},{4,5},{5,4},{6,7},{7,6},{8,9},{9,8},{10,11... | collective-permute-start | bytes 1179656 | tf_op jit(solution)/shard_map/ppermute | solution.py:274
  104.2 1.9 %collective-permute-start.15 = (f32[3,4,64,128]{3,2,1,0:T(8,128)}, f32[3,4,64,128]{3,2,1,0:T(8,128)S(1)}, u32[]{:S(2)}, u32[]{:S(2)}) collective-permute-start(f32[3,4,64,128]{3,2,1,0:T(8,128)} %collective-permute-done.11.refs_6_), channel_id=1, source_target_pairs={{0,1},{1,0},{2,3},{3,2},{4,5},{5,4},{6,7},{7,6},{8,9},{9,8},{10,11... | collective-permute-start | bytes 1179656 | tf_op jit(solution)/shard_map/ppermute | solution.py:274
  104.2 17.1 %collective-permute-start.16 = (f32[3,4,64,128]{3,2,1,0:T(8,128)}, f32[3,4,64,128]{3,2,1,0:T(8,128)}, u32[]{:S(2)}, u32[]{:S(2)}) collective-permute-start(f32[3,4,64,128]{3,2,1,0:T(8,128)} %collective-permute-done.12.refs_7_), channel_id=1, source_target_pairs={{0,1},{1,0},{2,3},{3,2},{4,5},{5,4},{6,7},{7,6},{8,9},{9,8},{10,11... | collective-permute-start | bytes 1179656 | tf_op jit(solution)/shard_map/ppermute | solution.py:274
  104.7 36.9 %collective-permute-start.23 = (f32[3,4,64,128]{3,2,1,0:T(8,128)}, f32[3,4,64,128]{3,2,1,0:T(8,128)S(1)}, u32[]{:S(2)}, u32[]{:S(2)}) collective-permute-start(f32[3,4,64,128]{3,2,1,0:T(8,128)} %get-tuple-element.81.refs_4_), channel_id=1, source_target_pairs={{0,1},{1,0},{2,3},{3,2},{4,5},{5,4},{6,7},{7,6},{8,9},{9,8},{10,11... | collective-permute-start | bytes 1179656 | tf_op jit(solution)/shard_map/ppermute | solution.py:274
  104.8 38.7 %collective-permute-start.24 = (f32[3,4,64,128]{3,2,1,0:T(8,128)S(1)}, f32[3,4,64,128]{3,2,1,0:T(8,128)S(1)}, u32[]{:S(2)}, u32[]{:S(2)}) collective-permute-start(f32[3,4,64,128]{3,2,1,0:T(8,128)S(1)} %collective-permute-done.20.refs_5_), channel_id=1, source_target_pairs={{0,1},{1,0},{2,3},{3,2},{4,5},{5,4},{6,7},{7,6},{8,9},{9,8},{10,11... | collective-permute-start | bytes 1179656 | tf_op jit(solution)/shard_map/ppermute | solution.py:274
  105.2 16.0 %copy-start.21 = (f32[3,4,64,128]{3,2,1,0:T(8,128)}, f32[3,4,64,128]{3,2,1,0:T(8,128)S(1)}, u32[]{:S(2)}) copy-start(f32[3,4,64,128]{3,2,1,0:T(8,128)S(1)} %collective-permute-done.14.refs_9_) | copy-start | bytes 1179652
  105.3 39.1 %collective-permute-start.25 = (f32[3,4,64,128]{3,2,1,0:T(8,128)S(1)}, f32[3,4,64,128]{3,2,1,0:T(8,128)}, u32[]{:S(2)}, u32[]{:S(2)}) collective-permute-start(f32[3,4,64,128]{3,2,1,0:T(8,128)S(1)} %collective-permute-done.21.refs_6_), channel_id=1, source_target_pairs={{0,1},{1,0},{2,3},{3,2},{4,5},{5,4},{6,7},{7,6},{8,9},{9,8},{10,11... | collective-permute-start | bytes 1179656 | tf_op jit(solution)/shard_map/ppermute | solution.py:274
  106.9 38.8 %collective-permute-start.26 = (f32[3,4,64,128]{3,2,1,0:T(8,128)}, f32[3,4,64,128]{3,2,1,0:T(8,128)}, u32[]{:S(2)}, u32[]{:S(2)}) collective-permute-start(f32[3,4,64,128]{3,2,1,0:T(8,128)} %collective-permute-done.22.refs_7_), channel_id=1, source_target_pairs={{0,1},{1,0},{2,3},{3,2},{4,5},{5,4},{6,7},{7,6},{8,9},{9,8},{10,11... | collective-permute-start | bytes 1179656 | tf_op jit(solution)/shard_map/ppermute | solution.py:274
  121.3 20.4 %copy-start.27 = (f32[4,64,128]{2,1,0:T(8,128)S(1)}, f32[4,64,128]{2,1,0:T(8,128)}, u32[]{:S(2)}) copy-start(f32[4,64,128]{2,1,0:T(8,128)} %get-tuple-element.57) | copy-start | bytes 393220
  121.3 22.3 %copy-start.25 = (f32[4,64,128]{2,1,0:T(8,128)S(1)}, f32[4,64,128]{2,1,0:T(8,128)}, u32[]{:S(2)}) copy-start(f32[4,64,128]{2,1,0:T(8,128)} %get-tuple-element.58) | copy-start | bytes 393220
  121.3 39.7 %collective-permute-start.7 = (f32[4,64,128]{2,1,0:T(8,128)}, f32[4,64,128]{2,1,0:T(8,128)S(1)}, u32[]{:S(2)}, u32[]{:S(2)}) collective-permute-start(f32[4,64,128]{2,1,0:T(8,128)} %get-tuple-element.56), channel_id=1, source_target_pairs={{0,4},{4,8},{8,12},{12,0},{1,5},{5,9},{9,13},{13,1},{2,6},{6,10},{... | collective-permute-start | bytes 393224 | tf_op jit(solution)/shard_map/ppermute | solution.py:269
  141.7 20.9 %collective-permute-start.8 = (f32[4,64,128]{2,1,0:T(8,128)S(1)}, f32[4,64,128]{2,1,0:T(8,128)S(1)}, u32[]{:S(2)}, u32[]{:S(2)}) collective-permute-start(f32[4,64,128]{2,1,0:T(8,128)S(1)} %copy-done.27), channel_id=1, source_target_pairs={{0,8},{4,12},{8,0},{12,4},{1,9},{5,13},{9,1},{13,5},{2,10},{6,14},... | collective-permute-start | bytes 393224 | tf_op jit(solution)/shard_map/ppermute | solution.py:269
  143.6 19.5 %collective-permute-start.9 = (f32[4,64,128]{2,1,0:T(8,128)S(1)}, f32[4,64,128]{2,1,0:T(8,128)S(1)}, u32[]{:S(2)}, u32[]{:S(2)}) collective-permute-start(f32[4,64,128]{2,1,0:T(8,128)S(1)} %copy-done.25), channel_id=1, source_target_pairs={{0,12},{4,0},{8,4},{12,8},{1,13},{5,1},{9,5},{13,9},{2,14},{6,2},{... | collective-permute-start | bytes 393224 | tf_op jit(solution)/shard_map/ppermute | solution.py:269
  144.3 20.6 %collective-permute-start.17 = (f32[4,64,128]{2,1,0:T(8,128)}, f32[4,64,128]{2,1,0:T(8,128)S(1)}, u32[]{:S(2)}, u32[]{:S(2)}) collective-permute-start(f32[4,64,128]{2,1,0:T(8,128)} %get-tuple-element.71), channel_id=1, source_target_pairs={{0,4},{4,8},{8,12},{12,0},{1,5},{5,9},{9,13},{13,1},{2,6},{6,10},{... | collective-permute-start | bytes 393224 | tf_op jit(solution)/shard_map/ppermute | solution.py:269
  145.6 15.3 %copy-start.26 = (f32[4,64,128]{2,1,0:T(8,128)S(1)}, f32[4,64,128]{2,1,0:T(8,128)}, u32[]{:S(2)}) copy-start(f32[4,64,128]{2,1,0:T(8,128)} %get-tuple-element.73) | copy-start | bytes 393220
  145.6 21.7 %collective-permute-start.18 = (f32[4,64,128]{2,1,0:T(8,128)}, f32[4,64,128]{2,1,0:T(8,128)S(1)}, u32[]{:S(2)}, u32[]{:S(2)}) collective-permute-start(f32[4,64,128]{2,1,0:T(8,128)} %get-tuple-element.72), channel_id=1, source_target_pairs={{0,8},{4,12},{8,0},{12,4},{1,9},{5,13},{9,1},{13,5},{2,10},{6,14},... | collective-permute-start | bytes 393224 | tf_op jit(solution)/shard_map/ppermute | solution.py:269
  161.0 16.0 %copy-start = (f32[4,64,128]{2,1,0:T(8,128)}, f32[4,64,128]{2,1,0:T(8,128)S(1)}, u32[]{:S(2)}) copy-start(f32[4,64,128]{2,1,0:T(8,128)S(1)} %collective-permute-done.7.refs_1_) | copy-start | bytes 393220
  161.0 6.4 %collective-permute-start.19 = (f32[4,64,128]{2,1,0:T(8,128)S(1)}, f32[4,64,128]{2,1,0:T(8,128)S(1)}, u32[]{:S(2)}, u32[]{:S(2)}) collective-permute-start(f32[4,64,128]{2,1,0:T(8,128)S(1)} %copy-done.26), channel_id=1, source_target_pairs={{0,12},{4,0},{8,4},{12,8},{1,13},{5,1},{9,5},{13,9},{2,14},{6,2},{... | collective-permute-start | bytes 393224 | tf_op jit(solution)/shard_map/ppermute | solution.py:269
  162.6 14.4 %copy-start.1 = (f32[4,64,128]{2,1,0:T(8,128)}, f32[4,64,128]{2,1,0:T(8,128)S(1)}, u32[]{:S(2)}) copy-start(f32[4,64,128]{2,1,0:T(8,128)S(1)} %collective-permute-done.8.refs_2_) | copy-start | bytes 393220
  162.6 8.5 %collective-permute-start.27 = (f32[4,64,128]{2,1,0:T(8,128)}, f32[4,64,128]{2,1,0:T(8,128)S(1)}, u32[]{:S(2)}, u32[]{:S(2)}) collective-permute-start(f32[4,64,128]{2,1,0:T(8,128)} %get-tuple-element.86), channel_id=1, source_target_pairs={{0,4},{4,8},{8,12},{12,0},{1,5},{5,9},{9,13},{13,1},{2,6},{6,10},{... | collective-permute-start | bytes 393224 | tf_op jit(solution)/shard_map/ppermute | solution.py:269
  163.1 13.9 %copy-start.2 = (f32[4,64,128]{2,1,0:T(8,128)}, f32[4,64,128]{2,1,0:T(8,128)S(1)}, u32[]{:S(2)}) copy-start(f32[4,64,128]{2,1,0:T(8,128)S(1)} %collective-permute-done.9.refs_3_) | copy-start | bytes 393220
  163.1 13.9 %collective-permute-start.28 = (f32[4,64,128]{2,1,0:T(8,128)}, f32[4,64,128]{2,1,0:T(8,128)S(1)}, u32[]{:S(2)}, u32[]{:S(2)}) collective-permute-start(f32[4,64,128]{2,1,0:T(8,128)} %get-tuple-element.87), channel_id=1, source_target_pairs={{0,8},{4,12},{8,0},{12,4},{1,9},{5,13},{9,1},{13,5},{2,10},{6,14},... | collective-permute-start | bytes 393224 | tf_op jit(solution)/shard_map/ppermute | solution.py:269
  164.9 12.1 %copy-start.3 = (f32[4,64,128]{2,1,0:T(8,128)}, f32[4,64,128]{2,1,0:T(8,128)S(1)}, u32[]{:S(2)}) copy-start(f32[4,64,128]{2,1,0:T(8,128)S(1)} %collective-permute-done.17.refs_5_) | copy-start | bytes 393220
  164.9 12.1 %collective-permute-start.29 = (f32[4,64,128]{2,1,0:T(8,128)}, f32[4,64,128]{2,1,0:T(8,128)S(1)}, u32[]{:S(2)}, u32[]{:S(2)}) collective-permute-start(f32[4,64,128]{2,1,0:T(8,128)} %get-tuple-element.88), channel_id=1, source_target_pairs={{0,12},{4,0},{8,4},{12,8},{1,13},{5,1},{9,5},{13,9},{2,14},{6,2},{... | collective-permute-start | bytes 393224 | tf_op jit(solution)/shard_map/ppermute | solution.py:269
  167.4 9.6 %copy-start.5 = (f32[4,64,128]{2,1,0:T(8,128)}, f32[4,64,128]{2,1,0:T(8,128)S(1)}, u32[]{:S(2)}) copy-start(f32[4,64,128]{2,1,0:T(8,128)S(1)} %collective-permute-done.19.refs_7_) | copy-start | bytes 393220
  (10 other events, 30.9 us)
where the time goes:
time: 181 us; the launch traced here: 180 us
  starting transfers between devices  79 us (44%)
  Pallas kernels  52 us (29%)
  waiting for transfers between devices  47.2 us (26%)
    ppermute x18, starting transfers between devices, around(): lax.ppermute(value, 'frm', [(i, (i + hop) % size) for i in range(size)])  76.9 us
    ppermute x18, waiting for transfers between devices, around(): lax.ppermute(value, 'frm', [(i, (i + hop) % size) for i in range(size)])  46.4 us
    pallas_call x3, Pallas kernels, attend_head(): pl.pallas_call(functools.partial(attend_kernel, slot, parts, per_part), o...  42.5 us
    pallas_call x3, Pallas kernels, pack(): pl.pallas_call(functools.partial(pack_kernel, slot, parts, channels // DH...  7.18 us
  transfers between devices with their start and end apart: 30, of which 7 were waited for; matrix products, arithmetic and copies ran while one was open for 0% of the time, Pallas kernels for 26%

commit v1 on v0

--- a/solution.py
+++ b/solution.py
@@ -14,6 +14,9 @@
 KSTRIDE = 4
 WMAX = 2
 MASKED = -1e30
+GROUP = 4
+ATTEND_VMEM = 24 * 2**20
+BLEND = 8
 
 
 def lowpass_table(frames):
@@ -24,14 +27,18 @@
     return (keep @ waves / frames).astype(np.float32)
 
 
+def wires(parts):
+    return sorted(range(1, parts), key=lambda hop: (hop.bit_count() % 2 == 0, -hop))
+
+
 def pack_kernel(slot, parts, per_part, *refs):
     sources, outs = refs[:3], refs[3 : 3 + parts]
     held, load_sem, store_sem = refs[3 + parts :]
     me = lax.axis_index("frm")
-    order = [*range(1, parts), 0]
+    order = [*wires(parts), 0]
     loads, stores = {}, {}
     for hop in order:
-        owner = lax.rem(me + hop, parts)
+        owner = lax.bitwise_xor(me, hop)
         columns = pl.ds(pl.multiple_of((owner * per_part + slot) * DH, DH), DH)
         for at in range(3):
             loads[hop, at] = pltpu.make_async_copy(
@@ -70,22 +77,14 @@
     return high, (value - high.astype(jnp.float32)).astype(jnp.bfloat16)
 
 
-def weighted(scores, values):
-    highest = jnp.max(scores, axis=1, keepdims=True)
-    weights = jnp.exp(scores - highest)
-    total = jnp.sum(weights, axis=1, keepdims=True)
-    high, low = split(weights)
-    wide = jnp.dot(high, values, preferred_element_type=jnp.float32)
-    rest = jnp.dot(low, values[:, :DH], preferred_element_type=jnp.float32)
-    return (wide[:, :DH] + wide[:, DH:] + rest) / total
-
-
-def attend_kernel(slot, parts, per_part, *refs):
+def attend_kernel(slot, parts, per_part, riders, *refs):
     windows, strides, cutoffs, table = refs[:4]
-    mine, theirs = refs[4 : 4 + parts], refs[4 + parts : 4 + 2 * parts]
-    outs = refs[4 + 2 * parts : 4 + 3 * parts]
+    refs = refs[4:]
+    mine, theirs, refs = refs[:parts], refs[parts : 2 * parts], refs[2 * parts :]
+    earlier, refs = (refs[:parts], refs[parts:]) if riders else ((), refs)
+    outs, refs = refs[:parts], refs[parts:]
     (q_in, k_in, v_in, q_cat, k_cat, v_cat, kg_cat, vg_cat, local, diff, load_sem, store_sem) = refs[
-        4 + 3 * parts :
+        :12
     ]
     frames, rows, _ = q_in.shape
     tokens = k_in.shape[1]
@@ -96,25 +95,33 @@
 
     loads = []
     for hop in range(parts):
-        owner = lax.rem(me + parts - hop, parts)
+        owner = lax.bitwise_xor(me, hop)
         span = pl.ds(owner * frames_dev, frames_dev)
         near, far = pl.ds(0, rows), pl.ds(rows, rows)
+        loads.append([])
         for at, (source, target) in enumerate(
             (
                 (mine[hop].at[0], q_in.at[span]),
                 (mine[hop].at[1], k_in.at[span, near]),
+                (theirs[hop].at[1], k_in.at[span, far]),
                 (mine[hop].at[2], v_in.at[span, near]),
-                (theirs[hop].at[1], k_in.at[span, far]),
                 (theirs[hop].at[2], v_in.at[span, far]),
             )
         ):
             copy = pltpu.make_async_copy(source, target, load_sem.at[hop, at])
             copy.start()
-            loads.append(copy)
-    for copy in loads:
-        copy.wait()
-
-    score_scale = DH ** (-0.5)
+            loads[-1].append(copy)
+
+    if riders:
+        held, ride_sem = refs[12:]
+        rides = [
+            pltpu.make_async_copy(earlier[hop], held.at[hop], ride_sem.at[0, hop])
+            for hop in range(parts)
+        ]
+        for copy in rides:
+            copy.start()
+
+    score_scale = DH ** (-0.5) * math.log2(math.e)
 
     def prepare(frame, carry):
         q_at = pl.ds(pl.multiple_of(frame * rows, rows), rows)
@@ -127,65 +134,105 @@
         k_cat[k_at, 0:DH] = k_high
         k_cat[k_at, DH : 2 * DH] = k_high
         k_cat[k_at, 2 * DH : 3 * DH] = k_low
-        v_high, v_low = split(v_in[frame])
-        v_cat[k_at, 0:DH] = v_high
-        v_cat[k_at, DH : 2 * DH] = v_low
+        v_high, v_low = split(v_in[frame].T)
+        v_cat[0:DH, k_at] = v_high
+        v_cat[DH : 2 * DH, k_at] = v_low
         return carry
 
-    lax.fori_loop(0, frames, prepare, 0)
+    for hop in range(parts):
+        owner = lax.bitwise_xor(me, hop)
+        for copy in loads[hop]:
+            copy.wait()
+        lax.fori_loop(owner * frames_dev, (owner + 1) * frames_dev, prepare, 0)
     key_frames = frames // KSTRIDE
     for at in range(key_frames):
         source = pl.ds(at * KSTRIDE * tokens, tokens)
         target = pl.ds(at * tokens, tokens)
         kg_cat[target, :] = k_cat[source, :]
-        vg_cat[target, :] = v_cat[source, :]
-
-    def scores_of(query_rows, key_rows):
-        return lax.dot_general(
-            query_rows, key_rows, (((1,), (1,)), ((), ())), preferred_element_type=jnp.float32
+        vg_cat[:, target] = v_cat[:, source]
+
+    group = GROUP
+    reach = min(2 * WMAX + group, frames)
+    group_rows = group * rows
+    lane_frame = lax.broadcasted_iota(jnp.int32, (1, group_rows), 1) // rows
+
+    def weighted(key_rows, bias, value_columns, query_rows):
+        scores = lax.dot_general(
+            key_rows, query_rows, (((1,), (1,)), ((), ())), preferred_element_type=jnp.float32
         )
-
-    pair = 2
-    reach = min(2 * WMAX + pair, frames)
-    pair_rows = pair * rows
-    key_frame = lax.broadcasted_iota(jnp.int32, (1, key_frames * tokens), 1) // tokens * KSTRIDE
-    global_bias = jnp.where(lax.rem(key_frame, stride) == 0, 0.0, MASKED)
-
-    def per_pair(step, carry):
-        first = step * pair
+        parts_of = [scores[at * tokens : (at + 1) * tokens] for at in range(len(bias))]
+        peaks = [
+            jnp.max(part, axis=0, keepdims=True) + shift for part, shift in zip(parts_of, bias)
+        ]
+        highest = functools.reduce(jnp.maximum, peaks)
+        weights = jnp.concatenate(
+            [jnp.exp2(part - (highest - shift)) for part, shift in zip(parts_of, bias)], axis=0
+        )
+        total = jnp.sum(weights, axis=0, keepdims=True)
+        high, low = split(weights)
+        wide = jnp.dot(value_columns, high, preferred_element_type=jnp.float32)
+        rest = jnp.dot(value_columns[:DH], low, preferred_element_type=jnp.float32)
+        return (wide[:DH] + wide[DH:] + rest) / total
+
+    global_bias = [
+        jnp.where(lax.rem(at * KSTRIDE, stride) == 0, 0.0, MASKED) for at in range(key_frames)
+    ]
+
+    def per_group(step, carry):
+        first = step * group
         start = jnp.clip(first - WMAX, 0, frames - reach)
-        q_part = q_cat[pl.ds(pl.multiple_of(first * rows, pair_rows), pair_rows), :]
+        q_part = q_cat[pl.ds(pl.multiple_of(first * rows, group_rows), group_rows), :]
         k_at = pl.ds(pl.multiple_of(start * tokens, tokens), reach * tokens)
-        near_frame = start + lax.broadcasted_iota(jnp.int32, (pair_rows, reach * tokens), 1) // tokens
-        query_frame = first + lax.broadcasted_iota(jnp.int32, (pair_rows, reach * tokens), 0) // rows
-        scores = scores_of(q_part, k_cat[k_at, :])
-        scores = jnp.where(jnp.abs(near_frame - query_frame) <= window, scores, MASKED)
-        local_part = weighted(scores, v_cat[k_at, :])
-        global_part = weighted(scores_of(q_part, kg_cat[...]) + global_bias, vg_cat[...])
-        difference = global_part - local_part
-        for at in range(pair):
+        local_bias = [
+            jnp.where(jnp.abs(start + at - first - lane_frame) <= window, 0.0, MASKED)
+            for at in range(reach)
+        ]
+        local_part = weighted(k_cat[k_at, :], local_bias, v_cat[:, k_at], q_part)
+        global_part = weighted(kg_cat[...], global_bias, vg_cat[...], q_part)
+        difference = (global_part - local_part).T
+        local_part = local_part.T
+        for at in range(group):
             local[first + at] = local_part[at * rows : (at + 1) * rows]
             diff[first + at] = difference[at * rows : (at + 1) * rows]
         return carry
 
-    lax.fori_loop(0, frames // pair, per_pair, 0)
-
-    kept = jnp.clip(cutoff, 0, frames // 2)
-
-    def blend(frame, carry):
-        total = local[frame]
-        for other in range(frames):
-            total += table[kept, lax.rem(frame + frames - other, frames)] * diff[other]
-        q_in[frame] = total
+    lax.fori_loop(0, frames // group, per_group, 0)
+
+    stores = []
+    for hop in range(parts if riders else 0):
+        rides[hop].wait()
+        stores.append(
+            pltpu.make_async_copy(held.at[hop], outs[hop].at[0:riders], ride_sem.at[1, hop])
+        )
+        stores[-1].start()
+
+    half = frames // 2
+    kept = jnp.clip(cutoff, 0, half)
+    even = [0.5 * (table[kept, at] + table[kept, at + half]) for at in range(half)]
+    odd = [0.5 * (table[kept, at] - table[kept, at + half]) for at in range(half)]
+
+    def blend(row, carry):
+        at = pl.ds(pl.multiple_of(row * BLEND, BLEND), BLEND)
+        first = [diff[frame, at] for frame in range(half)]
+        second = [diff[frame + half, at] for frame in range(half)]
+        sums = [x + y for x, y in zip(first, second)]
+        gaps = [x - y for x, y in zip(first, second)]
+        for frame in range(half):
+            periodic = sum(even[(frame - other) % half] * sums[other] for other in range(half))
+            turning = sum(
+                (odd[frame - other] if other <= frame else -odd[frame - other + half]) * gaps[other]
+                for other in range(half)
+            )
+            q_in[frame, at] = local[frame, at] + (periodic + turning)
+            q_in[frame + half, at] = local[frame + half, at] + (periodic - turning)
         return carry
 
-    lax.fori_loop(0, frames, blend, 0)
-    stores = []
+    lax.fori_loop(0, rows // BLEND, blend, 0)
     for hop in range(parts):
-        owner = lax.rem(me + hop, parts)
+        owner = lax.bitwise_xor(me, hop)
         stores.append(
             pltpu.make_async_copy(
-                q_in.at[pl.ds(owner * frames_dev, frames_dev)], outs[hop], store_sem.at[hop]
+                q_in.at[pl.ds(owner * frames_dev, frames_dev)], outs[hop].at[riders], store_sem.at[hop]
             )
         )
         stores[-1].start()
@@ -193,17 +240,25 @@
         copy.wait()
 
 
-def attend_head(slot, parts, scalars, table, mine, theirs):
+def attend_head(slot, parts, scalars, table, mine, theirs, earlier):
     _, frames_dev, rows, _ = mine[0].shape
     frames, tokens = frames_dev * parts, 2 * rows
     per_part = scalars[0].shape[0] // parts
     key_frames = frames // KSTRIDE
+    riders = earlier[0].shape[0] if earlier else 0
+    result = (riders + 1, frames_dev, rows, DH)
+    scratch = []
+    if riders:
+        scratch = [
+            pltpu.VMEM((parts, riders, frames_dev, rows, DH), jnp.float32),
+            pltpu.SemaphoreType.DMA((2, parts)),
+        ]
     flops = 12 * frames * rows * (5 + key_frames) * tokens * DH
     return pl.pallas_call(
-        functools.partial(attend_kernel, slot, parts, per_part),
-        out_shape=[jax.ShapeDtypeStruct((frames_dev, rows, DH), jnp.float32)] * parts,
+        functools.partial(attend_kernel, slot, parts, per_part, riders),
+        out_shape=[jax.ShapeDtypeStruct(result, jnp.float32)] * parts,
         in_specs=[pl.BlockSpec(memory_space=pltpu.SMEM)] * 4
-        + [pl.BlockSpec(memory_space=pl.ANY)] * (2 * parts),
+        + [pl.BlockSpec(memory_space=pl.ANY)] * (2 * parts + len(earlier)),
         out_specs=[pl.BlockSpec(memory_space=pl.ANY)] * parts,
         scratch_shapes=[
             pltpu.VMEM((frames, rows, DH), jnp.float32),
@@ -211,62 +266,66 @@
             pltpu.VMEM((frames, tokens, DH), jnp.float32),
             pltpu.VMEM((frames * rows, 3 * DH), jnp.bfloat16),
             pltpu.VMEM((frames * tokens, 3 * DH), jnp.bfloat16),
-            pltpu.VMEM((frames * tokens, 2 * DH), jnp.bfloat16),
+            pltpu.VMEM((2 * DH, frames * tokens), jnp.bfloat16),
             pltpu.VMEM((key_frames * tokens, 3 * DH), jnp.bfloat16),
-            pltpu.VMEM((key_frames * tokens, 2 * DH), jnp.bfloat16),
+            pltpu.VMEM((2 * DH, key_frames * tokens), jnp.bfloat16),
             pltpu.VMEM((frames, rows, DH), jnp.float32),
             pltpu.VMEM((frames, rows, DH), jnp.float32),
             pltpu.SemaphoreType.DMA((parts, 5)),
             pltpu.SemaphoreType.DMA((parts,)),
-        ],
+        ]
+        + scratch,
         cost_estimate=pl.CostEstimate(
             flops=flops,
             bytes_accessed=6 * frames * rows * DH * 4,
             transcendentals=frames * rows * (5 + key_frames) * tokens,
         ),
-    )(*scalars, table, *mine, *theirs)
-
-
-def unpack_kernel(parts, per_part, *refs):
-    count = parts * per_part
-    pieces, out = refs[:count], refs[count]
-    held, load_sem, store_sem = refs[count + 1 :]
+        compiler_params=pltpu.CompilerParams(vmem_limit_bytes=ATTEND_VMEM),
+    )(*scalars, table, *mine, *theirs, *earlier)
+
+
+def unpack_kernel(parts, per_part, first, *refs):
+    pieces, refs = refs[:parts], refs[parts:]
+    out, held, load_sem, store_sem = refs[-4:]
+    slots = held.shape[1]
     me = lax.axis_index("frm")
     loads, stores = [], []
-    for at in range(count):
-        loads.append(pltpu.make_async_copy(pieces[at], held.at[at], load_sem.at[at]))
+    for hop in range(parts):
+        loads.append(pltpu.make_async_copy(pieces[hop], held.at[hop], load_sem.at[hop]))
         loads[-1].start()
-    for at in range(count):
-        slot, hop = at // parts, at % parts
-        owner = lax.rem(me + parts - hop, parts)
-        columns = pl.ds(pl.multiple_of((owner * per_part + slot) * DH, DH), DH)
-        loads[at].wait()
-        stores.append(pltpu.make_async_copy(held.at[at], out.at[:, :, columns], store_sem.at[at]))
-        stores[-1].start()
+    for hop in range(parts):
+        owner = lax.bitwise_xor(me, hop)
+        loads[hop].wait()
+        for at in range(slots):
+            columns = pl.ds(pl.multiple_of((owner * per_part + first + at) * DH, DH), DH)
+            stores.append(
+                pltpu.make_async_copy(held.at[hop, at], out.at[:, :, columns], store_sem.at[hop, at])
+            )
+            stores[-1].start()
     for copy in stores:
         copy.wait()
 
 
-def unpack(parts, pieces):
-    frames_dev, rows, _ = pieces[0].shape
-    count = len(pieces)
+def unpack(parts, per_part, first, pieces, out=None):
+    slots, frames_dev, rows, _ = pieces[0].shape
+    operands = list(pieces) if out is None else [*pieces, out]
     return pl.pallas_call(
-        functools.partial(unpack_kernel, parts, count // parts),
-        out_shape=jax.ShapeDtypeStruct((frames_dev, rows, count * DH), jnp.float32),
-        in_specs=[pl.BlockSpec(memory_space=pl.ANY)] * count,
+        functools.partial(unpack_kernel, parts, per_part, first),
+        out_shape=jax.ShapeDtypeStruct((frames_dev, rows, parts * per_part * DH), jnp.float32),
+        in_specs=[pl.BlockSpec(memory_space=pl.ANY)] * len(operands),
         out_specs=pl.BlockSpec(memory_space=pl.ANY),
         scratch_shapes=[
-            pltpu.VMEM((count, frames_dev, rows, DH), jnp.float32),
-            pltpu.SemaphoreType.DMA((count,)),
-            pltpu.SemaphoreType.DMA((count,)),
+            pltpu.VMEM((parts, slots, frames_dev, rows, DH), jnp.float32),
+            pltpu.SemaphoreType.DMA((parts,)),
+            pltpu.SemaphoreType.DMA((parts, slots)),
         ],
-        name="unpack",
-    )(*pieces)
+        input_output_aliases={} if out is None else {parts: 0},
+    )(*operands)
 
 
 def around(value, hop):
     size = lax.axis_size("frm")
-    return lax.ppermute(value, "frm", [(i, (i + hop) % size) for i in range(size)])
+    return lax.ppermute(value, "frm", [(i, i ^ hop) for i in range(size)])
 
 
 def swap(value):
@@ -280,22 +339,28 @@
     frames = queries.shape[0] * parts
     table = jnp.asarray(lowpass_table(frames))
     scalars = (windows, strides, cutoffs)
-    packed, sources, moved, pieces = [], (queries, key_states, value_states), [], []
+    packed, sources, moved = [], (queries, key_states, value_states), []
     for slot in range(per_part):
         packed.append(pack(slot, parts, *sources))
         packed[-1], sources = lax.optimization_barrier((packed[-1], sources))
-        moved.append([packed[-1][0]])
-        for hop in range(1, parts):
-            moved[-1].append(around(packed[-1][hop], hop))
+        moved.append([packed[-1][0]] + [None] * (parts - 1))
+        for hop in wires(parts):
+            moved[-1][hop] = around(packed[-1][hop], hop)
+    earlier, out, first = (), None, 0
     for slot, mine in enumerate(moved):
         theirs = []
         for hop in range(parts):
             theirs.append(swap(mine[hop]))
-        done = attend_head(slot, parts, scalars, table, mine, theirs)
-        pieces.append(done[0])
-        for hop in range(1, parts):
-            pieces.append(around(done[hop], hop))
-    return unpack(parts, pieces)
+        done = attend_head(slot, parts, scalars, table, mine, theirs, earlier)
+        if slot < per_part - 2:
+            earlier = done
+            continue
+        earlier, landed = (), [done[0]] + [None] * (parts - 1)
+        for hop in wires(parts):
+            landed[hop] = around(done[hop], hop)
+        out = unpack(parts, per_part, first, landed, out)
+        first = slot + 1
+    return out
 
 
 def with_halo(value, sides, width):
@@ -416,7 +481,7 @@
 
 
 def splits_by_heads(heads_local, parts, pos_count):
-    return heads_local % parts == 0 and pos_count == 2
+    return heads_local % parts == 0 and pos_count == 2 and parts.bit_count() == 1
 
 
 def shards(queries, key_states, value_states, windows, strides, cutoffs):

time: 181 us -> 180 us (level)
  starting transfers between devices: 79 us -> 52 us
  waiting for transfers between devices: 47.2 us -> 71.3 us
    ppermute x18 -> x15, starting transfers between devices: 76.9 us -> 50 us  [around(): return lax.ppermute(value, 'frm', [(i, i ^ hop) for i in range(size)])]
    ppermute x18 -> x15, waiting for transfers between devices: 46.4 us -> 70.3 us  [around(): return lax.ppermute(value, 'frm', [(i, i ^ hop) for i in range(size)])]
    pallas_call x4 -> x5, Pallas kernels: 44.9 us -> 46.6 us  [the longest x3 42.8 us: attend_head(): pl.pallas_call(functools.partial(attend_kernel, slot, parts, per_part, ri...]
  transfers between devices with their start and end apart: 30 -> 27, of which waited for: 7 -> 8; matrix products, arithmetic and copies ran while one was open for 0% -> 0% of each run, Pallas kernels for 26% -> 27%
where the time goes in v1:
time: 180 us
  waiting for transfers between devices  71.3 us (40%)
  Pallas kernels  53.7 us (30%)
  starting transfers between devices  52 us (29%)
  local copies, waits for them, and re-layouts  2.86 us (2%)
    ppermute x15, waiting for transfers between devices, around(): return lax.ppermute(value, 'frm', [(i, i ^ hop) for i in range(size)])  70.3 us
    ppermute x15, starting transfers between devices, around(): return lax.ppermute(value, 'frm', [(i, i ^ hop) for i in range(size)])  50 us
    pallas_call x3, Pallas kernels, attend_head(): pl.pallas_call(functools.partial(attend_kernel, slot, parts, per_part, ri...  42.8 us
    pallas_call x3, Pallas kernels, pack(): pl.pallas_call(functools.partial(pack_kernel, slot, parts, channels // DH...  7.09 us
    pallas_call x2, Pallas kernels, unpack(): pl.pallas_call(functools.partial(unpack_kernel, parts, per_part, first),...  3.82 us
  transfers between devices with their start and end apart: 27, of which 8 were waited for; matrix products, arithmetic and copies ran while one was open for 0% of the time, Pallas kernels for 27%

profile of v1, /device:TPU:0, one launch (start us, length us, event | category | flops | bytes accessed | tf_op | source)
XLA Modules:
  0.0 180.2 jit_solution(2360538176024635499)
XLA Ops:
  0.0 2.4 %shard_map.73 = (f32[3,4,64,128]{3,2,1,0:T(8,128)}, f32[3,4,64,128]{3,2,1,0:T(8,128)}, f32[3,4,64,128]{3,2,1,0:T(8,128)}, f32[3,4,64,128]{3,2,1,0:T(8,128)}) custom-call(f32[4,64,1536]{2,1,0:T(8,128)} %refs_0_.6, f32[4,64,1536]{2,1,0:T(8,128)} %refs_1_.6, f32[4,64,1536]{2,1,0:T(8,128)} %refs_2_.6), custom_call_target="tpu_custom_call" | custom-call | bytes 3145728 | tf_op jit(solution)/shard_map/pallas_call | solution.py:61
  2.4 3.1 %collective-permute-start.17 = (f32[3,4,64,128]{3,2,1,0:T(8,128)}, f32[3,4,64,128]{3,2,1,0:T(8,128)S(1)}, u32[]{:S(2)}, u32[]{:S(2)}) collective-permute-start(f32[3,4,64,128]{3,2,1,0:T(8,128)} %get-tuple-element.78), channel_id=1, source_target_pairs={{0,4},{4,0},{8,12},{12,8},{1,5},{5,1},{9,13},{13,9},{2,6},{6,2},{1... | collective-permute-start | bytes 1179656 | tf_op jit(solution)/shard_map/ppermute | solution.py:328
  5.5 2.6 %collective-permute-start.18 = (f32[3,4,64,128]{3,2,1,0:T(8,128)}, f32[3,4,64,128]{3,2,1,0:T(8,128)S(1)}, u32[]{:S(2)}, u32[]{:S(2)}) collective-permute-start(f32[3,4,64,128]{3,2,1,0:T(8,128)} %get-tuple-element.79), channel_id=1, source_target_pairs={{0,8},{4,12},{8,0},{12,4},{1,9},{5,13},{9,1},{13,5},{2,10},{6,14},... | collective-permute-start | bytes 1179656 | tf_op jit(solution)/shard_map/ppermute | solution.py:328
  8.1 2.4 %shard_map.74 = (f32[3,4,64,128]{3,2,1,0:T(8,128)}, f32[3,4,64,128]{3,2,1,0:T(8,128)}, f32[3,4,64,128]{3,2,1,0:T(8,128)}, f32[3,4,64,128]{3,2,1,0:T(8,128)}) custom-call(f32[4,64,1536]{2,1,0:T(8,128)} %refs_0_.6, f32[4,64,1536]{2,1,0:T(8,128)} %refs_1_.6, f32[4,64,1536]{2,1,0:T(8,128)} %refs_2_.6), custom_call_target="tpu_custom_call" | custom-call | bytes 3145728 | tf_op jit(solution)/shard_map/pallas_call | solution.py:61
  10.5 0.0 copy-start.7
  10.5 1.0 collective-permute-start.10
  11.5 11.9 %collective-permute-done.17.refs_5_ = f32[3,4,64,128]{3,2,1,0:T(8,128)S(1)} collective-permute-done((f32[3,4,64,128]{3,2,1,0:T(8,128)}, f32[3,4,64,128]{3,2,1,0:T(8,128)S(1)}, u32[]{:S(2)}, u32[]{:S(2)}) %collective-permute-start.17) | collective-permute-done | bytes 393248 | tf_op jit(solution)/shard_map/ppermute | solution.py:328
  23.3 2.2 %collective-permute-start.11 = (f32[3,4,64,128]{3,2,1,0:T(8,128)}, f32[3,4,64,128]{3,2,1,0:T(8,128)S(1)}, u32[]{:S(2)}, u32[]{:S(2)}) collective-permute-start(f32[3,4,64,128]{3,2,1,0:T(8,128)} %get-tuple-element.75), channel_id=1, source_target_pairs={{0,8},{4,12},{8,0},{12,4},{1,9},{5,13},{9,1},{13,5},{2,10},{6,14},... | collective-permute-start | bytes 1179656 | tf_op jit(solution)/shard_map/ppermute | solution.py:328
  25.6 9.9 %collective-permute-done.18.refs_6_ = f32[3,4,64,128]{3,2,1,0:T(8,128)S(1)} collective-permute-done((f32[3,4,64,128]{3,2,1,0:T(8,128)}, f32[3,4,64,128]{3,2,1,0:T(8,128)S(1)}, u32[]{:S(2)}, u32[]{:S(2)}) %collective-permute-start.18) | collective-permute-done | bytes 393248 | tf_op jit(solution)/shard_map/ppermute | solution.py:328
  35.5 2.5 %collective-permute-start.12 = (f32[3,4,64,128]{3,2,1,0:T(8,128)}, f32[3,4,64,128]{3,2,1,0:T(8,128)S(1)}, u32[]{:S(2)}, u32[]{:S(2)}) collective-permute-start(f32[3,4,64,128]{3,2,1,0:T(8,128)} %get-tuple-element.76), channel_id=1, source_target_pairs={{0,12},{4,8},{8,4},{12,0},{1,13},{5,9},{9,5},{13,1},{2,14},{6,10},... | collective-permute-start | bytes 1179656 | tf_op jit(solution)/shard_map/ppermute | solution.py:328
  37.9 2.4 %shard_map.75 = (f32[3,4,64,128]{3,2,1,0:T(8,128)}, f32[3,4,64,128]{3,2,1,0:T(8,128)}, f32[3,4,64,128]{3,2,1,0:T(8,128)}, f32[3,4,64,128]{3,2,1,0:T(8,128)}) custom-call(f32[4,64,1536]{2,1,0:T(8,128)} %refs_0_.6, f32[4,64,1536]{2,1,0:T(8,128)} %refs_1_.6, f32[4,64,1536]{2,1,0:T(8,128)} %refs_2_.6), custom_call_target="tpu_custom_call" | custom-call | bytes 3145728 | tf_op jit(solution)/shard_map/pallas_call | solution.py:61
  40.3 0.1 collective-permute-start.13
  40.4 21.0 %collective-permute-start = (f32[3,4,64,128]{3,2,1,0:T(8,128)}, f32[3,4,64,128]{3,2,1,0:T(8,128)S(1)}, u32[]{:S(2)}, u32[]{:S(2)}) collective-permute-start(f32[3,4,64,128]{3,2,1,0:T(8,128)} %get-tuple-element.66), channel_id=1, source_target_pairs={{0,4},{4,0},{8,12},{12,8},{1,5},{5,1},{9,13},{13,9},{2,6},{6,2},{1... | collective-permute-start | bytes 1179656 | tf_op jit(solution)/shard_map/ppermute | solution.py:328
  61.4 1.1 collective-permute-start.1
  62.5 6.7 %collective-permute-done.11.refs_6_ = f32[3,4,64,128]{3,2,1,0:T(8,128)S(1)} collective-permute-done((f32[3,4,64,128]{3,2,1,0:T(8,128)}, f32[3,4,64,128]{3,2,1,0:T(8,128)S(1)}, u32[]{:S(2)}, u32[]{:S(2)}) %collective-permute-start.11) | collective-permute-done | bytes 393248 | tf_op jit(solution)/shard_map/ppermute | solution.py:328
  69.2 2.5 %collective-permute-start.2 = (f32[3,4,64,128]{3,2,1,0:T(8,128)}, f32[3,4,64,128]{3,2,1,0:T(8,128)S(1)}, u32[]{:S(2)}, u32[]{:S(2)}) collective-permute-start(f32[3,4,64,128]{3,2,1,0:T(8,128)} %get-tuple-element.68), channel_id=1, source_target_pairs={{0,12},{4,8},{8,4},{12,0},{1,13},{5,9},{9,5},{13,1},{2,14},{6,10},... | collective-permute-start | bytes 1179656 | tf_op jit(solution)/shard_map/ppermute | solution.py:328
  71.7 0.5 collective-permute-start.22
  72.2 4.0 %collective-permute-done.refs_5_ = f32[3,4,64,128]{3,2,1,0:T(8,128)S(1)} collective-permute-done((f32[3,4,64,128]{3,2,1,0:T(8,128)}, f32[3,4,64,128]{3,2,1,0:T(8,128)S(1)}, u32[]{:S(2)}, u32[]{:S(2)}) %collective-permute-start) | collective-permute-done | bytes 393248 | tf_op jit(solution)/shard_map/ppermute | solution.py:328
  76.2 0.1 collective-permute-start.23
  76.3 26.6 %collective-permute-done.1.refs_6_ = f32[3,4,64,128]{3,2,1,0:T(8,128)S(1)} collective-permute-done((f32[3,4,64,128]{3,2,1,0:T(8,128)}, f32[3,4,64,128]{3,2,1,0:T(8,128)S(1)}, u32[]{:S(2)}, u32[]{:S(2)}) %collective-permute-start.1) | collective-permute-done | bytes 393248 | tf_op jit(solution)/shard_map/ppermute | solution.py:328
  102.9 0.5 collective-permute-start.15
  103.4 0.1 collective-permute-start.16
  103.5 0.4 collective-permute-start.3
  104.0 0.1 collective-permute-start.4
  104.0 0.6 collective-permute-done.14.refs_9_
  104.6 0.1 collective-permute-start.5
  104.8 0.4 collective-permute-done.15.refs_10_
  105.2 0.1 collective-permute-start.6
  105.4 0.0 copy-start.8
  105.4 0.7 copy-done.8
  106.1 13.8 %shard_map.77 = (f32[1,4,64,128]{3,2,1,0:T(8,128)S(1)}, f32[1,4,64,128]{3,2,1,0:T(8,128)S(1)}, f32[1,4,64,128]{3,2,1,0:T(8,128)S(1)}, f32[1,4,64,128]{3,2,1,0:T(8,128)S(1)}) custom-call(s32[12]{0:T(128)S(1)} %copy-done.5, s32[12]{0:T(128)S(1)} %copy-done.6, s32[12]{0:T(128)S(1)} %copy-done.7, f32[9,16]{1,0:T(8,128)S(1)} %copy-done.8, ...), custom_call_target="tpu_custom_call" | custom-call | flops 1811939328 | bytes 3145728 | tf_op jit(solution)/shard_map/pallas_call | solution.py:257
  119.8 0.0 copy-start.2
  119.8 15.3 %shard_map.78 = (f32[2,4,64,128]{3,2,1,0:T(8,128)S(1)}, f32[2,4,64,128]{3,2,1,0:T(8,128)S(1)}, f32[2,4,64,128]{3,2,1,0:T(8,128)S(1)}, f32[2,4,64,128]{3,2,1,0:T(8,128)S(1)}) custom-call(s32[12]{0:T(128)S(1)} %copy-done.5, s32[12]{0:T(128)S(1)} %copy-done.6, s32[12]{0:T(128)S(1)} %copy-done.7, f32[9,16]{1,0:T(8,128)S(1)} %copy-done.8, ...), custom_call_target="tpu_custom_call" | custom-call | flops 1811939328 | bytes 3145728 | tf_op jit(solution)/shard_map/pallas_call | solution.py:257
  135.1 7.1 %collective-permute-start.24 = (f32[2,4,64,128]{3,2,1,0:T(8,128)S(1)}, f32[2,4,64,128]{3,2,1,0:T(8,128)S(1)}, u32[]{:S(2)}, u32[]{:S(2)}) collective-permute-start(f32[2,4,64,128]{3,2,1,0:T(8,128)S(1)} %get-tuple-element.86), channel_id=1, source_target_pairs={{0,4},{4,0},{8,12},{12,8},{1,5},{5,1},{9,13},{13,9},{2,6},{6,2},{1... | collective-permute-start | bytes 786440 | tf_op jit(solution)/shard_map/ppermute | solution.py:328
  142.3 1.1 collective-permute-start.25
  143.4 1.4 collective-permute-start.26
  144.8 13.8 %shard_map.76 = (f32[1,4,64,128]{3,2,1,0:T(8,128)S(1)}, f32[1,4,64,128]{3,2,1,0:T(8,128)S(1)}, f32[1,4,64,128]{3,2,1,0:T(8,128)S(1)}, f32[1,4,64,128]{3,2,1,0:T(8,128)S(1)}) custom-call(s32[12]{0:T(128)S(1)} %copy-done.5, s32[12]{0:T(128)S(1)} %copy-done.6, s32[12]{0:T(128)S(1)} %copy-done.7, f32[9,16]{1,0:T(8,128)S(1)} %copy-done.8, ...), custom_call_target="tpu_custom_call" | custom-call | flops 1811939328 | bytes 3145728 | tf_op jit(solution)/shard_map/pallas_call | solution.py:257
  158.6 0.6 copy-done.1
  159.2 0.9 collective-permute-start.7
  160.2 2.0 %collective-permute-start.8 = (f32[1,4,64,128]{3,2,1,0:T(8,128)S(1)}, f32[1,4,64,128]{3,2,1,0:T(8,128)S(1)}, u32[]{:S(2)}, u32[]{:S(2)}) collective-permute-start(f32[1,4,64,128]{3,2,1,0:T(8,128)S(1)} %get-tuple-element.71), channel_id=1, source_target_pairs={{0,8},{4,12},{8,0},{12,4},{1,9},{5,13},{9,1},{13,5},{2,10},{6,14},... | collective-permute-start | bytes 393224 | tf_op jit(solution)/shard_map/ppermute | solution.py:328
  162.2 1.4 collective-permute-start.9
  163.7 0.7 copy-done.10
  164.4 0.1 copy-done.11
  164.5 2.0 %shard_map.79.refs_4_ = f32[4,64,1536]{2,1,0:T(8,128)} custom-call(f32[2,4,64,128]{3,2,1,0:T(8,128)} %copy-done, f32[2,4,64,128]{3,2,1,0:T(8,128)} %copy-done.9, f32[2,4,64,128]{3,2,1,0:T(8,128)} %copy-done.10, f32[2,4,64,128]{3,2,1,0:T(8,128)} %copy-done.11), custom_call_target="tpu_custom_call" | custom-call | tf_op jit(solution)/shard_map/pallas_call | solution.py:312
  166.5 11.2 %collective-permute-done.8.refs_2_ = f32[1,4,64,128]{3,2,1,0:T(8,128)S(1)} collective-permute-done((f32[1,4,64,128]{3,2,1,0:T(8,128)S(1)}, f32[1,4,64,128]{3,2,1,0:T(8,128)S(1)}, u32[]{:S(2)}, u32[]{:S(2)}) %collective-permute-start.8) | collective-permute-done | bytes 131104 | tf_op jit(solution)/shard_map/ppermute | solution.py:328
  177.7 0.6 copy-done.13
  178.3 0.0 copy-done.14
  178.4 1.8 %shard_map.80 = f32[4,64,1536]{2,1,0:T(8,128)} custom-call(f32[1,4,64,128]{3,2,1,0:T(8,128)} %copy-done.1, f32[1,4,64,128]{3,2,1,0:T(8,128)} %copy-done.12, f32[1,4,64,128]{3,2,1,0:T(8,128)} %copy-done.13, f32[1,4,64,128]{3,2,1,0:T(8,128)} %copy-done.14, f32[4,64,1536]{2,1,0:T(8,128)} %shard_map.79.refs_4_), custom_call_target="tpu_custom_call", output_to_operand_aliasing={{}: (4, {})} | custom-call | tf_op jit(solution)/shard_map/pallas_call | solution.py:312
  (44 shorter events, 0.1 us)
Async XLA Ops:
  2.4 21.0 %collective-permute-start.17 = (f32[3,4,64,128]{3,2,1,0:T(8,128)}, f32[3,4,64,128]{3,2,1,0:T(8,128)S(1)}, u32[]{:S(2)}, u32[]{:S(2)}) collective-permute-start(f32[3,4,64,128]{3,2,1,0:T(8,128)} %get-tuple-element.78), channel_id=1, source_target_pairs={{0,4},{4,0},{8,12},{12,8},{1,5},{5,1},{9,13},{13,9},{2,6},{6,2},{1... | collective-permute-start | bytes 1179656 | tf_op jit(solution)/shard_map/ppermute | solution.py:328
  5.5 30.0 %collective-permute-start.18 = (f32[3,4,64,128]{3,2,1,0:T(8,128)}, f32[3,4,64,128]{3,2,1,0:T(8,128)S(1)}, u32[]{:S(2)}, u32[]{:S(2)}) collective-permute-start(f32[3,4,64,128]{3,2,1,0:T(8,128)} %get-tuple-element.79), channel_id=1, source_target_pairs={{0,8},{4,12},{8,0},{12,4},{1,9},{5,13},{9,1},{13,5},{2,10},{6,14},... | collective-permute-start | bytes 1179656 | tf_op jit(solution)/shard_map/ppermute | solution.py:328
  8.1 32.2 %collective-permute-start.19 = (f32[3,4,64,128]{3,2,1,0:T(8,128)}, f32[3,4,64,128]{3,2,1,0:T(8,128)S(1)}, u32[]{:S(2)}, u32[]{:S(2)}) collective-permute-start(f32[3,4,64,128]{3,2,1,0:T(8,128)} %get-tuple-element.80), channel_id=1, source_target_pairs={{0,12},{4,8},{8,4},{12,0},{1,13},{5,9},{9,5},{13,1},{2,14},{6,10},... | collective-permute-start | bytes 1179656 | tf_op jit(solution)/shard_map/ppermute | solution.py:328
  8.1 32.3 %collective-permute-start.20 = (f32[3,4,64,128]{3,2,1,0:T(8,128)}, f32[3,4,64,128]{3,2,1,0:T(8,128)S(1)}, u32[]{:S(2)}, u32[]{:S(2)}) collective-permute-start(f32[3,4,64,128]{3,2,1,0:T(8,128)} %get-tuple-element.77.refs_4_), channel_id=1, source_target_pairs={{0,1},{1,0},{2,3},{3,2},{4,5},{5,4},{6,7},{7,6},{8,9},{9,8},{10,11... | collective-permute-start | bytes 1179656 | tf_op jit(solution)/shard_map/ppermute | solution.py:333
  10.5 29.9 %copy-start.4 = (f32[3,4,64,128]{3,2,1,0:T(8,128)S(1)}, f32[3,4,64,128]{3,2,1,0:T(8,128)}, u32[]{:S(2)}) copy-start(f32[3,4,64,128]{3,2,1,0:T(8,128)} %get-tuple-element.73.refs_4_) | copy-start | bytes 1179652
  10.5 94.9 %copy-start.3 = (f32[3,4,64,128]{3,2,1,0:T(8,128)S(1)}, f32[3,4,64,128]{3,2,1,0:T(8,128)}, u32[]{:S(2)}) copy-start(f32[3,4,64,128]{3,2,1,0:T(8,128)} %get-tuple-element.77.refs_4_) | copy-start | bytes 1179652
  10.5 94.9 %copy-start.5 = (s32[12]{0:T(128)S(1)}, s32[12]{0:T(128)}, u32[]{:S(2)}) copy-start(s32[12]{0:T(128)} %refs_0_.9) | copy-start | bytes 148
  10.5 94.9 %copy-start.6 = (s32[12]{0:T(128)S(1)}, s32[12]{0:T(128)}, u32[]{:S(2)}) copy-start(s32[12]{0:T(128)} %refs_1_.9) | copy-start | bytes 148
  10.5 94.8 %copy-start.7 = (s32[12]{0:T(128)S(1)}, s32[12]{0:T(128)}, u32[]{:S(2)}) copy-start(s32[12]{0:T(128)} %refs_2_.9) | copy-start | bytes 148
  10.5 50.9 %collective-permute-start.10 = (f32[3,4,64,128]{3,2,1,0:T(8,128)}, f32[3,4,64,128]{3,2,1,0:T(8,128)S(1)}, u32[]{:S(2)}, u32[]{:S(2)}) collective-permute-start(f32[3,4,64,128]{3,2,1,0:T(8,128)} %get-tuple-element.74), channel_id=1, source_target_pairs={{0,4},{4,0},{8,12},{12,8},{1,5},{5,1},{9,13},{13,9},{2,6},{6,2},{1... | collective-permute-start | bytes 1179656 | tf_op jit(solution)/shard_map/ppermute | solution.py:328
  23.3 45.9 %collective-permute-start.11 = (f32[3,4,64,128]{3,2,1,0:T(8,128)}, f32[3,4,64,128]{3,2,1,0:T(8,128)S(1)}, u32[]{:S(2)}, u32[]{:S(2)}) collective-permute-start(f32[3,4,64,128]{3,2,1,0:T(8,128)} %get-tuple-element.75), channel_id=1, source_target_pairs={{0,8},{4,12},{8,0},{12,4},{1,9},{5,13},{9,1},{13,5},{2,10},{6,14},... | collective-permute-start | bytes 1179656 | tf_op jit(solution)/shard_map/ppermute | solution.py:328
  35.5 36.2 %collective-permute-start.12 = (f32[3,4,64,128]{3,2,1,0:T(8,128)}, f32[3,4,64,128]{3,2,1,0:T(8,128)S(1)}, u32[]{:S(2)}, u32[]{:S(2)}) collective-permute-start(f32[3,4,64,128]{3,2,1,0:T(8,128)} %get-tuple-element.76), channel_id=1, source_target_pairs={{0,12},{4,8},{8,4},{12,0},{1,13},{5,9},{9,5},{13,1},{2,14},{6,10},... | collective-permute-start | bytes 1179656 | tf_op jit(solution)/shard_map/ppermute | solution.py:328
  40.3 31.4 %collective-permute-start.13 = (f32[3,4,64,128]{3,2,1,0:T(8,128)S(1)}, f32[3,4,64,128]{3,2,1,0:T(8,128)S(1)}, u32[]{:S(2)}, u32[]{:S(2)}) collective-permute-start(f32[3,4,64,128]{3,2,1,0:T(8,128)S(1)} %copy-done.4), channel_id=1, source_target_pairs={{0,1},{1,0},{2,3},{3,2},{4,5},{5,4},{6,7},{7,6},{8,9},{9,8},{10,11... | collective-permute-start | bytes 1179656 | tf_op jit(solution)/shard_map/ppermute | solution.py:333
  40.4 35.8 %collective-permute-start = (f32[3,4,64,128]{3,2,1,0:T(8,128)}, f32[3,4,64,128]{3,2,1,0:T(8,128)S(1)}, u32[]{:S(2)}, u32[]{:S(2)}) collective-permute-start(f32[3,4,64,128]{3,2,1,0:T(8,128)} %get-tuple-element.66), channel_id=1, source_target_pairs={{0,4},{4,0},{8,12},{12,8},{1,5},{5,1},{9,13},{13,9},{2,6},{6,2},{1... | collective-permute-start | bytes 1179656 | tf_op jit(solution)/shard_map/ppermute | solution.py:328
  61.4 41.5 %collective-permute-start.1 = (f32[3,4,64,128]{3,2,1,0:T(8,128)}, f32[3,4,64,128]{3,2,1,0:T(8,128)S(1)}, u32[]{:S(2)}, u32[]{:S(2)}) collective-permute-start(f32[3,4,64,128]{3,2,1,0:T(8,128)} %get-tuple-element.67), channel_id=1, source_target_pairs={{0,8},{4,12},{8,0},{12,4},{1,9},{5,13},{9,1},{13,5},{2,10},{6,14},... | collective-permute-start | bytes 1179656 | tf_op jit(solution)/shard_map/ppermute | solution.py:328
  69.2 33.7 %collective-permute-start.2 = (f32[3,4,64,128]{3,2,1,0:T(8,128)}, f32[3,4,64,128]{3,2,1,0:T(8,128)S(1)}, u32[]{:S(2)}, u32[]{:S(2)}) collective-permute-start(f32[3,4,64,128]{3,2,1,0:T(8,128)} %get-tuple-element.68), channel_id=1, source_target_pairs={{0,12},{4,8},{8,4},{12,0},{1,13},{5,9},{9,5},{13,1},{2,14},{6,10},... | collective-permute-start | bytes 1179656 | tf_op jit(solution)/shard_map/ppermute | solution.py:328
  71.7 31.7 %collective-permute-start.21 = (f32[3,4,64,128]{3,2,1,0:T(8,128)S(1)}, f32[3,4,64,128]{3,2,1,0:T(8,128)S(1)}, u32[]{:S(2)}, u32[]{:S(2)}) collective-permute-start(f32[3,4,64,128]{3,2,1,0:T(8,128)S(1)} %collective-permute-done.17.refs_5_), channel_id=1, source_target_pairs={{0,1},{1,0},{2,3},{3,2},{4,5},{5,4},{6,7},{7,6},{8,9},{9,8},{10,11... | collective-permute-start | bytes 1179656 | tf_op jit(solution)/shard_map/ppermute | solution.py:333
  71.7 31.8 %collective-permute-start.22 = (f32[3,4,64,128]{3,2,1,0:T(8,128)S(1)}, f32[3,4,64,128]{3,2,1,0:T(8,128)S(1)}, u32[]{:S(2)}, u32[]{:S(2)}) collective-permute-start(f32[3,4,64,128]{3,2,1,0:T(8,128)S(1)} %collective-permute-done.18.refs_6_), channel_id=1, source_target_pairs={{0,1},{1,0},{2,3},{3,2},{4,5},{5,4},{6,7},{7,6},{8,9},{9,8},{10,11... | collective-permute-start | bytes 1179656 | tf_op jit(solution)/shard_map/ppermute | solution.py:333
  76.2 27.7 %collective-permute-start.23 = (f32[3,4,64,128]{3,2,1,0:T(8,128)S(1)}, f32[3,4,64,128]{3,2,1,0:T(8,128)S(1)}, u32[]{:S(2)}, u32[]{:S(2)}) collective-permute-start(f32[3,4,64,128]{3,2,1,0:T(8,128)S(1)} %collective-permute-done.19.refs_7_), channel_id=1, source_target_pairs={{0,1},{1,0},{2,3},{3,2},{4,5},{5,4},{6,7},{7,6},{8,9},{9,8},{10,11... | collective-permute-start | bytes 1179656 | tf_op jit(solution)/shard_map/ppermute | solution.py:333
  102.9 1.7 collective-permute-start.14
  102.9 2.3 %collective-permute-start.15 = (f32[3,4,64,128]{3,2,1,0:T(8,128)S(1)}, f32[3,4,64,128]{3,2,1,0:T(8,128)S(1)}, u32[]{:S(2)}, u32[]{:S(2)}) collective-permute-start(f32[3,4,64,128]{3,2,1,0:T(8,128)S(1)} %collective-permute-done.11.refs_6_), channel_id=1, source_target_pairs={{0,1},{1,0},{2,3},{3,2},{4,5},{5,4},{6,7},{7,6},{8,9},{9,8},{10,11... | collective-permute-start | bytes 1179656 | tf_op jit(solution)/shard_map/ppermute | solution.py:333
  103.4 16.4 %collective-permute-start.16 = (f32[3,4,64,128]{3,2,1,0:T(8,128)S(1)}, f32[3,4,64,128]{3,2,1,0:T(8,128)S(1)}, u32[]{:S(2)}, u32[]{:S(2)}) collective-permute-start(f32[3,4,64,128]{3,2,1,0:T(8,128)S(1)} %collective-permute-done.12.refs_7_), channel_id=1, source_target_pairs={{0,1},{1,0},{2,3},{3,2},{4,5},{5,4},{6,7},{7,6},{8,9},{9,8},{10,11... | collective-permute-start | bytes 1179656 | tf_op jit(solution)/shard_map/ppermute | solution.py:333
  103.5 38.8 %collective-permute-start.3 = (f32[3,4,64,128]{3,2,1,0:T(8,128)}, f32[3,4,64,128]{3,2,1,0:T(8,128)S(1)}, u32[]{:S(2)}, u32[]{:S(2)}) collective-permute-start(f32[3,4,64,128]{3,2,1,0:T(8,128)} %get-tuple-element.65.refs_4_), channel_id=1, source_target_pairs={{0,1},{1,0},{2,3},{3,2},{4,5},{5,4},{6,7},{7,6},{8,9},{9,8},{10,11... | collective-permute-start | bytes 1179656 | tf_op jit(solution)/shard_map/ppermute | solution.py:333
  104.0 39.4 %collective-permute-start.4 = (f32[3,4,64,128]{3,2,1,0:T(8,128)S(1)}, f32[3,4,64,128]{3,2,1,0:T(8,128)S(1)}, u32[]{:S(2)}, u32[]{:S(2)}) collective-permute-start(f32[3,4,64,128]{3,2,1,0:T(8,128)S(1)} %collective-permute-done.refs_5_), channel_id=1, source_target_pairs={{0,1},{1,0},{2,3},{3,2},{4,5},{5,4},{6,7},{7,6},{8,9},{9,8},{10,11... | collective-permute-start | bytes 1179656 | tf_op jit(solution)/shard_map/ppermute | solution.py:333
  104.6 40.2 %collective-permute-start.5 = (f32[3,4,64,128]{3,2,1,0:T(8,128)S(1)}, f32[3,4,64,128]{3,2,1,0:T(8,128)S(1)}, u32[]{:S(2)}, u32[]{:S(2)}) collective-permute-start(f32[3,4,64,128]{3,2,1,0:T(8,128)S(1)} %collective-permute-done.1.refs_6_), channel_id=1, source_target_pairs={{0,1},{1,0},{2,3},{3,2},{4,5},{5,4},{6,7},{7,6},{8,9},{9,8},{10,11... | collective-permute-start | bytes 1179656 | tf_op jit(solution)/shard_map/ppermute | solution.py:333
  105.2 39.6 %collective-permute-start.6 = (f32[3,4,64,128]{3,2,1,0:T(8,128)S(1)}, f32[3,4,64,128]{3,2,1,0:T(8,128)S(1)}, u32[]{:S(2)}, u32[]{:S(2)}) collective-permute-start(f32[3,4,64,128]{3,2,1,0:T(8,128)S(1)} %collective-permute-done.2.refs_7_), channel_id=1, source_target_pairs={{0,1},{1,0},{2,3},{3,2},{4,5},{5,4},{6,7},{7,6},{8,9},{9,8},{10,11... | collective-permute-start | bytes 1179656 | tf_op jit(solution)/shard_map/ppermute | solution.py:333
  105.4 0.7 copy-start.8
  119.8 25.0 %copy-start.2 = (f32[3,4,64,128]{3,2,1,0:T(8,128)S(1)}, f32[3,4,64,128]{3,2,1,0:T(8,128)}, u32[]{:S(2)}) copy-start(f32[3,4,64,128]{3,2,1,0:T(8,128)} %get-tuple-element.65.refs_4_) | copy-start | bytes 1179652
  135.1 23.5 %copy-start = (f32[2,4,64,128]{3,2,1,0:T(8,128)}, f32[2,4,64,128]{3,2,1,0:T(8,128)S(1)}, u32[]{:S(2)}) copy-start(f32[2,4,64,128]{3,2,1,0:T(8,128)S(1)} %get-tuple-element.85.refs_0_) | copy-start | bytes 786436
  135.1 27.1 %collective-permute-start.24 = (f32[2,4,64,128]{3,2,1,0:T(8,128)S(1)}, f32[2,4,64,128]{3,2,1,0:T(8,128)S(1)}, u32[]{:S(2)}, u32[]{:S(2)}) collective-permute-start(f32[2,4,64,128]{3,2,1,0:T(8,128)S(1)} %get-tuple-element.86), channel_id=1, source_target_pairs={{0,4},{4,0},{8,12},{12,8},{1,5},{5,1},{9,13},{13,9},{2,6},{6,2},{1... | collective-permute-start | bytes 786440 | tf_op jit(solution)/shard_map/ppermute | solution.py:328
  142.3 21.4 %collective-permute-start.25 = (f32[2,4,64,128]{3,2,1,0:T(8,128)S(1)}, f32[2,4,64,128]{3,2,1,0:T(8,128)S(1)}, u32[]{:S(2)}, u32[]{:S(2)}) collective-permute-start(f32[2,4,64,128]{3,2,1,0:T(8,128)S(1)} %get-tuple-element.87), channel_id=1, source_target_pairs={{0,8},{4,12},{8,0},{12,4},{1,9},{5,13},{9,1},{13,5},{2,10},{6,14},... | collective-permute-start | bytes 786440 | tf_op jit(solution)/shard_map/ppermute | solution.py:328
  143.4 20.3 %collective-permute-start.26 = (f32[2,4,64,128]{3,2,1,0:T(8,128)S(1)}, f32[2,4,64,128]{3,2,1,0:T(8,128)S(1)}, u32[]{:S(2)}, u32[]{:S(2)}) collective-permute-start(f32[2,4,64,128]{3,2,1,0:T(8,128)S(1)} %get-tuple-element.88), channel_id=1, source_target_pairs={{0,12},{4,8},{8,4},{12,0},{1,13},{5,9},{9,5},{13,1},{2,14},{6,10},... | collective-permute-start | bytes 786440 | tf_op jit(solution)/shard_map/ppermute | solution.py:328
  158.6 0.6 copy-start.1
  159.2 7.2 %collective-permute-start.7 = (f32[1,4,64,128]{3,2,1,0:T(8,128)S(1)}, f32[1,4,64,128]{3,2,1,0:T(8,128)S(1)}, u32[]{:S(2)}, u32[]{:S(2)}) collective-permute-start(f32[1,4,64,128]{3,2,1,0:T(8,128)S(1)} %get-tuple-element.70), channel_id=1, source_target_pairs={{0,4},{4,0},{8,12},{12,8},{1,5},{5,1},{9,13},{13,9},{2,6},{6,2},{1... | collective-permute-start | bytes 393224 | tf_op jit(solution)/shard_map/ppermute | solution.py:328
  160.2 17.5 %collective-permute-start.8 = (f32[1,4,64,128]{3,2,1,0:T(8,128)S(1)}, f32[1,4,64,128]{3,2,1,0:T(8,128)S(1)}, u32[]{:S(2)}, u32[]{:S(2)}) collective-permute-start(f32[1,4,64,128]{3,2,1,0:T(8,128)S(1)} %get-tuple-element.71), channel_id=1, source_target_pairs={{0,8},{4,12},{8,0},{12,4},{1,9},{5,13},{9,1},{13,5},{2,10},{6,14},... | collective-permute-start | bytes 393224 | tf_op jit(solution)/shard_map/ppermute | solution.py:328
  162.2 1.5 copy-start.9
  162.2 15.5 %collective-permute-start.9 = (f32[1,4,64,128]{3,2,1,0:T(8,128)S(1)}, f32[1,4,64,128]{3,2,1,0:T(8,128)S(1)}, u32[]{:S(2)}, u32[]{:S(2)}) collective-permute-start(f32[1,4,64,128]{3,2,1,0:T(8,128)S(1)} %get-tuple-element.72), channel_id=1, source_target_pairs={{0,12},{4,8},{8,4},{12,0},{1,13},{5,9},{9,5},{13,1},{2,14},{6,10},... | collective-permute-start | bytes 393224 | tf_op jit(solution)/shard_map/ppermute | solution.py:328
  163.6 0.7 copy-start.10
  163.6 0.8 copy-start.11
  166.5 11.2 %copy-start.12 = (f32[1,4,64,128]{3,2,1,0:T(8,128)}, f32[1,4,64,128]{3,2,1,0:T(8,128)S(1)}, u32[]{:S(2)}) copy-start(f32[1,4,64,128]{3,2,1,0:T(8,128)S(1)} %collective-permute-done.7.refs_1_) | copy-start | bytes 393220
  177.7 0.7 copy-start.13
  177.7 0.7 copy-start.14

commit v2 on v1

--- a/solution.py
+++ b/solution.py
@@ -15,6 +15,7 @@
 WMAX = 2
 MASKED = -1e30
 GROUP = 4
+HALF_GROUP = 2
 ATTEND_VMEM = 24 * 2**20
 BLEND = 8
 
@@ -54,12 +55,12 @@
         stores[hop].wait()
 
 
-def pack(slot, parts, queries, key_states, value_states):
-    frames_dev, rows, channels = queries.shape
+def pack(slot, parts, queries, key_states, value_states, per_part):
+    frames_dev, rows, _ = queries.shape
     piece = (3, frames_dev, rows, DH)
     moved = parts * math.prod(piece) * 4
     return pl.pallas_call(
-        functools.partial(pack_kernel, slot, parts, channels // DH // parts),
+        functools.partial(pack_kernel, slot, parts, per_part),
         out_shape=[jax.ShapeDtypeStruct(piece, jnp.float32)] * parts,
         in_specs=[pl.BlockSpec(memory_space=pl.ANY)] * 3,
         out_specs=[pl.BlockSpec(memory_space=pl.ANY)] * parts,
@@ -240,10 +241,9 @@
         copy.wait()
 
 
-def attend_head(slot, parts, scalars, table, mine, theirs, earlier):
+def attend_head(slot, parts, scalars, table, mine, theirs, earlier, per_part):
     _, frames_dev, rows, _ = mine[0].shape
     frames, tokens = frames_dev * parts, 2 * rows
-    per_part = scalars[0].shape[0] // parts
     key_frames = frames // KSTRIDE
     riders = earlier[0].shape[0] if earlier else 0
     result = (riders + 1, frames_dev, rows, DH)
@@ -306,12 +306,12 @@
         copy.wait()
 
 
-def unpack(parts, per_part, first, pieces, out=None):
+def unpack(parts, per_part, first, pieces, channels):
     slots, frames_dev, rows, _ = pieces[0].shape
-    operands = list(pieces) if out is None else [*pieces, out]
+    operands = list(pieces)
     return pl.pallas_call(
         functools.partial(unpack_kernel, parts, per_part, first),
-        out_shape=jax.ShapeDtypeStruct((frames_dev, rows, parts * per_part * DH), jnp.float32),
+        out_shape=jax.ShapeDtypeStruct((frames_dev, rows, channels), jnp.float32),
         in_specs=[pl.BlockSpec(memory_space=pl.ANY)] * len(operands),
         out_specs=pl.BlockSpec(memory_space=pl.ANY),
         scratch_shapes=[
@@ -319,8 +319,496 @@
             pltpu.SemaphoreType.DMA((parts,)),
             pltpu.SemaphoreType.DMA((parts, slots)),
         ],
-        input_output_aliases={} if out is None else {parts: 0},
+        name="unpack",
     )(*operands)
+
+
+def swap_pack_kernel(slots, *refs):
+    sources, out = refs[:3], refs[3]
+    held, load_sem, store_sem = refs[4:]
+    core = lax.axis_index("pos")
+    loads = []
+    for slot in range(slots):
+        for side in range(2):
+            columns = head_columns(slot, side, 1 - core)
+            for kind in range(3):
+                loads.append(
+                    pltpu.make_async_copy(
+                        sources[kind].at[:, :, columns],
+                        held.at[slot, side, kind],
+                        load_sem.at[slot, side, kind],
+                    )
+                )
+                loads[-1].start()
+    stores = []
+    for slot in range(slots):
+        for copy in loads[6 * slot : 6 * slot + 6]:
+            copy.wait()
+        stores.append(pltpu.make_async_copy(held.at[slot], out.at[slot], store_sem.at[slot]))
+        stores[-1].start()
+    for copy in stores:
+        copy.wait()
+
+
+def swap_pack(slots, queries, key_states, value_states):
+    frames_dev, rows, _ = queries.shape
+    piece = (slots, 2, 3, frames_dev, rows, DH)
+    return pl.pallas_call(
+        functools.partial(swap_pack_kernel, slots),
+        out_shape=jax.ShapeDtypeStruct(piece, jnp.float32),
+        in_specs=[pl.BlockSpec(memory_space=pl.ANY)] * 3,
+        out_specs=pl.BlockSpec(memory_space=pl.ANY),
+        scratch_shapes=[
+            pltpu.VMEM(piece, jnp.float32),
+            pltpu.SemaphoreType.DMA((slots, 2, 3)),
+            pltpu.SemaphoreType.DMA((slots,)),
+        ],
+        name="swap_pack",
+    )(queries, key_states, value_states)
+
+
+def full_pack_kernel(slot, *refs):
+    sources, swapped = refs[:3], refs[3]
+    side_out, key_out, halo_out = refs[4], refs[5:7], refs[7:9]
+    held, load_sem, store_sem = refs[9:]
+    frames_dev, rows, _ = sources[0].shape
+    me, core = lax.axis_index("frm"), lax.axis_index("pos")
+    near_end = jnp.where(me < lax.axis_size("frm") // 2, frames_dev - WMAX, 1)
+    near, far = pl.ds(0, rows), pl.ds(rows, rows)
+    loads = []
+    for at in (1, 0):
+        side = lax.bitwise_xor(lax.rem(me, 2), at)
+        columns = head_columns(slot, side, core)
+        for kind in range(3) if at else range(1, 3):
+            loads += [
+                pltpu.make_async_copy(
+                    sources[kind].at[:, :, columns], held.at[at, kind, :, near], load_sem.at[at, kind, 0]
+                ),
+                pltpu.make_async_copy(
+                    swapped.at[slot, side, kind], held.at[at, kind, :, far], load_sem.at[at, kind, 1]
+                ),
+            ]
+    for copy in loads:
+        copy.start()
+    stores = []
+    for at, count in ((1, 6), (0, 4)):
+        for copy in loads[:count]:
+            copy.wait()
+        loads = loads[count:]
+        if at:
+            stores.append(pltpu.make_async_copy(held.at[1], side_out, store_sem.at[0, 0]))
+        stores += [
+            pltpu.make_async_copy(
+                held.at[at, 1:3, pl.ds(near_end, WMAX)], halo_out[at], store_sem.at[1, at]
+            ),
+            pltpu.make_async_copy(held.at[at, 1:3, 0:1], key_out[at], store_sem.at[2, at]),
+        ]
+        for copy in stores[-3 if at else -2 :]:
+            copy.start()
+    for copy in stores:
+        copy.wait()
+
+
+def full_pack(slot, queries, key_states, value_states, swapped):
+    frames_dev, rows, _ = queries.shape
+    tokens = 2 * rows
+    side, key, halo = ((3, frames_dev), (2, 1), (2, WMAX))
+    shapes = [side, key, key, halo, halo]
+    outs = pl.pallas_call(
+        functools.partial(full_pack_kernel, slot),
+        out_shape=[jax.ShapeDtypeStruct((*x, tokens, DH), jnp.float32) for x in shapes],
+        in_specs=[pl.BlockSpec(memory_space=pl.ANY)] * 4,
+        out_specs=[pl.BlockSpec(memory_space=pl.ANY)] * 5,
+        scratch_shapes=[
+            pltpu.VMEM((2, 3, frames_dev, tokens, DH), jnp.float32),
+            pltpu.SemaphoreType.DMA((2, 3, 2)),
+            pltpu.SemaphoreType.DMA((3, 2)),
+        ],
+    )(queries, key_states, value_states, swapped)
+    return outs[0], outs[1:3], outs[3:5]
+
+
+def head_columns(slot, side, core):
+    return pl.ds(pl.multiple_of((4 * slot + 2 * side + core) * DH, DH), DH)
+
+
+def attention(key_rows, bias, value_columns, query_rows):
+    scores = lax.dot_general(
+        key_rows, query_rows, (((1,), (1,)), ((), ())), preferred_element_type=jnp.float32
+    )
+    tokens = scores.shape[0] // len(bias)
+    blocks = [scores[at * tokens : (at + 1) * tokens] for at in range(len(bias))]
+    peaks = [jnp.max(block, axis=0, keepdims=True) + shift for block, shift in zip(blocks, bias)]
+    highest = functools.reduce(jnp.maximum, peaks)
+    weights = jnp.concatenate(
+        [jnp.exp2(block - (highest - shift)) for block, shift in zip(blocks, bias)], axis=0
+    )
+    total = jnp.sum(weights, axis=0, keepdims=True)
+    high, low = split(weights)
+    wide = jnp.dot(value_columns, high, preferred_element_type=jnp.float32)
+    rest = jnp.dot(value_columns[:DH], low, preferred_element_type=jnp.float32)
+    return (wide[:DH] + wide[DH:] + rest) / total
+
+
+def waves(frames, top):
+    angle = 2.0 * np.pi / frames * np.arange(frames // 2)
+    rows = [np.ones(frames // 2)]
+    for k in range(1, top + 1):
+        rows += [np.cos(k * angle), np.sin(k * angle)]
+    return [[float(x) for x in row] for row in rows]
+
+
+def half_sign(row, half):
+    return 1.0 - 2.0 * half.astype(jnp.float32) if (row + 1) // 2 % 2 else 1.0
+
+
+def attend_half_kernel(slot, parts, top, *refs):
+    windows, strides = refs[:2]
+    sources, refs = refs[2:5], refs[5:]
+    swapped, beside = refs[:2]
+    keys, halos, refs = refs[2:4], refs[4:6], refs[6:]
+    local_out, sums_out, refs = refs[0], refs[1], refs[2:]
+    (q_in, k_in, v_in, kx_in, vx_in, q_cat, k_cat, v_cat, kg_cat, vg_cat, local, diff, sums) = refs[:13]
+    load_sem, far_sem, store_sem = refs[13:]
+    frames, tokens, _ = q_in.shape
+    frames_dev, rows = frames // 2, tokens // 2
+    me, core = lax.axis_index("frm"), lax.axis_index("pos")
+    half, side = me // 2, lax.rem(me, 2)
+    head = 4 * slot + 2 * side + core
+    window, stride = windows[head], strides[head]
+    columns = head_columns(slot, side, core)
+    mine = pl.ds(side * frames_dev, frames_dev)
+    others = pl.ds((1 - side) * frames_dev, frames_dev)
+    near, far = pl.ds(0, rows), pl.ds(rows, rows)
+
+    copies = []
+    for at, target in enumerate((q_in, k_in, v_in)):
+        copies += [
+            pltpu.make_async_copy(sources[at].at[:, :, columns], target.at[mine, near], load_sem.at[at, 0]),
+            pltpu.make_async_copy(
+                swapped.at[slot, side, at], target.at[mine, far], load_sem.at[at, 1]
+            ),
+            pltpu.make_async_copy(beside.at[at], target.at[others], load_sem.at[at, 2]),
+        ]
+    for kind, target in enumerate((kx_in, vx_in)):
+        for at in range(2):
+            copies.append(
+                pltpu.make_async_copy(
+                    keys[at].at[kind], target.at[pl.ds(at, 1)], far_sem.at[0, kind, at]
+                )
+            )
+    for copy in copies:
+        copy.start()
+    inner = (me > 0) & (me < parts - 1)
+
+    def halo_copies(source):
+        return [
+            pltpu.make_async_copy(
+                halos[source].at[kind], target.at[pl.ds(2, WMAX)], far_sem.at[1, kind, 0]
+            )
+            for kind, target in enumerate((kx_in, vx_in))
+        ]
+
+    for taken, first in ((inner, 1), (jnp.logical_not(inner), 0)):
+
+        @pl.when(taken)
+        def _(first=first):
+            for copy in halo_copies(first):
+                copy.start()
+            for copy in halo_copies(first):
+                copy.wait()
+
+    for copy in copies:
+        copy.wait()
+
+    score_scale = DH ** (-0.5) * math.log2(math.e)
+
+    def place(keys_f32, values_f32, to_keys, to_values, block):
+        at = pl.ds(pl.multiple_of(block * tokens, tokens), tokens)
+        k_high, k_low = split(keys_f32)
+        to_keys[at, 0:DH] = k_high
+        to_keys[at, DH : 2 * DH] = k_high
+        to_keys[at, 2 * DH : 3 * DH] = k_low
+        v_high, v_low = split(values_f32.T)
+        to_values[0:DH, at] = v_high
+        to_values[DH : 2 * DH, at] = v_low
+
+    def prepare(frame, carry):
+        at = pl.ds(pl.multiple_of(frame * tokens, tokens), tokens)
+        high, low = split(q_in[frame] * score_scale)
+        q_cat[at, 0:DH] = high
+        q_cat[at, DH : 2 * DH] = low
+        q_cat[at, 2 * DH : 3 * DH] = high
+        place(k_in[frame], v_in[frame], k_cat, v_cat, frame + WMAX)
+        return carry
+
+    lax.fori_loop(0, frames, prepare, 0)
+    edge = jnp.where(half == 0, frames + WMAX, 0)
+    edge_from = (jnp.where(half == 0, side, 2), jnp.where(half == 0, 2, 3))
+    for at in range(WMAX):
+        place(kx_in[edge_from[at]], vx_in[edge_from[at]], k_cat, v_cat, edge + at)
+    key_frame = [frames * half, frames * half + frames_dev]
+    for at in range(2):
+        source, target = pl.ds((WMAX + at * frames_dev) * tokens, tokens), pl.ds(at * tokens, tokens)
+        kg_cat[target, :] = k_cat[source, :]
+        vg_cat[:, target] = v_cat[:, source]
+        place(kx_in[at], vx_in[at], kg_cat, vg_cat, 2 + at)
+        key_frame.append(lax.bitwise_xor(me, 2 + at) * frames_dev)
+    global_bias = [jnp.where(lax.rem(frame, stride) == 0, 0.0, MASKED) for frame in key_frame]
+
+    group = HALF_GROUP
+    reach = 2 * WMAX + group
+    group_rows = group * tokens
+    lane_frame = lax.broadcasted_iota(jnp.int32, (1, group_rows), 1) // tokens
+    lowest = WMAX * (1 - half)
+
+    def per_group(step, carry):
+        first = step * group + WMAX
+        start = jnp.clip(first - WMAX, lowest, lowest + frames + WMAX - reach)
+        q_part = q_cat[pl.ds(pl.multiple_of(step * group_rows, group_rows), group_rows), :]
+        k_at = pl.ds(pl.multiple_of(start * tokens, tokens), reach * tokens)
+        local_bias = [
+            jnp.where(jnp.abs(start + at - first - lane_frame) <= window, 0.0, MASKED)
+            for at in range(reach)
+        ]
+        local_part = attention(k_cat[k_at, :], local_bias, v_cat[:, k_at], q_part)
+        global_part = attention(kg_cat[...], global_bias, vg_cat[...], q_part)
+        difference = (global_part - local_part).T
+        local_part = local_part.T
+        for at in range(group):
+            local[step * group + at] = local_part[at * tokens : (at + 1) * tokens]
+            diff[step * group + at] = difference[at * tokens : (at + 1) * tokens]
+        return carry
+
+    lax.fori_loop(0, frames // group, per_group, 0)
+    to_local = pltpu.make_async_copy(local, local_out, store_sem.at[0])
+    to_local.start()
+    table = waves(2 * frames, top)
+
+    def gather(row, carry):
+        at = pl.ds(pl.multiple_of(row * BLEND, BLEND), BLEND)
+        parts_of = [diff[frame, at] for frame in range(frames)]
+        for wave, values in enumerate(table):
+            total = sum(value * part for value, part in zip(values, parts_of))
+            sums[wave, at] = total * half_sign(wave, half)
+        return carry
+
+    lax.fori_loop(0, tokens // BLEND, gather, 0)
+    to_sums = pltpu.make_async_copy(sums, sums_out, store_sem.at[1])
+    to_sums.start()
+    to_local.wait()
+    to_sums.wait()
+
+
+def attend_half(slot, parts, top, scalars, sources, swapped, beside, keys, halos):
+    frames_dev, rows, _ = sources[0].shape
+    frames, tokens = 2 * frames_dev, 2 * rows
+    waves_count = 2 * top + 1
+    f32, bf16 = jnp.float32, jnp.bfloat16
+    return pl.pallas_call(
+        functools.partial(attend_half_kernel, slot, parts, top),
+        out_shape=[
+            jax.ShapeDtypeStruct((frames, tokens, DH), f32),
+            jax.ShapeDtypeStruct((waves_count, tokens, DH), f32),
+        ],
+        in_specs=[pl.BlockSpec(memory_space=pltpu.SMEM)] * 2
+        + [pl.BlockSpec(memory_space=pl.ANY)] * 9,
+        out_specs=[pl.BlockSpec(memory_space=pl.ANY)] * 2,
+        scratch_shapes=[pltpu.VMEM((frames, tokens, DH), f32)] * 3
+        + [pltpu.VMEM((4, tokens, DH), f32)] * 2
+        + [
+            pltpu.VMEM((frames * tokens, 3 * DH), bf16),
+            pltpu.VMEM(((frames + 2 * WMAX) * tokens, 3 * DH), bf16),
+            pltpu.VMEM((2 * DH, (frames + 2 * WMAX) * tokens), bf16),
+            pltpu.VMEM((4 * tokens, 3 * DH), bf16),
+            pltpu.VMEM((2 * DH, 4 * tokens), bf16),
+            pltpu.VMEM((frames, tokens, DH), f32),
+            pltpu.VMEM((frames, tokens, DH), f32),
+            pltpu.VMEM((waves_count, tokens, DH), f32),
+            pltpu.SemaphoreType.DMA((3, 3)),
+            pltpu.SemaphoreType.DMA((2, 2, 2)),
+            pltpu.SemaphoreType.DMA((2,)),
+        ],
+        cost_estimate=pl.CostEstimate(
+            flops=12 * frames * tokens * 10 * tokens * DH,
+            bytes_accessed=6 * frames * tokens * DH * 4,
+            transcendentals=frames * tokens * 10 * tokens,
+        ),
+        compiler_params=pltpu.CompilerParams(vmem_limit_bytes=ATTEND_VMEM),
+    )(*scalars[:2], *sources, swapped, beside, *keys, *halos)
+
+
+def mix_kernel(first, slots, top, *refs):
+    cutoffs, refs = refs[0], refs[1:]
+    outs, scratch = refs[3 * slots : 3 * slots + 4], refs[3 * slots + 4 :]
+    local, own, other, load_sem, store_sem = scratch
+    _, frames, tokens, _ = local.shape
+    frames_dev, rows = frames // 2, tokens // 2
+    me, core = lax.axis_index("frm"), lax.axis_index("pos")
+    half, side = me // 2, lax.rem(me, 2)
+    copies = [
+        [
+            pltpu.make_async_copy(refs[slots * at + slot], target.at[slot], load_sem.at[slot, at])
+            for at, target in enumerate((own, other, local))
+        ]
+        for slot in range(slots)
+    ]
+    for copy in sum(copies, []):
+        copy.start()
+    table = waves(2 * frames, top)
+    mine = pl.ds(side * frames_dev, frames_dev)
+    others = pl.ds((1 - side) * frames_dev, frames_dev)
+    near, far = pl.ds(0, rows), pl.ds(rows, rows)
+    stores = []
+    for slot in range(slots):
+        cutoff = cutoffs[4 * (first + slot) + 2 * side + core]
+        scales = []
+        for wave in range(len(table)):
+            k = (wave + 1) // 2
+            share = (1.0 if k == 0 else 2.0) / (2 * frames)
+            scales.append(jnp.where(cutoff >= k, share, 0.0) * half_sign(wave, half))
+        for copy in copies[slot]:
+            copy.wait()
+
+        def blend(row, carry, slot=slot, scales=scales):
+            at = pl.ds(pl.multiple_of(row * BLEND, BLEND), BLEND)
+            parts_of = [
+                scale * (own[slot, wave, at] + other[slot, wave, at])
+                for wave, scale in enumerate(scales)
+            ]
+            for frame in range(frames):
+                local[slot, frame, at] += sum(
+                    values[frame] * part for values, part in zip(table, parts_of)
+                )
+            return carry
+
+        lax.fori_loop(0, tokens // BLEND, blend, 0)
+        for at, span in enumerate(((others, near), (others, far), (mine, far), (mine, near))):
+            stores.append(
+                pltpu.make_async_copy(
+                    local.at[slot, *span], outs[at].at[slot], store_sem.at[slot, at]
+                )
+            )
+            stores[-1].start()
+    for copy in stores:
+        copy.wait()
+
+
+def mix(first, top, cutoffs, halves, passed):
+    slots = len(halves)
+    frames, tokens, _ = halves[0][0].shape
+    sums = passed[0].shape
+    piece = (slots, frames // 2, tokens // 2, DH)
+    return pl.pallas_call(
+        functools.partial(mix_kernel, first, slots, top),
+        out_shape=[jax.ShapeDtypeStruct(piece, jnp.float32)] * 4,
+        in_specs=[pl.BlockSpec(memory_space=pltpu.SMEM)]
+        + [pl.BlockSpec(memory_space=pl.ANY)] * (3 * slots),
+        out_specs=[pl.BlockSpec(memory_space=pl.ANY)] * 4,
+        scratch_shapes=[
+            pltpu.VMEM((slots, frames, tokens, DH), jnp.float32),
+            pltpu.VMEM((slots, *sums), jnp.float32),
+            pltpu.VMEM((slots, *sums), jnp.float32),
+            pltpu.SemaphoreType.DMA((slots, 3)),
+            pltpu.SemaphoreType.DMA((slots, 4)),
+        ],
+    )(cutoffs, *[x[1] for x in halves], *passed, *[x[0] for x in halves])
+
+
+def half_unpack_kernel(first, *refs):
+    pieces, refs = refs[:4], refs[4:]
+    out, held, load_sem, store_sem = refs[-4:]
+    slots = held.shape[1]
+    me, core = lax.axis_index("frm"), lax.axis_index("pos")
+    flips = ((1, 0), (1, 1), (0, 1), (0, 0))
+    loads, stores = [], []
+    for at in range(4):
+        loads.append(pltpu.make_async_copy(pieces[at], held.at[at], load_sem.at[at]))
+        loads[-1].start()
+    for at, (side, flip) in enumerate(flips):
+        loads[at].wait()
+        for slot in range(slots):
+            columns = head_columns(
+                first + slot, lax.bitwise_xor(lax.rem(me, 2), side), lax.bitwise_xor(core, flip)
+            )
+            stores.append(
+                pltpu.make_async_copy(
+                    held.at[at, slot], out.at[:, :, columns], store_sem.at[at, slot]
+                )
+            )
+            stores[-1].start()
+    for copy in stores:
+        copy.wait()
+
+
+def half_unpack(first, pieces, out):
+    slots, frames_dev, rows, _ = pieces[0].shape
+    return pl.pallas_call(
+        functools.partial(half_unpack_kernel, first),
+        out_shape=jax.ShapeDtypeStruct(out.shape, jnp.float32),
+        in_specs=[pl.BlockSpec(memory_space=pl.ANY)] * 5,
+        out_specs=pl.BlockSpec(memory_space=pl.ANY),
+        scratch_shapes=[
+            pltpu.VMEM((4, slots, frames_dev, rows, DH), jnp.float32),
+            pltpu.SemaphoreType.DMA((4,)),
+            pltpu.SemaphoreType.DMA((4, slots)),
+        ],
+        input_output_aliases={4: 0},
+    )(*pieces, out)
+
+
+def across(value, hop, flip, chips=None):
+    chips = range(lax.axis_size("frm")) if chips is None else chips
+    pairs = [(2 * z + c, 2 * (z ^ hop) + (c ^ flip)) for z in chips for c in range(2)]
+    return lax.ppermute(value, ("frm", "pos"), pairs)
+
+
+def by_halves(queries, key_states, value_states, windows, strides, cutoffs):
+    parts = lax.axis_size("frm")
+    frames_dev, _, channels = queries.shape
+    slots = channels // DH // 4 - 1
+    frames = frames_dev * parts
+    top = frames // 8
+    table = jnp.asarray(lowpass_table(frames))
+    scalars, sources = (windows, strides, cutoffs), (queries, key_states, value_states)
+    inner = (parts // 2 - 1, parts // 2)
+    packed = pack(4 * slots, parts, *sources, 1)
+    packed, sources = lax.optimization_barrier((packed, sources))
+    mine = [packed[0]] + [None] * (parts - 1)
+    for hop in wires(parts):
+        mine[hop] = around(packed[hop], hop)
+    swapped = across(swap_pack(slots, *sources), 0, 1)
+    beside, far_keys, far_halos = [], [], []
+    for slot in range(slots):
+        side, keys, halos = full_pack(slot, *sources, swapped)
+        far_keys.append([])
+        far_halos.append([])
+        for at in range(2):
+            far_halos[-1].append(across(halos[at], 2 + at, 0, inner))
+            far_keys[-1].append(across(keys[at], 2 + at, 0))
+        beside.append(across(side, 1, 0))
+    theirs = []
+    for hop in range(parts):
+        theirs.append(swap(mine[hop]))
+    done = attend_head(4 * slots, parts, scalars, table, mine, theirs, (), 1)
+    landed = [done[0]] + [None] * (parts - 1)
+    for hop in wires(parts):
+        landed[hop] = around(done[hop], hop)
+    pieces = []
+    for slot in range(slots):
+        half = attend_half(
+            slot, parts, top, scalars, sources, swapped, beside[slot], far_keys[slot], far_halos[slot]
+        )
+        passed = across(half[1], 2, 0)
+        mixed = mix(slot, top, cutoffs, [half], [passed])
+        near = across(mixed[0], 1, 0)
+        far = across(mixed[1], 1, 1)
+        other = across(mixed[2], 0, 1)
+        pieces.append([near, far, other, mixed[3]])
+    out = unpack(parts, 1, 4 * slots, landed, channels)
+    for slot in range(slots):
+        out = half_unpack(slot, pieces[slot], out)
+    return out
 
 
 def around(value, hop):
@@ -331,36 +819,6 @@
 def swap(value):
     size = lax.axis_size("pos")
     return lax.ppermute(value, "pos", [(i, size - 1 - i) for i in range(size)])
-
-
-def by_heads(queries, key_states, value_states, windows, strides, cutoffs):
-    parts = lax.axis_size("frm")
-    per_part = queries.shape[2] // DH // parts
-    frames = queries.shape[0] * parts
-    table = jnp.asarray(lowpass_table(frames))
-    scalars = (windows, strides, cutoffs)
-    packed, sources, moved = [], (queries, key_states, value_states), []
-    for slot in range(per_part):
-        packed.append(pack(slot, parts, *sources))
-        packed[-1], sources = lax.optimization_barrier((packed[-1], sources))
-        moved.append([packed[-1][0]] + [None] * (parts - 1))
-        for hop in wires(parts):
-            moved[-1][hop] = around(packed[-1][hop], hop)
-    earlier, out, first = (), None, 0
-    for slot, mine in enumerate(moved):
-        theirs = []
-        for hop in range(parts):
-            theirs.append(swap(mine[hop]))
-        done = attend_head(slot, parts, scalars, table, mine, theirs, earlier)
-        if slot < per_part - 2:
-            earlier = done
-            continue
-        earlier, landed = (), [done[0]] + [None] * (parts - 1)
-        for hop in wires(parts):
-            landed[hop] = around(done[hop], hop)
-        out = unpack(parts, per_part, first, landed, out)
-        first = slot + 1
-    return out
 
 
 def with_halo(value, sides, width):
@@ -480,14 +938,14 @@
     return blended.reshape(frames_dev, half_tokens, channels)
 
 
-def splits_by_heads(heads_local, parts, pos_count):
-    return heads_local % parts == 0 and pos_count == 2 and parts.bit_count() == 1
+def in_halves(heads_local, frames_dev, parts, pos_count):
+    return heads_local % 4 == 0 and heads_local > 4 and frames_dev == KSTRIDE and (parts, pos_count) == (4, 2)
 
 
 def shards(queries, key_states, value_states, windows, strides, cutoffs):
     heads_local = queries.shape[2] // DH
-    if splits_by_heads(heads_local, lax.axis_size("frm"), lax.axis_size("pos")):
-        return by_heads(queries, key_states, value_states, windows, strides, cutoffs)
+    if in_halves(heads_local, queries.shape[0], lax.axis_size("frm"), lax.axis_size("pos")):
+        return by_halves(queries, key_states, value_states, windows, strides, cutoffs)
     return by_frames(queries, key_states, value_states, windows, strides, cutoffs)
 
 

time: 180 us -> 173 us (0.961)
  starting transfers between devices: 52 us -> 33.3 us
  local copies, waits for them, and re-layouts: 2.86 us -> 8.3 us
  Pallas kernels: 53.7 us -> 56.5 us
  waiting for transfers between devices: 71.3 us -> 73.4 us
    ppermute x0 -> x19, waiting for transfers between devices: none -> 54.7 us  [across(): return lax.ppermute(value, ('frm', 'pos'), pairs)]
    ppermute x15 -> x6, waiting for transfers between devices: 70.3 us -> 18.7 us  [around(): return lax.ppermute(value, 'frm', [(i, i ^ hop) for i in range(size)])]
    ppermute x15 -> x6, starting transfers between devices: 50 us -> 9.62 us  [around(): return lax.ppermute(value, 'frm', [(i, i ^ hop) for i in range(size)])]
    pallas_call x3 -> x10, Pallas kernels: 7.09 us -> 41.2 us  [the longest x2 21.6 us: attend_half(): pl.pallas_call(functools.partial(attend_half_kernel, slot, parts, top), o...]
    pallas_call x3 -> x1, Pallas kernels: 42.8 us -> 13.4 us  [attend_head(): pl.pallas_call(functools.partial(attend_kernel, slot, parts, per_part, ri...]
    ppermute x0 -> x19, starting transfers between devices: none -> 23.1 us  [across(): return lax.ppermute(value, ('frm', 'pos'), pairs)]
    unnamed x30 -> x52, local copies, waits for them, and re-layouts: 2.86 us -> 8.3 us
    pallas_call x2 -> x1, Pallas kernels: 3.82 us -> 1.85 us  [unpack(): pl.pallas_call(functools.partial(unpack_kernel, parts, per_part, first),...]
  transfers between devices with their start and end apart: 27 -> 29, of which waited for: 8 -> 10; matrix products, arithmetic and copies ran while one was open for 0% -> 0% of each run, Pallas kernels for 27% -> 29%
where the time goes in v2:
time: 173 us; the launch traced here: 172 us
  waiting for transfers between devices  73.4 us (42%)
  Pallas kernels  56.5 us (33%)
  starting transfers between devices  33.3 us (19%)
  local copies, waits for them, and re-layouts  8.3 us (5%)
    ppermute x19, waiting for transfers between devices, across(): return lax.ppermute(value, ('frm', 'pos'), pairs)  54.7 us
    ppermute x19, starting transfers between devices, across(): return lax.ppermute(value, ('frm', 'pos'), pairs)  23.1 us
    pallas_call x2, Pallas kernels, attend_half(): pl.pallas_call(functools.partial(attend_half_kernel, slot, parts, top), o...  21.6 us
    ppermute x6, waiting for transfers between devices, around(): return lax.ppermute(value, 'frm', [(i, i ^ hop) for i in range(size)])  18.7 us
    pallas_call x1, Pallas kernels, attend_head(): pl.pallas_call(functools.partial(attend_kernel, slot, parts, per_part, ri...  13.4 us
    ppermute x6, starting transfers between devices, around(): return lax.ppermute(value, 'frm', [(i, i ^ hop) for i in range(size)])  9.62 us
    unnamed x52, local copies, waits for them, and re-layouts  8.3 us
    pallas_call x2, Pallas kernels, mix(): pl.pallas_call(functools.partial(mix_kernel, first, slots, top), out_shap...  6.15 us
  transfers between devices with their start and end apart: 29, of which 10 were waited for; matrix products, arithmetic and copies ran while one was open for 0% of the time, Pallas kernels for 29%

profile of v2, /device:TPU:0, one launch (start us, length us, event | category | flops | bytes accessed | tf_op | source)
XLA Modules:
  0.0 171.9 jit_solution(15133931321062326344)
XLA Ops:
  0.0 2.4 %shard_map.73 = (f32[3,4,64,128]{3,2,1,0:T(8,128)}, f32[3,4,64,128]{3,2,1,0:T(8,128)}, f32[3,4,64,128]{3,2,1,0:T(8,128)}, f32[3,4,64,128]{3,2,1,0:T(8,128)}) custom-call(f32[4,64,1536]{2,1,0:T(8,128)} %refs_2_.7, f32[4,64,1536]{2,1,0:T(8,128)} %refs_3_.2, f32[4,64,1536]{2,1,0:T(8,128)} %refs_4_.1), custom_call_target="tpu_custom_call" | custom-call | bytes 3145728 | tf_op jit(solution)/shard_map/pallas_call | solution.py:62
  2.4 2.5 %swap_pack.1 = f32[2,2,3,4,64,128]{5,4,3,2,1,0:T(8,128)} custom-call(f32[4,64,1536]{2,1,0:T(8,128)} %refs_2_.7, f32[4,64,1536]{2,1,0:T(8,128)} %refs_3_.2, f32[4,64,1536]{2,1,0:T(8,128)} %refs_4_.1), custom_call_target="tpu_custom_call" | custom-call | tf_op jit(solution)/shard_map/swap_pack/pallas_call | solution.py:356
  5.5 2.6 %collective-permute-start.19 = (f32[3,4,64,128]{3,2,1,0:T(8,128)}, f32[3,4,64,128]{3,2,1,0:T(8,128)}, u32[]{:S(2)}, u32[]{:S(2)}) collective-permute-start(f32[3,4,64,128]{3,2,1,0:T(8,128)} %get-tuple-element.72), channel_id=1, source_target_pairs={{0,4},{4,0},{8,12},{12,8},{1,5},{5,1},{9,13},{13,9},{2,6},{6,2},{1... | collective-permute-start | bytes 1179656 | tf_op jit(solution)/shard_map/ppermute | solution.py:816
  8.1 2.6 %collective-permute-start.20 = (f32[3,4,64,128]{3,2,1,0:T(8,128)}, f32[3,4,64,128]{3,2,1,0:T(8,128)}, u32[]{:S(2)}, u32[]{:S(2)}) collective-permute-start(f32[3,4,64,128]{3,2,1,0:T(8,128)} %get-tuple-element.73), channel_id=1, source_target_pairs={{0,8},{4,12},{8,0},{12,4},{1,9},{5,13},{9,1},{13,5},{2,10},{6,14},... | collective-permute-start | bytes 1179656 | tf_op jit(solution)/shard_map/ppermute | solution.py:816
  10.7 1.1 copy-done.3
  11.8 2.5 %shard_map.77 = (f32[3,4,128,128]{3,2,1,0:T(8,128)}, f32[2,1,128,128]{3,2,1,0:T(8,128)}, f32[2,1,128,128]{3,2,1,0:T(8,128)}, f32[2,2,128,128]{3,2,1,0:T(8,128)}, f32[2,2,128,128]{3,2,1,0:T(8,128)}) custom-call(f32[4,64,1536]{2,1,0:T(8,128)} %refs_2_.7, f32[4,64,1536]{2,1,0:T(8,128)} %refs_3_.2, f32[4,64,1536]{2,1,0:T(8,128)} %refs_4_.1, ...), custom_call_target="tpu_custom_call" | custom-call | tf_op jit(solution)/shard_map/pallas_call | solution.py:417
  14.4 1.0 collective-permute-start.10
  15.4 2.5 %shard_map.74 = (f32[3,4,128,128]{3,2,1,0:T(8,128)}, f32[2,1,128,128]{3,2,1,0:T(8,128)}, f32[2,1,128,128]{3,2,1,0:T(8,128)}, f32[2,2,128,128]{3,2,1,0:T(8,128)}, f32[2,2,128,128]{3,2,1,0:T(8,128)}) custom-call(f32[4,64,1536]{2,1,0:T(8,128)} %refs_2_.7, f32[4,64,1536]{2,1,0:T(8,128)} %refs_3_.2, f32[4,64,1536]{2,1,0:T(8,128)} %refs_4_.1, ...), custom_call_target="tpu_custom_call" | custom-call | tf_op jit(solution)/shard_map/pallas_call | solution.py:417
  17.9 1.2 collective-permute-start.1
  19.1 7.3 %collective-permute-done.19.refs_5_ = f32[3,4,64,128]{3,2,1,0:T(8,128)} collective-permute-done((f32[3,4,64,128]{3,2,1,0:T(8,128)}, f32[3,4,64,128]{3,2,1,0:T(8,128)}, u32[]{:S(2)}, u32[]{:S(2)}) %collective-permute-start.19) | collective-permute-done | bytes 393248 | tf_op jit(solution)/shard_map/ppermute | solution.py:816
  26.3 1.4 collective-permute-start.11
  27.7 10.5 %collective-permute-done.20.refs_6_ = f32[3,4,64,128]{3,2,1,0:T(8,128)} collective-permute-done((f32[3,4,64,128]{3,2,1,0:T(8,128)}, f32[3,4,64,128]{3,2,1,0:T(8,128)}, u32[]{:S(2)}, u32[]{:S(2)}) %collective-permute-start.20) | collective-permute-done | bytes 393248 | tf_op jit(solution)/shard_map/ppermute | solution.py:816
  38.2 2.5 %collective-permute-start.12 = (f32[2,1,128,128]{3,2,1,0:T(8,128)}, f32[2,1,128,128]{3,2,1,0:T(8,128)S(1)}, u32[]{:S(2)}, u32[]{:S(2)}) collective-permute-start(f32[2,1,128,128]{3,2,1,0:T(8,128)} %get-tuple-element.62), channel_id=1, source_target_pairs={{0,12},{1,13},{4,8},{5,9},{8,4},{9,5},{12,0},{13,1},{2,14},{3,15},... | collective-permute-start | bytes 393224 | tf_op jit(solution)/shard_map/ppermute | solution.py:763
  40.7 1.3 collective-permute-start.13
  42.0 29.4 %collective-permute-done.11.refs_7_ = f32[2,1,128,128]{3,2,1,0:T(8,128)S(1)} collective-permute-done((f32[2,1,128,128]{3,2,1,0:T(8,128)}, f32[2,1,128,128]{3,2,1,0:T(8,128)S(1)}, u32[]{:S(2)}, u32[]{:S(2)}) %collective-permute-start.11) | collective-permute-done | bytes 131104 | tf_op jit(solution)/shard_map/ppermute | solution.py:763
  71.4 3.3 %collective-permute-start.2 = (f32[2,1,128,128]{3,2,1,0:T(8,128)}, f32[2,1,128,128]{3,2,1,0:T(8,128)S(1)}, u32[]{:S(2)}, u32[]{:S(2)}) collective-permute-start(f32[2,1,128,128]{3,2,1,0:T(8,128)} %get-tuple-element.50), channel_id=1, source_target_pairs={{0,8},{1,9},{4,12},{5,13},{8,0},{9,1},{12,4},{13,5},{2,10},{3,11},... | collective-permute-start | bytes 393224 | tf_op jit(solution)/shard_map/ppermute | solution.py:763
  74.7 2.0 %collective-permute-done.12.refs_8_ = f32[2,1,128,128]{3,2,1,0:T(8,128)S(1)} collective-permute-done((f32[2,1,128,128]{3,2,1,0:T(8,128)}, f32[2,1,128,128]{3,2,1,0:T(8,128)S(1)}, u32[]{:S(2)}, u32[]{:S(2)}) %collective-permute-start.12) | collective-permute-done | bytes 131104 | tf_op jit(solution)/shard_map/ppermute | solution.py:763
  76.7 1.3 collective-permute-start.3
  78.0 7.1 %collective-permute-done.2.refs_7_ = f32[2,1,128,128]{3,2,1,0:T(8,128)S(1)} collective-permute-done((f32[2,1,128,128]{3,2,1,0:T(8,128)}, f32[2,1,128,128]{3,2,1,0:T(8,128)S(1)}, u32[]{:S(2)}, u32[]{:S(2)}) %collective-permute-start.2) | collective-permute-done | bytes 131104 | tf_op jit(solution)/shard_map/ppermute | solution.py:763
  85.1 0.7 collective-permute-start.14
  85.8 1.3 collective-permute-start.4
  87.1 0.7 collective-permute-start.5
  87.9 12.5 %collective-permute-done.4.refs_9_ = f32[2,2,128,128]{3,2,1,0:T(8,128)S(1)} collective-permute-done((f32[2,2,128,128]{3,2,1,0:T(8,128)}, f32[2,2,128,128]{3,2,1,0:T(8,128)S(1)}, u32[]{:S(2)}, u32[]{:S(2)}) %collective-permute-start.4) | collective-permute-done | bytes 262176 | tf_op jit(solution)/shard_map/ppermute | solution.py:763
  101.0 1.4 copy-done.2
  102.4 1.4 copy-done.4
  103.8 10.9 %shard_map.78 = (f32[8,128,128]{2,1,0:T(8,128)S(1)}, f32[5,128,128]{2,1,0:T(8,128)S(1)}) custom-call(s32[12]{0:T(128)S(1)} %copy-done.10, s32[12]{0:T(128)S(1)} %copy-done.11, f32[4,64,1536]{2,1,0:T(8,128)S(1)} %copy-done, f32[4,64,1536]{2,1,0:T(8,128)S(1)} %copy-done.1, f32[4,64,1536]{2,1,0:T(8,128)S(1)} %copy-done.2, ...), custom_call_target="tpu_custom_call" | custom-call | flops 2013265920 | bytes 3145728 | tf_op jit(solution)/shard_map/pallas_call | solution.py:608
  114.7 0.8 copy-done.6
  115.5 5.8 %collective-permute-start.15 = (f32[5,128,128]{2,1,0:T(8,128)S(1)}, f32[5,128,128]{2,1,0:T(8,128)S(1)}, u32[]{:S(2)}, u32[]{:S(2)}) collective-permute-start(f32[5,128,128]{2,1,0:T(8,128)S(1)} %get-tuple-element.65.refs_1_), channel_id=1, source_target_pairs={{0,8},{1,9},{4,12},{5,13},{8,0},{9,1},{12,4},{13,5},{2,10},{3,11},... | collective-permute-start | bytes 983048 | tf_op jit(solution)/shard_map/ppermute | solution.py:763
  121.3 10.7 %shard_map.75 = (f32[8,128,128]{2,1,0:T(8,128)S(1)}, f32[5,128,128]{2,1,0:T(8,128)S(1)}) custom-call(s32[12]{0:T(128)S(1)} %copy-done.10, s32[12]{0:T(128)S(1)} %copy-done.11, f32[4,64,1536]{2,1,0:T(8,128)S(1)} %copy-done, f32[4,64,1536]{2,1,0:T(8,128)S(1)} %copy-done.1, f32[4,64,1536]{2,1,0:T(8,128)S(1)} %copy-done.2, ...), custom_call_target="tpu_custom_call" | custom-call | flops 2013265920 | bytes 3145728 | tf_op jit(solution)/shard_map/pallas_call | solution.py:608
  132.2 13.4 %shard_map.80 = (f32[1,4,64,128]{3,2,1,0:T(8,128)S(1)}, f32[1,4,64,128]{3,2,1,0:T(8,128)S(1)}, f32[1,4,64,128]{3,2,1,0:T(8,128)S(1)}, f32[1,4,64,128]{3,2,1,0:T(8,128)S(1)}) custom-call(s32[12]{0:T(128)S(1)} %copy-done.10, s32[12]{0:T(128)S(1)} %copy-done.11, s32[12]{0:T(128)S(1)} %copy-done.12, f32[9,16]{1,0:T(8,128)S(1)} %copy-done.13, ...), custom_call_target="tpu_custom_call" | custom-call | flops 1811939328 | bytes 3145728 | tf_op jit(solution)/shard_map/pallas_call | solution.py:257
  145.6 0.6 copy-done.9
  146.3 1.9 %collective-permute-start.26 = (f32[1,4,64,128]{3,2,1,0:T(8,128)S(1)}, f32[1,4,64,128]{3,2,1,0:T(8,128)S(1)}, u32[]{:S(2)}, u32[]{:S(2)}) collective-permute-start(f32[1,4,64,128]{3,2,1,0:T(8,128)S(1)} %get-tuple-element.76), channel_id=1, source_target_pairs={{0,4},{4,0},{8,12},{12,8},{1,5},{5,1},{9,13},{13,9},{2,6},{6,2},{1... | collective-permute-start | bytes 393224 | tf_op jit(solution)/shard_map/ppermute | solution.py:816
  148.2 1.0 collective-permute-start.27
  149.2 1.5 collective-permute-start.28
  150.7 0.7 copy-done.15
  151.4 3.1 %shard_map.79 = (f32[1,4,64,128]{3,2,1,0:T(8,128)}, f32[1,4,64,128]{3,2,1,0:T(8,128)}, f32[1,4,64,128]{3,2,1,0:T(8,128)}, f32[1,4,64,128]{3,2,1,0:T(8,128)}) custom-call(s32[12]{0:T(128)} %refs_2_.8, f32[5,128,128]{2,1,0:T(8,128)} %copy-done.8, f32[5,128,128]{2,1,0:T(8,128)} %copy-done.15, f32[8,128,128]{2,1,0:T(8,128)} %copy-done.6), custom_call_target="tpu_custom_call" | custom-call | tf_op jit(solution)/shard_map/pallas_call | solution.py:702
  154.5 1.1 collective-permute-start.16
  155.6 0.7 copy-done.14
  156.3 3.1 %shard_map.76 = (f32[1,4,64,128]{3,2,1,0:T(8,128)}, f32[1,4,64,128]{3,2,1,0:T(8,128)}, f32[1,4,64,128]{3,2,1,0:T(8,128)}, f32[1,4,64,128]{3,2,1,0:T(8,128)}) custom-call(s32[12]{0:T(128)} %refs_2_.8, f32[5,128,128]{2,1,0:T(8,128)} %copy-done.7, f32[5,128,128]{2,1,0:T(8,128)} %copy-done.14, f32[8,128,128]{2,1,0:T(8,128)} %copy-done.5), custom_call_target="tpu_custom_call" | custom-call | tf_op jit(solution)/shard_map/pallas_call | solution.py:702
  159.9 0.9 collective-permute-done.27.refs_2_
  161.3 1.6 collective-permute-done.16.refs_0_
  162.9 1.9 %unpack.1.refs_4_ = f32[4,64,1536]{2,1,0:T(8,128)} custom-call(f32[1,4,64,128]{3,2,1,0:T(8,128)} %copy-done.9, f32[1,4,64,128]{3,2,1,0:T(8,128)} %copy-done.16, f32[1,4,64,128]{3,2,1,0:T(8,128)} %copy-done.17, f32[1,4,64,128]{3,2,1,0:T(8,128)} %copy-done.18), custom_call_target="tpu_custom_call" | custom-call | tf_op jit(solution)/shard_map/unpack/pallas_call | solution.py:312
  164.8 0.6 copy-done.20
  165.5 1.8 %shard_map.81.refs_4_ = f32[4,64,1536]{2,1,0:T(8,128)} custom-call(f32[1,4,64,128]{3,2,1,0:T(8,128)} %copy-done.19, f32[1,4,64,128]{3,2,1,0:T(8,128)} %copy-done.20, f32[1,4,64,128]{3,2,1,0:T(8,128)} %copy-done.23, f32[1,4,64,128]{3,2,1,0:T(8,128)} %get-tuple-element.70.refs_3_, f32[4,64,1536]{2,1,0:T(8,128)} %unpack.1.refs_4_), custom_call_target="tpu_custom_call", output_to_operand_aliasing={{}: (4, {})} | custom-call | tf_op jit(solution)/shard_map/pallas_call | solution.py:746
  167.3 1.2 collective-permute-done.7.refs_0_
  168.5 0.9 collective-permute-done.8.refs_1_
  169.4 0.6 copy-done.22
  170.1 1.8 %shard_map.82 = f32[4,64,1536]{2,1,0:T(8,128)} custom-call(f32[1,4,64,128]{3,2,1,0:T(8,128)} %copy-done.21, f32[1,4,64,128]{3,2,1,0:T(8,128)} %copy-done.22, f32[1,4,64,128]{3,2,1,0:T(8,128)} %copy-done.24, f32[1,4,64,128]{3,2,1,0:T(8,128)} %get-tuple-element.59.refs_3_, f32[4,64,1536]{2,1,0:T(8,128)} %shard_map.81.refs_4_), custom_call_target="tpu_custom_call", output_to_operand_aliasing={{}: (4, {})} | custom-call | tf_op jit(solution)/shard_map/pallas_call | solution.py:746
  (74 shorter events, 2.6 us)
Async XLA Ops:
  2.4 8.3 %copy-start.25 = (f32[3,4,64,128]{3,2,1,0:T(8,128)S(1)}, f32[3,4,64,128]{3,2,1,0:T(8,128)}, u32[]{:S(2)}) copy-start(f32[3,4,64,128]{3,2,1,0:T(8,128)} %get-tuple-element.74) | copy-start | bytes 1179652
  4.9 5.8 %collective-permute-start = (f32[2,2,3,4,64,128]{5,4,3,2,1,0:T(8,128)}, f32[2,2,3,4,64,128]{5,4,3,2,1,0:T(8,128)S(1)}, u32[]{:S(2)}, u32[]{:S(2)}) collective-permute-start(f32[2,2,3,4,64,128]{5,4,3,2,1,0:T(8,128)} %swap_pack.1), channel_id=1, source_target_pairs={{0,1},{1,0},{4,5},{5,4},{8,9},{9,8},{12,13},{13,12},{2,3},{3,2},{6... | collective-permute-start | bytes 4718600 | tf_op jit(solution)/shard_map/ppermute | solution.py:763
  5.5 20.9 %collective-permute-start.19 = (f32[3,4,64,128]{3,2,1,0:T(8,128)}, f32[3,4,64,128]{3,2,1,0:T(8,128)}, u32[]{:S(2)}, u32[]{:S(2)}) collective-permute-start(f32[3,4,64,128]{3,2,1,0:T(8,128)} %get-tuple-element.72), channel_id=1, source_target_pairs={{0,4},{4,0},{8,12},{12,8},{1,5},{5,1},{9,13},{13,9},{2,6},{6,2},{1... | collective-permute-start | bytes 1179656 | tf_op jit(solution)/shard_map/ppermute | solution.py:816
  8.1 30.1 %collective-permute-start.20 = (f32[3,4,64,128]{3,2,1,0:T(8,128)}, f32[3,4,64,128]{3,2,1,0:T(8,128)}, u32[]{:S(2)}, u32[]{:S(2)}) collective-permute-start(f32[3,4,64,128]{3,2,1,0:T(8,128)} %get-tuple-element.73), channel_id=1, source_target_pairs={{0,8},{4,12},{8,0},{12,4},{1,9},{5,13},{9,1},{13,5},{2,10},{6,14},... | collective-permute-start | bytes 1179656 | tf_op jit(solution)/shard_map/ppermute | solution.py:816
  10.7 30.0 %collective-permute-start.21 = (f32[3,4,64,128]{3,2,1,0:T(8,128)S(1)}, f32[3,4,64,128]{3,2,1,0:T(8,128)}, u32[]{:S(2)}, u32[]{:S(2)}) collective-permute-start(f32[3,4,64,128]{3,2,1,0:T(8,128)S(1)} %copy-done.25), channel_id=1, source_target_pairs={{0,12},{4,8},{8,4},{12,0},{1,13},{5,9},{9,5},{13,1},{2,14},{6,10},... | collective-permute-start | bytes 1179656 | tf_op jit(solution)/shard_map/ppermute | solution.py:816
  10.7 1.1 copy-start.3
  14.4 86.6 %copy-start = (f32[4,64,1536]{2,1,0:T(8,128)S(1)}, f32[4,64,1536]{2,1,0:T(8,128)}, u32[]{:S(2)}) copy-start(f32[4,64,1536]{2,1,0:T(8,128)} %refs_2_.7) | copy-start | bytes 4718596
  14.4 86.6 %copy-start.1 = (f32[4,64,1536]{2,1,0:T(8,128)S(1)}, f32[4,64,1536]{2,1,0:T(8,128)}, u32[]{:S(2)}) copy-start(f32[4,64,1536]{2,1,0:T(8,128)} %refs_3_.2) | copy-start | bytes 4718596
  14.4 86.6 %copy-start.10 = (s32[12]{0:T(128)S(1)}, s32[12]{0:T(128)}, u32[]{:S(2)}) copy-start(s32[12]{0:T(128)} %refs_0_.14) | copy-start | bytes 148
  14.4 86.6 %copy-start.11 = (s32[12]{0:T(128)S(1)}, s32[12]{0:T(128)}, u32[]{:S(2)}) copy-start(s32[12]{0:T(128)} %refs_1_.10) | copy-start | bytes 148
  14.4 86.5 %collective-permute-start.10 = (f32[3,4,128,128]{3,2,1,0:T(8,128)}, f32[3,4,128,128]{3,2,1,0:T(8,128)}, u32[]{:S(2)}, u32[]{:S(2)}) collective-permute-start(f32[3,4,128,128]{3,2,1,0:T(8,128)} %get-tuple-element.60), channel_id=1, source_target_pairs={{0,4},{1,5},{4,0},{5,1},{8,12},{9,13},{12,8},{13,9},{2,6},{3,7},{6... | collective-permute-start | bytes 2359304 | tf_op jit(solution)/shard_map/ppermute | solution.py:763
  17.9 97.6 %collective-permute-start.1 = (f32[3,4,128,128]{3,2,1,0:T(8,128)}, f32[3,4,128,128]{3,2,1,0:T(8,128)S(1)}, u32[]{:S(2)}, u32[]{:S(2)}) collective-permute-start(f32[3,4,128,128]{3,2,1,0:T(8,128)} %get-tuple-element.49), channel_id=1, source_target_pairs={{0,4},{1,5},{4,0},{5,1},{8,12},{9,13},{12,8},{13,9},{2,6},{3,7},{6... | collective-permute-start | bytes 2359304 | tf_op jit(solution)/shard_map/ppermute | solution.py:763
  26.3 45.0 %collective-permute-start.11 = (f32[2,1,128,128]{3,2,1,0:T(8,128)}, f32[2,1,128,128]{3,2,1,0:T(8,128)S(1)}, u32[]{:S(2)}, u32[]{:S(2)}) collective-permute-start(f32[2,1,128,128]{3,2,1,0:T(8,128)} %get-tuple-element.61), channel_id=1, source_target_pairs={{0,8},{1,9},{4,12},{5,13},{8,0},{9,1},{12,4},{13,5},{2,10},{3,11},... | collective-permute-start | bytes 393224 | tf_op jit(solution)/shard_map/ppermute | solution.py:763
  38.2 38.4 %collective-permute-start.12 = (f32[2,1,128,128]{3,2,1,0:T(8,128)}, f32[2,1,128,128]{3,2,1,0:T(8,128)S(1)}, u32[]{:S(2)}, u32[]{:S(2)}) collective-permute-start(f32[2,1,128,128]{3,2,1,0:T(8,128)} %get-tuple-element.62), channel_id=1, source_target_pairs={{0,12},{1,13},{4,8},{5,9},{8,4},{9,5},{12,0},{13,1},{2,14},{3,15},... | collective-permute-start | bytes 393224 | tf_op jit(solution)/shard_map/ppermute | solution.py:763
  40.7 46.3 %collective-permute-start.13 = (f32[2,2,128,128]{3,2,1,0:T(8,128)}, f32[2,2,128,128]{3,2,1,0:T(8,128)S(1)}, u32[]{:S(2)}, u32[]{:S(2)}) collective-permute-start(f32[2,2,128,128]{3,2,1,0:T(8,128)} %get-tuple-element.63), channel_id=1, source_target_pairs={{4,12},{5,13},{8,0},{9,1},{6,14},{7,15},{10,2},{11,3},{20,28},{21,... | collective-permute-start | bytes 786440 | tf_op jit(solution)/shard_map/ppermute | solution.py:763
  71.4 13.7 %collective-permute-start.2 = (f32[2,1,128,128]{3,2,1,0:T(8,128)}, f32[2,1,128,128]{3,2,1,0:T(8,128)S(1)}, u32[]{:S(2)}, u32[]{:S(2)}) collective-permute-start(f32[2,1,128,128]{3,2,1,0:T(8,128)} %get-tuple-element.50), channel_id=1, source_target_pairs={{0,8},{1,9},{4,12},{5,13},{8,0},{9,1},{12,4},{13,5},{2,10},{3,11},... | collective-permute-start | bytes 393224 | tf_op jit(solution)/shard_map/ppermute | solution.py:763
  76.7 9.1 %collective-permute-start.3 = (f32[2,1,128,128]{3,2,1,0:T(8,128)}, f32[2,1,128,128]{3,2,1,0:T(8,128)S(1)}, u32[]{:S(2)}, u32[]{:S(2)}) collective-permute-start(f32[2,1,128,128]{3,2,1,0:T(8,128)} %get-tuple-element.51), channel_id=1, source_target_pairs={{0,12},{1,13},{4,8},{5,9},{8,4},{9,5},{12,0},{13,1},{2,14},{3,15},... | collective-permute-start | bytes 393224 | tf_op jit(solution)/shard_map/ppermute | solution.py:763
  85.1 2.7 %collective-permute-start.14 = (f32[2,2,128,128]{3,2,1,0:T(8,128)}, f32[2,2,128,128]{3,2,1,0:T(8,128)S(1)}, u32[]{:S(2)}, u32[]{:S(2)}) collective-permute-start(f32[2,2,128,128]{3,2,1,0:T(8,128)} %get-tuple-element.64), channel_id=1, source_target_pairs={{4,8},{5,9},{8,4},{9,5},{6,10},{7,11},{10,6},{11,7},{20,24},{21,25... | collective-permute-start | bytes 786440 | tf_op jit(solution)/shard_map/ppermute | solution.py:763
  85.8 14.6 %collective-permute-start.4 = (f32[2,2,128,128]{3,2,1,0:T(8,128)}, f32[2,2,128,128]{3,2,1,0:T(8,128)S(1)}, u32[]{:S(2)}, u32[]{:S(2)}) collective-permute-start(f32[2,2,128,128]{3,2,1,0:T(8,128)} %get-tuple-element.52), channel_id=1, source_target_pairs={{4,12},{5,13},{8,0},{9,1},{6,14},{7,15},{10,2},{11,3},{20,28},{21,... | collective-permute-start | bytes 786440 | tf_op jit(solution)/shard_map/ppermute | solution.py:763
  87.1 13.3 %collective-permute-start.5 = (f32[2,2,128,128]{3,2,1,0:T(8,128)}, f32[2,2,128,128]{3,2,1,0:T(8,128)S(1)}, u32[]{:S(2)}, u32[]{:S(2)}) collective-permute-start(f32[2,2,128,128]{3,2,1,0:T(8,128)} %get-tuple-element.53), channel_id=1, source_target_pairs={{4,8},{5,9},{8,4},{9,5},{6,10},{7,11},{10,6},{11,7},{20,24},{21,25... | collective-permute-start | bytes 786440 | tf_op jit(solution)/shard_map/ppermute | solution.py:763
  87.8 44.2 %collective-permute-start.22 = (f32[3,4,64,128]{3,2,1,0:T(8,128)}, f32[3,4,64,128]{3,2,1,0:T(8,128)S(1)}, u32[]{:S(2)}, u32[]{:S(2)}) collective-permute-start(f32[3,4,64,128]{3,2,1,0:T(8,128)} %get-tuple-element.71.refs_4_), channel_id=1, source_target_pairs={{0,1},{1,0},{2,3},{3,2},{4,5},{5,4},{6,7},{7,6},{8,9},{9,8},{10,11... | collective-permute-start | bytes 1179656 | tf_op jit(solution)/shard_map/ppermute | solution.py:821
  100.4 31.7 %collective-permute-start.23 = (f32[3,4,64,128]{3,2,1,0:T(8,128)}, f32[3,4,64,128]{3,2,1,0:T(8,128)S(1)}, u32[]{:S(2)}, u32[]{:S(2)}) collective-permute-start(f32[3,4,64,128]{3,2,1,0:T(8,128)} %collective-permute-done.19.refs_5_), channel_id=1, source_target_pairs={{0,1},{1,0},{2,3},{3,2},{4,5},{5,4},{6,7},{7,6},{8,9},{9,8},{10,11... | collective-permute-start | bytes 1179656 | tf_op jit(solution)/shard_map/ppermute | solution.py:821
  100.4 31.8 %collective-permute-start.24 = (f32[3,4,64,128]{3,2,1,0:T(8,128)}, f32[3,4,64,128]{3,2,1,0:T(8,128)S(1)}, u32[]{:S(2)}, u32[]{:S(2)}) collective-permute-start(f32[3,4,64,128]{3,2,1,0:T(8,128)} %collective-permute-done.20.refs_6_), channel_id=1, source_target_pairs={{0,1},{1,0},{2,3},{3,2},{4,5},{5,4},{6,7},{7,6},{8,9},{9,8},{10,11... | collective-permute-start | bytes 1179656 | tf_op jit(solution)/shard_map/ppermute | solution.py:821
  100.9 31.2 %collective-permute-start.25 = (f32[3,4,64,128]{3,2,1,0:T(8,128)}, f32[3,4,64,128]{3,2,1,0:T(8,128)S(1)}, u32[]{:S(2)}, u32[]{:S(2)}) collective-permute-start(f32[3,4,64,128]{3,2,1,0:T(8,128)} %collective-permute-done.21.refs_7_), channel_id=1, source_target_pairs={{0,1},{1,0},{2,3},{3,2},{4,5},{5,4},{6,7},{7,6},{8,9},{9,8},{10,11... | collective-permute-start | bytes 1179656 | tf_op jit(solution)/shard_map/ppermute | solution.py:821
  101.0 1.4 copy-start.2
  102.4 1.4 copy-start.4
  114.7 0.8 copy-start.6
  115.5 16.5 %copy-start.8 = (f32[5,128,128]{2,1,0:T(8,128)}, f32[5,128,128]{2,1,0:T(8,128)S(1)}, u32[]{:S(2)}) copy-start(f32[5,128,128]{2,1,0:T(8,128)S(1)} %get-tuple-element.65.refs_1_) | copy-start | bytes 983044
  115.5 16.6 %copy-start.12 = (s32[12]{0:T(128)S(1)}, s32[12]{0:T(128)}, u32[]{:S(2)}) copy-start(s32[12]{0:T(128)} %refs_2_.8) | copy-start | bytes 148
  115.5 16.6 %copy-start.13 = (f32[9,16]{1,0:T(8,128)S(1)}, f32[9,16]{1,0:T(8,128)}, u32[]{:S(2)}) copy-start(f32[9,16]{1,0:T(8,128)} %constant.2.clone.refs_3_) | copy-start | bytes 1732
  115.5 35.1 %collective-permute-start.15 = (f32[5,128,128]{2,1,0:T(8,128)S(1)}, f32[5,128,128]{2,1,0:T(8,128)S(1)}, u32[]{:S(2)}, u32[]{:S(2)}) collective-permute-start(f32[5,128,128]{2,1,0:T(8,128)S(1)} %get-tuple-element.65.refs_1_), channel_id=1, source_target_pairs={{0,8},{1,9},{4,12},{5,13},{8,0},{9,1},{12,4},{13,5},{2,10},{3,11},... | collective-permute-start | bytes 983048 | tf_op jit(solution)/shard_map/ppermute | solution.py:763
  132.0 13.6 %copy-start.5 = (f32[8,128,128]{2,1,0:T(8,128)}, f32[8,128,128]{2,1,0:T(8,128)S(1)}, u32[]{:S(2)}) copy-start(f32[8,128,128]{2,1,0:T(8,128)S(1)} %get-tuple-element.55.refs_3_) | copy-start | bytes 1572868
  132.0 13.6 %copy-start.7 = (f32[5,128,128]{2,1,0:T(8,128)}, f32[5,128,128]{2,1,0:T(8,128)S(1)}, u32[]{:S(2)}) copy-start(f32[5,128,128]{2,1,0:T(8,128)S(1)} %get-tuple-element.54.refs_1_) | copy-start | bytes 983044
  132.0 23.5 %collective-permute-start.6 = (f32[5,128,128]{2,1,0:T(8,128)S(1)}, f32[5,128,128]{2,1,0:T(8,128)S(1)}, u32[]{:S(2)}, u32[]{:S(2)}) collective-permute-start(f32[5,128,128]{2,1,0:T(8,128)S(1)} %get-tuple-element.54.refs_1_), channel_id=1, source_target_pairs={{0,8},{1,9},{4,12},{5,13},{8,0},{9,1},{12,4},{13,5},{2,10},{3,11},... | collective-permute-start | bytes 983048 | tf_op jit(solution)/shard_map/ppermute | solution.py:763
  146.3 13.1 %collective-permute-start.26 = (f32[1,4,64,128]{3,2,1,0:T(8,128)S(1)}, f32[1,4,64,128]{3,2,1,0:T(8,128)S(1)}, u32[]{:S(2)}, u32[]{:S(2)}) collective-permute-start(f32[1,4,64,128]{3,2,1,0:T(8,128)S(1)} %get-tuple-element.76), channel_id=1, source_target_pairs={{0,4},{4,0},{8,12},{12,8},{1,5},{5,1},{9,13},{13,9},{2,6},{6,2},{1... | collective-permute-start | bytes 393224 | tf_op jit(solution)/shard_map/ppermute | solution.py:816
  148.2 12.5 %collective-permute-start.27 = (f32[1,4,64,128]{3,2,1,0:T(8,128)S(1)}, f32[1,4,64,128]{3,2,1,0:T(8,128)S(1)}, u32[]{:S(2)}, u32[]{:S(2)}) collective-permute-start(f32[1,4,64,128]{3,2,1,0:T(8,128)S(1)} %get-tuple-element.77), channel_id=1, source_target_pairs={{0,8},{4,12},{8,0},{12,4},{1,9},{5,13},{9,1},{13,5},{2,10},{6,14},... | collective-permute-start | bytes 393224 | tf_op jit(solution)/shard_map/ppermute | solution.py:816
  149.2 11.7 %collective-permute-start.28 = (f32[1,4,64,128]{3,2,1,0:T(8,128)S(1)}, f32[1,4,64,128]{3,2,1,0:T(8,128)S(1)}, u32[]{:S(2)}, u32[]{:S(2)}) collective-permute-start(f32[1,4,64,128]{3,2,1,0:T(8,128)S(1)} %get-tuple-element.78), channel_id=1, source_target_pairs={{0,12},{4,8},{8,4},{12,0},{1,13},{5,9},{9,5},{13,1},{2,14},{6,10},... | collective-permute-start | bytes 393224 | tf_op jit(solution)/shard_map/ppermute | solution.py:816
  154.5 8.4 %collective-permute-start.16 = (f32[1,4,64,128]{3,2,1,0:T(8,128)}, f32[1,4,64,128]{3,2,1,0:T(8,128)S(1)}, u32[]{:S(2)}, u32[]{:S(2)}) collective-permute-start(f32[1,4,64,128]{3,2,1,0:T(8,128)} %get-tuple-element.67), channel_id=1, source_target_pairs={{0,4},{1,5},{4,0},{5,1},{8,12},{9,13},{12,8},{13,9},{2,6},{3,7},{6... | collective-permute-start | bytes 393224 | tf_op jit(solution)/shard_map/ppermute | solution.py:763
  155.5 9.2 %collective-permute-start.17 = (f32[1,4,64,128]{3,2,1,0:T(8,128)}, f32[1,4,64,128]{3,2,1,0:T(8,128)S(1)}, u32[]{:S(2)}, u32[]{:S(2)}) collective-permute-start(f32[1,4,64,128]{3,2,1,0:T(8,128)} %get-tuple-element.68), channel_id=1, source_target_pairs={{0,5},{1,4},{4,1},{5,0},{8,13},{9,12},{12,9},{13,8},{2,7},{3,6},{6... | collective-permute-start | bytes 393224 | tf_op jit(solution)/shard_map/ppermute | solution.py:763
  159.4 3.5 %copy-start.16 = (f32[1,4,64,128]{3,2,1,0:T(8,128)}, f32[1,4,64,128]{3,2,1,0:T(8,128)S(1)}, u32[]{:S(2)}) copy-start(f32[1,4,64,128]{3,2,1,0:T(8,128)S(1)} %collective-permute-done.26.refs_1_) | copy-start | bytes 393220
  159.4 5.4 %collective-permute-start.18 = (f32[1,4,64,128]{3,2,1,0:T(8,128)}, f32[1,4,64,128]{3,2,1,0:T(8,128)S(1)}, u32[]{:S(2)}, u32[]{:S(2)}) collective-permute-start(f32[1,4,64,128]{3,2,1,0:T(8,128)} %get-tuple-element.69), channel_id=1, source_target_pairs={{0,1},{1,0},{4,5},{5,4},{8,9},{9,8},{12,13},{13,12},{2,3},{3,2},{6... | collective-permute-start | bytes 393224 | tf_op jit(solution)/shard_map/ppermute | solution.py:763
  160.7 2.2 %copy-start.17 = (f32[1,4,64,128]{3,2,1,0:T(8,128)}, f32[1,4,64,128]{3,2,1,0:T(8,128)S(1)}, u32[]{:S(2)}) copy-start(f32[1,4,64,128]{3,2,1,0:T(8,128)S(1)} %collective-permute-done.27.refs_2_) | copy-start | bytes 393220
  160.7 7.8 %collective-permute-start.7 = (f32[1,4,64,128]{3,2,1,0:T(8,128)}, f32[1,4,64,128]{3,2,1,0:T(8,128)S(1)}, u32[]{:S(2)}, u32[]{:S(2)}) collective-permute-start(f32[1,4,64,128]{3,2,1,0:T(8,128)} %get-tuple-element.56), channel_id=1, source_target_pairs={{0,4},{1,5},{4,0},{5,1},{8,12},{9,13},{12,8},{13,9},{2,6},{3,7},{6... | collective-permute-start | bytes 393224 | tf_op jit(solution)/shard_map/ppermute | solution.py:763
  160.9 2.0 %copy-start.18 = (f32[1,4,64,128]{3,2,1,0:T(8,128)}, f32[1,4,64,128]{3,2,1,0:T(8,128)S(1)}, u32[]{:S(2)}) copy-start(f32[1,4,64,128]{3,2,1,0:T(8,128)S(1)} %collective-permute-done.28.refs_3_) | copy-start | bytes 393220
  160.9 8.5 %collective-permute-start.8 = (f32[1,4,64,128]{3,2,1,0:T(8,128)}, f32[1,4,64,128]{3,2,1,0:T(8,128)S(1)}, u32[]{:S(2)}, u32[]{:S(2)}) collective-permute-start(f32[1,4,64,128]{3,2,1,0:T(8,128)} %get-tuple-element.57), channel_id=1, source_target_pairs={{0,5},{1,4},{4,1},{5,0},{8,13},{9,12},{12,9},{13,8},{2,7},{3,6},{6... | collective-permute-start | bytes 393224 | tf_op jit(solution)/shard_map/ppermute | solution.py:763
  162.9 1.9 %copy-start.19 = (f32[1,4,64,128]{3,2,1,0:T(8,128)}, f32[1,4,64,128]{3,2,1,0:T(8,128)S(1)}, u32[]{:S(2)}) copy-start(f32[1,4,64,128]{3,2,1,0:T(8,128)S(1)} %collective-permute-done.16.refs_0_) | copy-start | bytes 393220
  162.9 6.5 %collective-permute-start.9 = (f32[1,4,64,128]{3,2,1,0:T(8,128)}, f32[1,4,64,128]{3,2,1,0:T(8,128)S(1)}, u32[]{:S(2)}, u32[]{:S(2)}) collective-permute-start(f32[1,4,64,128]{3,2,1,0:T(8,128)} %get-tuple-element.58), channel_id=1, source_target_pairs={{0,1},{1,0},{4,5},{5,4},{8,9},{9,8},{12,13},{13,12},{2,3},{3,2},{6... | collective-permute-start | bytes 393224 | tf_op jit(solution)/shard_map/ppermute | solution.py:763
  168.5 0.9 copy-start.21
  (7 other events, 4.8 us)

commit v3 on v2

--- a/solution.py
+++ b/solution.py
@@ -15,8 +15,10 @@
 WMAX = 2
 MASKED = -1e30
 GROUP = 4
-HALF_GROUP = 2
-ATTEND_VMEM = 24 * 2**20
+HALF_GROUP = 4
+ATTEND_VMEM = 30 * 2**20
+MOVE_VMEM = 10 * 2**20
+FIRST_VMEM = 60 * 2**20
 BLEND = 8
 
 
@@ -70,6 +72,7 @@
             pltpu.SemaphoreType.DMA((parts,)),
         ],
         cost_estimate=pl.CostEstimate(flops=0, bytes_accessed=2 * moved, transcendentals=0),
+        compiler_params=pltpu.CompilerParams(vmem_limit_bytes=FIRST_VMEM),
     )(queries, key_states, value_states)
 
 
@@ -78,11 +81,10 @@
     return high, (value - high.astype(jnp.float32)).astype(jnp.bfloat16)
 
 
-def attend_kernel(slot, parts, per_part, riders, *refs):
+def attend_kernel(slot, parts, per_part, *refs):
     windows, strides, cutoffs, table = refs[:4]
     refs = refs[4:]
     mine, theirs, refs = refs[:parts], refs[parts : 2 * parts], refs[2 * parts :]
-    earlier, refs = (refs[:parts], refs[parts:]) if riders else ((), refs)
     outs, refs = refs[:parts], refs[parts:]
     (q_in, k_in, v_in, q_cat, k_cat, v_cat, kg_cat, vg_cat, local, diff, load_sem, store_sem) = refs[
         :12
@@ -113,15 +115,6 @@
             copy.start()
             loads[-1].append(copy)
 
-    if riders:
-        held, ride_sem = refs[12:]
-        rides = [
-            pltpu.make_async_copy(earlier[hop], held.at[hop], ride_sem.at[0, hop])
-            for hop in range(parts)
-        ]
-        for copy in rides:
-            copy.start()
-
     score_scale = DH ** (-0.5) * math.log2(math.e)
 
     def prepare(frame, carry):
@@ -200,13 +193,6 @@
     lax.fori_loop(0, frames // group, per_group, 0)
 
     stores = []
-    for hop in range(parts if riders else 0):
-        rides[hop].wait()
-        stores.append(
-            pltpu.make_async_copy(held.at[hop], outs[hop].at[0:riders], ride_sem.at[1, hop])
-        )
-        stores[-1].start()
-
     half = frames // 2
     kept = jnp.clip(cutoff, 0, half)
     even = [0.5 * (table[kept, at] + table[kept, at + half]) for at in range(half)]
@@ -233,7 +219,7 @@
         owner = lax.bitwise_xor(me, hop)
         stores.append(
             pltpu.make_async_copy(
-                q_in.at[pl.ds(owner * frames_dev, frames_dev)], outs[hop].at[riders], store_sem.at[hop]
+                q_in.at[pl.ds(owner * frames_dev, frames_dev)], outs[hop], store_sem.at[hop]
             )
         )
         stores[-1].start()
@@ -241,24 +227,17 @@
         copy.wait()
 
 
-def attend_head(slot, parts, scalars, table, mine, theirs, earlier, per_part):
+def attend_head(slot, parts, scalars, table, mine, theirs, per_part):
     _, frames_dev, rows, _ = mine[0].shape
     frames, tokens = frames_dev * parts, 2 * rows
     key_frames = frames // KSTRIDE
-    riders = earlier[0].shape[0] if earlier else 0
-    result = (riders + 1, frames_dev, rows, DH)
-    scratch = []
-    if riders:
-        scratch = [
-            pltpu.VMEM((parts, riders, frames_dev, rows, DH), jnp.float32),
-            pltpu.SemaphoreType.DMA((2, parts)),
-        ]
+    result = (frames_dev, rows, DH)
     flops = 12 * frames * rows * (5 + key_frames) * tokens * DH
     return pl.pallas_call(
-        functools.partial(attend_kernel, slot, parts, per_part, riders),
+        functools.partial(attend_kernel, slot, parts, per_part),
         out_shape=[jax.ShapeDtypeStruct(result, jnp.float32)] * parts,
         in_specs=[pl.BlockSpec(memory_space=pltpu.SMEM)] * 4
-        + [pl.BlockSpec(memory_space=pl.ANY)] * (2 * parts + len(earlier)),
+        + [pl.BlockSpec(memory_space=pl.ANY)] * (2 * parts),
         out_specs=[pl.BlockSpec(memory_space=pl.ANY)] * parts,
         scratch_shapes=[
             pltpu.VMEM((frames, rows, DH), jnp.float32),
@@ -273,54 +252,48 @@
             pltpu.VMEM((frames, rows, DH), jnp.float32),
             pltpu.SemaphoreType.DMA((parts, 5)),
             pltpu.SemaphoreType.DMA((parts,)),
-        ]
-        + scratch,
+        ],
         cost_estimate=pl.CostEstimate(
             flops=flops,
             bytes_accessed=6 * frames * rows * DH * 4,
             transcendentals=frames * rows * (5 + key_frames) * tokens,
         ),
         compiler_params=pltpu.CompilerParams(vmem_limit_bytes=ATTEND_VMEM),
-    )(*scalars, table, *mine, *theirs, *earlier)
-
-
-def unpack_kernel(parts, per_part, first, *refs):
-    pieces, refs = refs[:parts], refs[parts:]
-    out, held, load_sem, store_sem = refs[-4:]
-    slots = held.shape[1]
-    me = lax.axis_index("frm")
-    loads, stores = [], []
-    for hop in range(parts):
-        loads.append(pltpu.make_async_copy(pieces[hop], held.at[hop], load_sem.at[hop]))
-        loads[-1].start()
-    for hop in range(parts):
-        owner = lax.bitwise_xor(me, hop)
-        loads[hop].wait()
-        for at in range(slots):
-            columns = pl.ds(pl.multiple_of((owner * per_part + first + at) * DH, DH), DH)
-            stores.append(
-                pltpu.make_async_copy(held.at[hop, at], out.at[:, :, columns], store_sem.at[hop, at])
+    )(*scalars, table, *mine, *theirs)
+
+
+def unpack_kernel(slots, parts, *refs):
+    count = parts + 4 * slots
+    pieces, out, store_sem = refs[:count], refs[count], refs[count + 1]
+    me, core = lax.axis_index("frm"), lax.axis_index("pos")
+    stores = []
+    for at in range(count):
+        if at < parts:
+            head = 4 * slots + lax.bitwise_xor(me, at)
+            columns = pl.ds(pl.multiple_of(head * DH, DH), DH)
+        else:
+            slot, (side, flip) = (at - parts) // 4, ((1, 0), (1, 1), (0, 1), (0, 0))[(at - parts) % 4]
+            columns = head_columns(
+                slot, lax.bitwise_xor(lax.rem(me, 2), side), lax.bitwise_xor(core, flip)
             )
-            stores[-1].start()
+        stores.append(pltpu.make_async_copy(pieces[at], out.at[:, :, columns], store_sem.at[at]))
+        stores[-1].start()
     for copy in stores:
         copy.wait()
 
 
-def unpack(parts, per_part, first, pieces, channels):
-    slots, frames_dev, rows, _ = pieces[0].shape
-    operands = list(pieces)
+def unpack(slots, parts, pieces, channels):
+    frames_dev, rows, _ = pieces[0].shape
+    count = len(pieces)
     return pl.pallas_call(
-        functools.partial(unpack_kernel, parts, per_part, first),
+        functools.partial(unpack_kernel, slots, parts),
         out_shape=jax.ShapeDtypeStruct((frames_dev, rows, channels), jnp.float32),
-        in_specs=[pl.BlockSpec(memory_space=pl.ANY)] * len(operands),
+        in_specs=[pl.BlockSpec(memory_space=pltpu.VMEM)] * count,
         out_specs=pl.BlockSpec(memory_space=pl.ANY),
-        scratch_shapes=[
-            pltpu.VMEM((parts, slots, frames_dev, rows, DH), jnp.float32),
-            pltpu.SemaphoreType.DMA((parts,)),
-            pltpu.SemaphoreType.DMA((parts, slots)),
-        ],
+        scratch_shapes=[pltpu.SemaphoreType.DMA((count,))],
+        compiler_params=pltpu.CompilerParams(vmem_limit_bytes=MOVE_VMEM),
         name="unpack",
-    )(*operands)
+    )(*pieces)
 
 
 def swap_pack_kernel(slots, *refs):
@@ -363,6 +336,7 @@
             pltpu.SemaphoreType.DMA((slots, 2, 3)),
             pltpu.SemaphoreType.DMA((slots,)),
         ],
+        compiler_params=pltpu.CompilerParams(vmem_limit_bytes=FIRST_VMEM),
         name="swap_pack",
     )(queries, key_states, value_states)
 
@@ -424,6 +398,7 @@
             pltpu.SemaphoreType.DMA((2, 3, 2)),
             pltpu.SemaphoreType.DMA((3, 2)),
         ],
+        compiler_params=pltpu.CompilerParams(vmem_limit_bytes=MOVE_VMEM),
     )(queries, key_states, value_states, swapped)
     return outs[0], outs[1:3], outs[3:5]
 
@@ -686,7 +661,7 @@
         for at, span in enumerate(((others, near), (others, far), (mine, far), (mine, near))):
             stores.append(
                 pltpu.make_async_copy(
-                    local.at[slot, *span], outs[at].at[slot], store_sem.at[slot, at]
+                    local.at[slot, *span], outs[at], store_sem.at[slot, at]
                 )
             )
             stores[-1].start()
@@ -698,7 +673,7 @@
     slots = len(halves)
     frames, tokens, _ = halves[0][0].shape
     sums = passed[0].shape
-    piece = (slots, frames // 2, tokens // 2, DH)
+    piece = (frames // 2, tokens // 2, DH)
     return pl.pallas_call(
         functools.partial(mix_kernel, first, slots, top),
         out_shape=[jax.ShapeDtypeStruct(piece, jnp.float32)] * 4,
@@ -712,49 +687,8 @@
             pltpu.SemaphoreType.DMA((slots, 3)),
             pltpu.SemaphoreType.DMA((slots, 4)),
         ],
+        compiler_params=pltpu.CompilerParams(vmem_limit_bytes=MOVE_VMEM),
     )(cutoffs, *[x[1] for x in halves], *passed, *[x[0] for x in halves])
-
-
-def half_unpack_kernel(first, *refs):
-    pieces, refs = refs[:4], refs[4:]
-    out, held, load_sem, store_sem = refs[-4:]
-    slots = held.shape[1]
-    me, core = lax.axis_index("frm"), lax.axis_index("pos")
-    flips = ((1, 0), (1, 1), (0, 1), (0, 0))
-    loads, stores = [], []
-    for at in range(4):
-        loads.append(pltpu.make_async_copy(pieces[at], held.at[at], load_sem.at[at]))
-        loads[-1].start()
-    for at, (side, flip) in enumerate(flips):
-        loads[at].wait()
-        for slot in range(slots):
-            columns = head_columns(
-                first + slot, lax.bitwise_xor(lax.rem(me, 2), side), lax.bitwise_xor(core, flip)
-            )
-            stores.append(
-                pltpu.make_async_copy(
-                    held.at[at, slot], out.at[:, :, columns], store_sem.at[at, slot]
-                )
-            )
-            stores[-1].start()
-    for copy in stores:
-        copy.wait()
-
-
-def half_unpack(first, pieces, out):
-    slots, frames_dev, rows, _ = pieces[0].shape
-    return pl.pallas_call(
-        functools.partial(half_unpack_kernel, first),
-        out_shape=jax.ShapeDtypeStruct(out.shape, jnp.float32),
-        in_specs=[pl.BlockSpec(memory_space=pl.ANY)] * 5,
-        out_specs=pl.BlockSpec(memory_space=pl.ANY),
-        scratch_shapes=[
-            pltpu.VMEM((4, slots, frames_dev, rows, DH), jnp.float32),
-            pltpu.SemaphoreType.DMA((4,)),
-            pltpu.SemaphoreType.DMA((4, slots)),
-        ],
-        input_output_aliases={4: 0},
-    )(*pieces, out)
 
 
 def across(value, hop, flip, chips=None):
@@ -790,7 +724,7 @@
     theirs = []
     for hop in range(parts):
         theirs.append(swap(mine[hop]))
-    done = attend_head(4 * slots, parts, scalars, table, mine, theirs, (), 1)
+    done = attend_head(4 * slots, parts, scalars, table, mine, theirs, 1)
     landed = [done[0]] + [None] * (parts - 1)
     for hop in wires(parts):
         landed[hop] = around(done[hop], hop)
@@ -805,10 +739,7 @@
         far = across(mixed[1], 1, 1)
         other = across(mixed[2], 0, 1)
         pieces.append([near, far, other, mixed[3]])
-    out = unpack(parts, 1, 4 * slots, landed, channels)
-    for slot in range(slots):
-        out = half_unpack(slot, pieces[slot], out)
-    return out
+    return unpack(slots, parts, landed + sum(pieces, []), channels)
 
 
 def around(value, hop):

time: 173 us -> 165 us (0.954)
  Pallas kernels: 56.5 us -> 40.4 us
  waiting for transfers between devices: 73.4 us -> 86.8 us
  local copies, waits for them, and re-layouts: 8.3 us -> 1.46 us
  starting transfers between devices: 33.3 us -> 35.6 us
    ppermute x19, waiting for transfers between devices: 54.7 us -> 63.4 us  [across(): return lax.ppermute(value, ('frm', 'pos'), pairs)]
    unnamed x52 -> x20, local copies, waits for them, and re-layouts: 8.3 us -> 1.46 us
    pallas_call x2, Pallas kernels: 21.6 us -> 16.2 us  [attend_half(): pl.pallas_call(functools.partial(attend_half_kernel, slot, parts, top), o...]
    ppermute x6, waiting for transfers between devices: 18.7 us -> 23.4 us  [around(): return lax.ppermute(value, 'frm', [(i, i ^ hop) for i in range(size)])]
    pallas_call x4 -> x2, Pallas kernels: 18.9 us -> 15 us  [the longest x1 13.7 us: attend_head(): pl.pallas_call(functools.partial(attend_kernel, slot, parts, per_part), o...]
    pallas_call x2, Pallas kernels: 5.01 us -> 1.48 us  [full_pack(): pl.pallas_call(functools.partial(full_pack_kernel, slot), out_shape=[jax....]
    pallas_call x2, Pallas kernels: 6.15 us -> 2.71 us  [mix(): pl.pallas_call(functools.partial(mix_kernel, first, slots, top), out_shap...]
    ppermute x19, starting transfers between devices: 23.1 us -> 24.9 us  [across(): return lax.ppermute(value, ('frm', 'pos'), pairs)]
  transfers between devices with their start and end apart: 29 -> 29, of which waited for: 10 -> 13; matrix products, arithmetic and copies ran while one was open for 0% -> 0% of each run, Pallas kernels for 29% -> 21%
where the time goes in v3:
time: 165 us
  waiting for transfers between devices  86.8 us (53%)
  Pallas kernels  40.4 us (24%)
  starting transfers between devices  35.6 us (22%)
    ppermute x19, waiting for transfers between devices, across(): return lax.ppermute(value, ('frm', 'pos'), pairs)  63.4 us
    ppermute x19, starting transfers between devices, across(): return lax.ppermute(value, ('frm', 'pos'), pairs)  24.9 us
    ppermute x6, waiting for transfers between devices, around(): return lax.ppermute(value, 'frm', [(i, i ^ hop) for i in range(size)])  23.4 us
    pallas_call x2, Pallas kernels, attend_half(): pl.pallas_call(functools.partial(attend_half_kernel, slot, parts, top), o...  16.2 us
    pallas_call x1, Pallas kernels, attend_head(): pl.pallas_call(functools.partial(attend_kernel, slot, parts, per_part), o...  13.7 us
    ppermute x6, starting transfers between devices, around(): return lax.ppermute(value, 'frm', [(i, i ^ hop) for i in range(size)])  9.98 us
  transfers between devices with their start and end apart: 29, of which 13 were waited for; matrix products, arithmetic and copies ran while one was open for 0% of the time, Pallas kernels for 21%

profile of v3, /device:TPU:0, one launch (start us, length us, event | category | flops | bytes accessed | tf_op | source)
XLA Modules:
  0.0 164.5 jit_solution(4000911878610358193)
XLA Ops:
  0.0 2.4 %shard_map.73 = (f32[3,4,64,128]{3,2,1,0:T(8,128)}, f32[3,4,64,128]{3,2,1,0:T(8,128)}, f32[3,4,64,128]{3,2,1,0:T(8,128)}, f32[3,4,64,128]{3,2,1,0:T(8,128)}) custom-call(f32[4,64,1536]{2,1,0:T(8,128)} %refs_2_.8, f32[4,64,1536]{2,1,0:T(8,128)} %refs_3_.2, f32[4,64,1536]{2,1,0:T(8,128)} %refs_4_.1), custom_call_target="tpu_custom_call" | custom-call | bytes 3145728 | tf_op jit(solution)/shard_map/pallas_call | solution.py:64
  2.4 2.6 %swap_pack.1 = f32[2,2,3,4,64,128]{5,4,3,2,1,0:T(8,128)} custom-call(f32[4,64,1536]{2,1,0:T(8,128)} %refs_2_.8, f32[4,64,1536]{2,1,0:T(8,128)} %refs_3_.2, f32[4,64,1536]{2,1,0:T(8,128)} %refs_4_.1), custom_call_target="tpu_custom_call" | custom-call | tf_op jit(solution)/shard_map/swap_pack/pallas_call | solution.py:329
  5.0 0.6 collective-permute-start.10
  5.6 2.6 %collective-permute-start = (f32[3,4,64,128]{3,2,1,0:T(8,128)}, f32[3,4,64,128]{3,2,1,0:T(8,128)S(1)}, u32[]{:S(2)}, u32[]{:S(2)}) collective-permute-start(f32[3,4,64,128]{3,2,1,0:T(8,128)} %get-tuple-element.47), channel_id=1, source_target_pairs={{0,4},{4,0},{8,12},{12,8},{1,5},{5,1},{9,13},{13,9},{2,6},{6,2},{1... | collective-permute-start | bytes 1179656 | tf_op jit(solution)/shard_map/ppermute | solution.py:747
  8.2 2.6 %collective-permute-start.1 = (f32[3,4,64,128]{3,2,1,0:T(8,128)}, f32[3,4,64,128]{3,2,1,0:T(8,128)S(1)}, u32[]{:S(2)}, u32[]{:S(2)}) collective-permute-start(f32[3,4,64,128]{3,2,1,0:T(8,128)} %get-tuple-element.48), channel_id=1, source_target_pairs={{0,8},{4,12},{8,0},{12,4},{1,9},{5,13},{9,1},{13,5},{2,10},{6,14},... | collective-permute-start | bytes 1179656 | tf_op jit(solution)/shard_map/ppermute | solution.py:747
  10.9 1.4 copy-done.2
  12.3 0.7 shard_map.78
  13.1 1.0 collective-permute-start.20
  14.1 0.7 shard_map.75
  14.8 1.2 collective-permute-start.11
  16.0 10.4 %collective-permute-done.refs_5_ = f32[3,4,64,128]{3,2,1,0:T(8,128)S(1)} collective-permute-done((f32[3,4,64,128]{3,2,1,0:T(8,128)}, f32[3,4,64,128]{3,2,1,0:T(8,128)S(1)}, u32[]{:S(2)}, u32[]{:S(2)}) %collective-permute-start) | collective-permute-done | bytes 393248 | tf_op jit(solution)/shard_map/ppermute | solution.py:747
  26.4 1.5 collective-permute-start.21
  27.8 10.4 %collective-permute-done.1.refs_6_ = f32[3,4,64,128]{3,2,1,0:T(8,128)S(1)} collective-permute-done((f32[3,4,64,128]{3,2,1,0:T(8,128)}, f32[3,4,64,128]{3,2,1,0:T(8,128)S(1)}, u32[]{:S(2)}, u32[]{:S(2)}) %collective-permute-start.1) | collective-permute-done | bytes 393248 | tf_op jit(solution)/shard_map/ppermute | solution.py:747
  38.3 2.5 %collective-permute-start.22 = (f32[2,1,128,128]{3,2,1,0:T(8,128)S(1)}, f32[2,1,128,128]{3,2,1,0:T(8,128)S(1)}, u32[]{:S(2)}, u32[]{:S(2)}) collective-permute-start(f32[2,1,128,128]{3,2,1,0:T(8,128)S(1)} %get-tuple-element.70), channel_id=1, source_target_pairs={{0,12},{1,13},{4,8},{5,9},{8,4},{9,5},{12,0},{13,1},{2,14},{3,15},... | collective-permute-start | bytes 393224 | tf_op jit(solution)/shard_map/ppermute | solution.py:697
  40.8 1.3 collective-permute-start.23
  42.0 29.4 %collective-permute-done.21.refs_7_ = f32[2,1,128,128]{3,2,1,0:T(8,128)S(1)} collective-permute-done((f32[2,1,128,128]{3,2,1,0:T(8,128)S(1)}, f32[2,1,128,128]{3,2,1,0:T(8,128)S(1)}, u32[]{:S(2)}, u32[]{:S(2)}) %collective-permute-start.21) | collective-permute-done | bytes 131104 | tf_op jit(solution)/shard_map/ppermute | solution.py:697
  71.4 3.4 %collective-permute-start.12 = (f32[2,1,128,128]{3,2,1,0:T(8,128)S(1)}, f32[2,1,128,128]{3,2,1,0:T(8,128)S(1)}, u32[]{:S(2)}, u32[]{:S(2)}) collective-permute-start(f32[2,1,128,128]{3,2,1,0:T(8,128)S(1)} %get-tuple-element.58), channel_id=1, source_target_pairs={{0,8},{1,9},{4,12},{5,13},{8,0},{9,1},{12,4},{13,5},{2,10},{3,11},... | collective-permute-start | bytes 393224 | tf_op jit(solution)/shard_map/ppermute | solution.py:697
  74.8 2.0 %collective-permute-done.22.refs_8_ = f32[2,1,128,128]{3,2,1,0:T(8,128)S(1)} collective-permute-done((f32[2,1,128,128]{3,2,1,0:T(8,128)S(1)}, f32[2,1,128,128]{3,2,1,0:T(8,128)S(1)}, u32[]{:S(2)}, u32[]{:S(2)}) %collective-permute-start.22) | collective-permute-done | bytes 131104 | tf_op jit(solution)/shard_map/ppermute | solution.py:697
  76.8 1.3 collective-permute-start.13
  78.2 7.1 %collective-permute-done.12.refs_7_ = f32[2,1,128,128]{3,2,1,0:T(8,128)S(1)} collective-permute-done((f32[2,1,128,128]{3,2,1,0:T(8,128)S(1)}, f32[2,1,128,128]{3,2,1,0:T(8,128)S(1)}, u32[]{:S(2)}, u32[]{:S(2)}) %collective-permute-start.12) | collective-permute-done | bytes 131104 | tf_op jit(solution)/shard_map/ppermute | solution.py:697
  85.2 0.7 collective-permute-start.24
  85.9 1.3 collective-permute-start.14
  87.2 0.7 collective-permute-start.15
  87.9 0.1 collective-permute-start.3
  88.0 12.0 %collective-permute-done.14.refs_9_ = f32[2,2,128,128]{3,2,1,0:T(8,128)S(1)} collective-permute-done((f32[2,2,128,128]{3,2,1,0:T(8,128)S(1)}, f32[2,2,128,128]{3,2,1,0:T(8,128)S(1)}, u32[]{:S(2)}, u32[]{:S(2)}) %collective-permute-start.14) | collective-permute-done | bytes 262176 | tf_op jit(solution)/shard_map/ppermute | solution.py:697
  100.0 0.5 collective-permute-start.5
  100.5 0.1 collective-permute-start.6
  100.6 8.1 %shard_map.79 = (f32[8,128,128]{2,1,0:T(8,128)S(1)}, f32[5,128,128]{2,1,0:T(8,128)S(1)}) custom-call(s32[12]{0:T(128)S(1)} %copy-done.4, s32[12]{0:T(128)S(1)} %copy-done.5, f32[4,64,1536]{2,1,0:T(8,128)S(1)} %copy-done, f32[4,64,1536]{2,1,0:T(8,128)S(1)} %copy-done.1, f32[4,64,1536]{2,1,0:T(8,128)S(1)} %copy-done.3, ...), custom_call_target="tpu_custom_call" | custom-call | flops 2013265920 | bytes 3145728 | tf_op jit(solution)/shard_map/pallas_call | solution.py:583
  108.7 6.0 %collective-permute-start.25 = (f32[5,128,128]{2,1,0:T(8,128)S(1)}, f32[5,128,128]{2,1,0:T(8,128)S(1)}, u32[]{:S(2)}, u32[]{:S(2)}) collective-permute-start(f32[5,128,128]{2,1,0:T(8,128)S(1)} %get-tuple-element.73.refs_1_), channel_id=1, source_target_pairs={{0,8},{1,9},{4,12},{5,13},{8,0},{9,1},{12,4},{13,5},{2,10},{3,11},... | collective-permute-start | bytes 983048 | tf_op jit(solution)/shard_map/ppermute | solution.py:697
  114.8 8.1 %shard_map.76 = (f32[8,128,128]{2,1,0:T(8,128)S(1)}, f32[5,128,128]{2,1,0:T(8,128)S(1)}) custom-call(s32[12]{0:T(128)S(1)} %copy-done.4, s32[12]{0:T(128)S(1)} %copy-done.5, f32[4,64,1536]{2,1,0:T(8,128)S(1)} %copy-done, f32[4,64,1536]{2,1,0:T(8,128)S(1)} %copy-done.1, f32[4,64,1536]{2,1,0:T(8,128)S(1)} %copy-done.3, ...), custom_call_target="tpu_custom_call" | custom-call | flops 2013265920 | bytes 3145728 | tf_op jit(solution)/shard_map/pallas_call | solution.py:583
  122.9 0.1 collective-permute-start.16
  123.0 13.7 %shard_map.74 = (f32[4,64,128]{2,1,0:T(8,128)S(1)}, f32[4,64,128]{2,1,0:T(8,128)S(1)}, f32[4,64,128]{2,1,0:T(8,128)S(1)}, f32[4,64,128]{2,1,0:T(8,128)S(1)}) custom-call(s32[12]{0:T(128)S(1)} %copy-done.4, s32[12]{0:T(128)S(1)} %copy-done.5, s32[12]{0:T(128)S(1)} %copy-done.6, f32[9,16]{1,0:T(8,128)S(1)} %copy-done.8, f32[3,4,64,128]{3,2,1,0:T(8,128)S(1)} %copy-done.7, ...), custom_call_target="tpu_custom_call" | custom-call | flops 1811939328 | bytes 3145728 | tf_op jit(solution)/shard_map/pallas_call | solution.py:236
  136.8 2.3 %collective-permute-start.7 = (f32[4,64,128]{2,1,0:T(8,128)S(1)}, f32[4,64,128]{2,1,0:T(8,128)S(1)}, u32[]{:S(2)}, u32[]{:S(2)}) collective-permute-start(f32[4,64,128]{2,1,0:T(8,128)S(1)} %get-tuple-element.51), channel_id=1, source_target_pairs={{0,4},{4,0},{8,12},{12,8},{1,5},{5,1},{9,13},{13,9},{2,6},{6,2},{1... | collective-permute-start | bytes 393224 | tf_op jit(solution)/shard_map/ppermute | solution.py:747
  139.1 0.7 collective-permute-start.8
  139.8 1.7 %collective-permute-start.9 = (f32[4,64,128]{2,1,0:T(8,128)S(1)}, f32[4,64,128]{2,1,0:T(8,128)S(1)}, u32[]{:S(2)}, u32[]{:S(2)}) collective-permute-start(f32[4,64,128]{2,1,0:T(8,128)S(1)} %get-tuple-element.53), channel_id=1, source_target_pairs={{0,12},{4,8},{8,4},{12,0},{1,13},{5,9},{9,5},{13,1},{2,14},{6,10},... | collective-permute-start | bytes 393224 | tf_op jit(solution)/shard_map/ppermute | solution.py:747
  141.5 1.4 shard_map.80
  142.9 1.1 collective-permute-start.26
  144.0 4.9 %collective-permute-done.16.refs_2_ = f32[5,128,128]{2,1,0:T(8,128)S(1)} collective-permute-done((f32[5,128,128]{2,1,0:T(8,128)S(1)}, f32[5,128,128]{2,1,0:T(8,128)S(1)}, u32[]{:S(2)}, u32[]{:S(2)}) %collective-permute-start.16) | collective-permute-done | bytes 327712 | tf_op jit(solution)/shard_map/ppermute | solution.py:697
  148.9 1.4 shard_map.77
  150.3 1.3 collective-permute-done.7.refs_1_
  151.7 1.2 collective-permute-done.8.refs_2_
  152.9 1.8 %collective-permute-start.18 = (f32[4,64,128]{2,1,0:T(8,128)S(1)}, f32[4,64,128]{2,1,0:T(8,128)S(1)}, u32[]{:S(2)}, u32[]{:S(2)}) collective-permute-start(f32[4,64,128]{2,1,0:T(8,128)S(1)} %get-tuple-element.65), channel_id=1, source_target_pairs={{0,5},{1,4},{4,1},{5,0},{8,13},{9,12},{12,9},{13,8},{2,7},{3,6},{6... | collective-permute-start | bytes 393224 | tf_op jit(solution)/shard_map/ppermute | solution.py:697
  154.7 0.4 collective-permute-done.26.refs_8_
  155.1 0.6 collective-permute-start.19
  155.7 2.0 %collective-permute-done.27.refs_9_ = f32[4,64,128]{2,1,0:T(8,128)S(1)} collective-permute-done((f32[4,64,128]{2,1,0:T(8,128)S(1)}, f32[4,64,128]{2,1,0:T(8,128)S(1)}, u32[]{:S(2)}, u32[]{:S(2)}) %collective-permute-start.27) | collective-permute-done | bytes 131104 | tf_op jit(solution)/shard_map/ppermute | solution.py:697
  157.7 3.0 %collective-permute-done.17.refs_4_ = f32[4,64,128]{2,1,0:T(8,128)S(1)} collective-permute-done((f32[4,64,128]{2,1,0:T(8,128)S(1)}, f32[4,64,128]{2,1,0:T(8,128)S(1)}, u32[]{:S(2)}, u32[]{:S(2)}) %collective-permute-start.17) | collective-permute-done | bytes 131104 | tf_op jit(solution)/shard_map/ppermute | solution.py:697
  160.7 2.6 %collective-permute-done.18.refs_5_ = f32[4,64,128]{2,1,0:T(8,128)S(1)} collective-permute-done((f32[4,64,128]{2,1,0:T(8,128)S(1)}, f32[4,64,128]{2,1,0:T(8,128)S(1)}, u32[]{:S(2)}, u32[]{:S(2)}) %collective-permute-start.18) | collective-permute-done | bytes 131104 | tf_op jit(solution)/shard_map/ppermute | solution.py:697
  163.3 1.2 unpack.1
  (40 shorter events, 0.1 us)
Async XLA Ops:
  2.4 8.5 %copy-start.9 = (f32[3,4,64,128]{3,2,1,0:T(8,128)S(1)}, f32[3,4,64,128]{3,2,1,0:T(8,128)}, u32[]{:S(2)}) copy-start(f32[3,4,64,128]{3,2,1,0:T(8,128)} %get-tuple-element.49) | copy-start | bytes 1179652
  2.4 8.5 %copy-start = (f32[4,64,1536]{2,1,0:T(8,128)S(1)}, f32[4,64,1536]{2,1,0:T(8,128)}, u32[]{:S(2)}) copy-start(f32[4,64,1536]{2,1,0:T(8,128)} %refs_2_.8) | copy-start | bytes 4718596
  2.4 8.5 %copy-start.1 = (f32[4,64,1536]{2,1,0:T(8,128)S(1)}, f32[4,64,1536]{2,1,0:T(8,128)}, u32[]{:S(2)}) copy-start(f32[4,64,1536]{2,1,0:T(8,128)} %refs_3_.2) | copy-start | bytes 4718596
  5.0 5.8 %collective-permute-start.10 = (f32[2,2,3,4,64,128]{5,4,3,2,1,0:T(8,128)}, f32[2,2,3,4,64,128]{5,4,3,2,1,0:T(8,128)S(1)}, u32[]{:S(2)}, u32[]{:S(2)}) collective-permute-start(f32[2,2,3,4,64,128]{5,4,3,2,1,0:T(8,128)} %swap_pack.1), channel_id=1, source_target_pairs={{0,1},{1,0},{4,5},{5,4},{8,9},{9,8},{12,13},{13,12},{2,3},{3,2},{6... | collective-permute-start | bytes 4718600 | tf_op jit(solution)/shard_map/ppermute | solution.py:697
  5.6 20.8 %collective-permute-start = (f32[3,4,64,128]{3,2,1,0:T(8,128)}, f32[3,4,64,128]{3,2,1,0:T(8,128)S(1)}, u32[]{:S(2)}, u32[]{:S(2)}) collective-permute-start(f32[3,4,64,128]{3,2,1,0:T(8,128)} %get-tuple-element.47), channel_id=1, source_target_pairs={{0,4},{4,0},{8,12},{12,8},{1,5},{5,1},{9,13},{13,9},{2,6},{6,2},{1... | collective-permute-start | bytes 1179656 | tf_op jit(solution)/shard_map/ppermute | solution.py:747
  8.2 30.0 %collective-permute-start.1 = (f32[3,4,64,128]{3,2,1,0:T(8,128)}, f32[3,4,64,128]{3,2,1,0:T(8,128)S(1)}, u32[]{:S(2)}, u32[]{:S(2)}) collective-permute-start(f32[3,4,64,128]{3,2,1,0:T(8,128)} %get-tuple-element.48), channel_id=1, source_target_pairs={{0,8},{4,12},{8,0},{12,4},{1,9},{5,13},{9,1},{13,5},{2,10},{6,14},... | collective-permute-start | bytes 1179656 | tf_op jit(solution)/shard_map/ppermute | solution.py:747
  10.8 29.9 %collective-permute-start.2 = (f32[3,4,64,128]{3,2,1,0:T(8,128)S(1)}, f32[3,4,64,128]{3,2,1,0:T(8,128)S(1)}, u32[]{:S(2)}, u32[]{:S(2)}) collective-permute-start(f32[3,4,64,128]{3,2,1,0:T(8,128)S(1)} %copy-done.9), channel_id=1, source_target_pairs={{0,12},{4,8},{8,4},{12,0},{1,13},{5,9},{9,5},{13,1},{2,14},{6,10},... | collective-permute-start | bytes 1179656 | tf_op jit(solution)/shard_map/ppermute | solution.py:747
  10.9 1.4 copy-start.2
  13.0 74.9 %copy-start.7 = (f32[3,4,64,128]{3,2,1,0:T(8,128)S(1)}, f32[3,4,64,128]{3,2,1,0:T(8,128)}, u32[]{:S(2)}) copy-start(f32[3,4,64,128]{3,2,1,0:T(8,128)} %get-tuple-element.46.refs_4_) | copy-start | bytes 1179652
  13.0 87.5 %copy-start.3 = (f32[4,64,1536]{2,1,0:T(8,128)S(1)}, f32[4,64,1536]{2,1,0:T(8,128)}, u32[]{:S(2)}) copy-start(f32[4,64,1536]{2,1,0:T(8,128)} %refs_4_.1) | copy-start | bytes 4718596
  13.0 87.5 %copy-start.4 = (s32[12]{0:T(128)S(1)}, s32[12]{0:T(128)}, u32[]{:S(2)}) copy-start(s32[12]{0:T(128)} %refs_0_.13) | copy-start | bytes 148
  13.1 87.5 %copy-start.5 = (s32[12]{0:T(128)S(1)}, s32[12]{0:T(128)}, u32[]{:S(2)}) copy-start(s32[12]{0:T(128)} %refs_1_.10) | copy-start | bytes 148
  13.1 87.4 %collective-permute-start.20 = (f32[3,4,128,128]{3,2,1,0:T(8,128)S(1)}, f32[3,4,128,128]{3,2,1,0:T(8,128)S(1)}, u32[]{:S(2)}, u32[]{:S(2)}) collective-permute-start(f32[3,4,128,128]{3,2,1,0:T(8,128)S(1)} %get-tuple-element.68), channel_id=1, source_target_pairs={{0,4},{1,5},{4,0},{5,1},{8,12},{9,13},{12,8},{13,9},{2,6},{3,7},{6... | collective-permute-start | bytes 2359304 | tf_op jit(solution)/shard_map/ppermute | solution.py:697
  14.8 93.9 %collective-permute-start.11 = (f32[3,4,128,128]{3,2,1,0:T(8,128)S(1)}, f32[3,4,128,128]{3,2,1,0:T(8,128)S(1)}, u32[]{:S(2)}, u32[]{:S(2)}) collective-permute-start(f32[3,4,128,128]{3,2,1,0:T(8,128)S(1)} %get-tuple-element.57), channel_id=1, source_target_pairs={{0,4},{1,5},{4,0},{5,1},{8,12},{9,13},{12,8},{13,9},{2,6},{3,7},{6... | collective-permute-start | bytes 2359304 | tf_op jit(solution)/shard_map/ppermute | solution.py:697
  26.4 45.0 %collective-permute-start.21 = (f32[2,1,128,128]{3,2,1,0:T(8,128)S(1)}, f32[2,1,128,128]{3,2,1,0:T(8,128)S(1)}, u32[]{:S(2)}, u32[]{:S(2)}) collective-permute-start(f32[2,1,128,128]{3,2,1,0:T(8,128)S(1)} %get-tuple-element.69), channel_id=1, source_target_pairs={{0,8},{1,9},{4,12},{5,13},{8,0},{9,1},{12,4},{13,5},{2,10},{3,11},... | collective-permute-start | bytes 393224 | tf_op jit(solution)/shard_map/ppermute | solution.py:697
  38.3 38.5 %collective-permute-start.22 = (f32[2,1,128,128]{3,2,1,0:T(8,128)S(1)}, f32[2,1,128,128]{3,2,1,0:T(8,128)S(1)}, u32[]{:S(2)}, u32[]{:S(2)}) collective-permute-start(f32[2,1,128,128]{3,2,1,0:T(8,128)S(1)} %get-tuple-element.70), channel_id=1, source_target_pairs={{0,12},{1,13},{4,8},{5,9},{8,4},{9,5},{12,0},{13,1},{2,14},{3,15},... | collective-permute-start | bytes 393224 | tf_op jit(solution)/shard_map/ppermute | solution.py:697
  40.8 46.5 %collective-permute-start.23 = (f32[2,2,128,128]{3,2,1,0:T(8,128)S(1)}, f32[2,2,128,128]{3,2,1,0:T(8,128)S(1)}, u32[]{:S(2)}, u32[]{:S(2)}) collective-permute-start(f32[2,2,128,128]{3,2,1,0:T(8,128)S(1)} %get-tuple-element.71), channel_id=1, source_target_pairs={{4,12},{5,13},{8,0},{9,1},{6,14},{7,15},{10,2},{11,3},{20,28},{21,... | collective-permute-start | bytes 786440 | tf_op jit(solution)/shard_map/ppermute | solution.py:697
  71.4 13.8 %collective-permute-start.12 = (f32[2,1,128,128]{3,2,1,0:T(8,128)S(1)}, f32[2,1,128,128]{3,2,1,0:T(8,128)S(1)}, u32[]{:S(2)}, u32[]{:S(2)}) collective-permute-start(f32[2,1,128,128]{3,2,1,0:T(8,128)S(1)} %get-tuple-element.58), channel_id=1, source_target_pairs={{0,8},{1,9},{4,12},{5,13},{8,0},{9,1},{12,4},{13,5},{2,10},{3,11},... | collective-permute-start | bytes 393224 | tf_op jit(solution)/shard_map/ppermute | solution.py:697
  76.8 9.1 %collective-permute-start.13 = (f32[2,1,128,128]{3,2,1,0:T(8,128)S(1)}, f32[2,1,128,128]{3,2,1,0:T(8,128)S(1)}, u32[]{:S(2)}, u32[]{:S(2)}) collective-permute-start(f32[2,1,128,128]{3,2,1,0:T(8,128)S(1)} %get-tuple-element.59), channel_id=1, source_target_pairs={{0,12},{1,13},{4,8},{5,9},{8,4},{9,5},{12,0},{13,1},{2,14},{3,15},... | collective-permute-start | bytes 393224 | tf_op jit(solution)/shard_map/ppermute | solution.py:697
  85.2 2.7 %collective-permute-start.24 = (f32[2,2,128,128]{3,2,1,0:T(8,128)S(1)}, f32[2,2,128,128]{3,2,1,0:T(8,128)S(1)}, u32[]{:S(2)}, u32[]{:S(2)}) collective-permute-start(f32[2,2,128,128]{3,2,1,0:T(8,128)S(1)} %get-tuple-element.72), channel_id=1, source_target_pairs={{4,8},{5,9},{8,4},{9,5},{6,10},{7,11},{10,6},{11,7},{20,24},{21,25... | collective-permute-start | bytes 786440 | tf_op jit(solution)/shard_map/ppermute | solution.py:697
  85.9 14.1 %collective-permute-start.14 = (f32[2,2,128,128]{3,2,1,0:T(8,128)S(1)}, f32[2,2,128,128]{3,2,1,0:T(8,128)S(1)}, u32[]{:S(2)}, u32[]{:S(2)}) collective-permute-start(f32[2,2,128,128]{3,2,1,0:T(8,128)S(1)} %get-tuple-element.60), channel_id=1, source_target_pairs={{4,12},{5,13},{8,0},{9,1},{6,14},{7,15},{10,2},{11,3},{20,28},{21,... | collective-permute-start | bytes 786440 | tf_op jit(solution)/shard_map/ppermute | solution.py:697
  87.2 12.8 %collective-permute-start.15 = (f32[2,2,128,128]{3,2,1,0:T(8,128)S(1)}, f32[2,2,128,128]{3,2,1,0:T(8,128)S(1)}, u32[]{:S(2)}, u32[]{:S(2)}) collective-permute-start(f32[2,2,128,128]{3,2,1,0:T(8,128)S(1)} %get-tuple-element.61), channel_id=1, source_target_pairs={{4,8},{5,9},{8,4},{9,5},{6,10},{7,11},{10,6},{11,7},{20,24},{21,25... | collective-permute-start | bytes 786440 | tf_op jit(solution)/shard_map/ppermute | solution.py:697
  87.9 35.0 %collective-permute-start.3 = (f32[3,4,64,128]{3,2,1,0:T(8,128)S(1)}, f32[3,4,64,128]{3,2,1,0:T(8,128)S(1)}, u32[]{:S(2)}, u32[]{:S(2)}) collective-permute-start(f32[3,4,64,128]{3,2,1,0:T(8,128)S(1)} %copy-done.7), channel_id=1, source_target_pairs={{0,1},{1,0},{2,3},{3,2},{4,5},{5,4},{6,7},{7,6},{8,9},{9,8},{10,11... | collective-permute-start | bytes 1179656 | tf_op jit(solution)/shard_map/ppermute | solution.py:752
  100.0 23.0 %collective-permute-start.4 = (f32[3,4,64,128]{3,2,1,0:T(8,128)S(1)}, f32[3,4,64,128]{3,2,1,0:T(8,128)S(1)}, u32[]{:S(2)}, u32[]{:S(2)}) collective-permute-start(f32[3,4,64,128]{3,2,1,0:T(8,128)S(1)} %collective-permute-done.refs_5_), channel_id=1, source_target_pairs={{0,1},{1,0},{2,3},{3,2},{4,5},{5,4},{6,7},{7,6},{8,9},{9,8},{10,11... | collective-permute-start | bytes 1179656 | tf_op jit(solution)/shard_map/ppermute | solution.py:752
  100.0 23.0 %collective-permute-start.5 = (f32[3,4,64,128]{3,2,1,0:T(8,128)S(1)}, f32[3,4,64,128]{3,2,1,0:T(8,128)S(1)}, u32[]{:S(2)}, u32[]{:S(2)}) collective-permute-start(f32[3,4,64,128]{3,2,1,0:T(8,128)S(1)} %collective-permute-done.1.refs_6_), channel_id=1, source_target_pairs={{0,1},{1,0},{2,3},{3,2},{4,5},{5,4},{6,7},{7,6},{8,9},{9,8},{10,11... | collective-permute-start | bytes 1179656 | tf_op jit(solution)/shard_map/ppermute | solution.py:752
  100.5 22.5 %collective-permute-start.6 = (f32[3,4,64,128]{3,2,1,0:T(8,128)S(1)}, f32[3,4,64,128]{3,2,1,0:T(8,128)S(1)}, u32[]{:S(2)}, u32[]{:S(2)}) collective-permute-start(f32[3,4,64,128]{3,2,1,0:T(8,128)S(1)} %collective-permute-done.2.refs_7_), channel_id=1, source_target_pairs={{0,1},{1,0},{2,3},{3,2},{4,5},{5,4},{6,7},{7,6},{8,9},{9,8},{10,11... | collective-permute-start | bytes 1179656 | tf_op jit(solution)/shard_map/ppermute | solution.py:752
  108.7 14.3 %copy-start.6 = (s32[12]{0:T(128)S(1)}, s32[12]{0:T(128)}, u32[]{:S(2)}) copy-start(s32[12]{0:T(128)} %refs_0_.14) | copy-start | bytes 148
  108.7 14.3 %copy-start.8 = (f32[9,16]{1,0:T(8,128)S(1)}, f32[9,16]{1,0:T(8,128)}, u32[]{:S(2)}) copy-start(f32[9,16]{1,0:T(8,128)} %constant.2.clone.refs_3_) | copy-start | bytes 1732
  108.7 32.8 %collective-permute-start.25 = (f32[5,128,128]{2,1,0:T(8,128)S(1)}, f32[5,128,128]{2,1,0:T(8,128)S(1)}, u32[]{:S(2)}, u32[]{:S(2)}) collective-permute-start(f32[5,128,128]{2,1,0:T(8,128)S(1)} %get-tuple-element.73.refs_1_), channel_id=1, source_target_pairs={{0,8},{1,9},{4,12},{5,13},{8,0},{9,1},{12,4},{13,5},{2,10},{3,11},... | collective-permute-start | bytes 983048 | tf_op jit(solution)/shard_map/ppermute | solution.py:697
  122.9 26.1 %collective-permute-start.16 = (f32[5,128,128]{2,1,0:T(8,128)S(1)}, f32[5,128,128]{2,1,0:T(8,128)S(1)}, u32[]{:S(2)}, u32[]{:S(2)}) collective-permute-start(f32[5,128,128]{2,1,0:T(8,128)S(1)} %get-tuple-element.62.refs_1_), channel_id=1, source_target_pairs={{0,8},{1,9},{4,12},{5,13},{8,0},{9,1},{12,4},{13,5},{2,10},{3,11},... | collective-permute-start | bytes 983048 | tf_op jit(solution)/shard_map/ppermute | solution.py:697
  136.8 14.9 %collective-permute-start.7 = (f32[4,64,128]{2,1,0:T(8,128)S(1)}, f32[4,64,128]{2,1,0:T(8,128)S(1)}, u32[]{:S(2)}, u32[]{:S(2)}) collective-permute-start(f32[4,64,128]{2,1,0:T(8,128)S(1)} %get-tuple-element.51), channel_id=1, source_target_pairs={{0,4},{4,0},{8,12},{12,8},{1,5},{5,1},{9,13},{13,9},{2,6},{6,2},{1... | collective-permute-start | bytes 393224 | tf_op jit(solution)/shard_map/ppermute | solution.py:747
  139.1 13.8 %collective-permute-start.8 = (f32[4,64,128]{2,1,0:T(8,128)S(1)}, f32[4,64,128]{2,1,0:T(8,128)S(1)}, u32[]{:S(2)}, u32[]{:S(2)}) collective-permute-start(f32[4,64,128]{2,1,0:T(8,128)S(1)} %get-tuple-element.52), channel_id=1, source_target_pairs={{0,8},{4,12},{8,0},{12,4},{1,9},{5,13},{9,1},{13,5},{2,10},{6,14},... | collective-permute-start | bytes 393224 | tf_op jit(solution)/shard_map/ppermute | solution.py:747
  139.8 13.1 %collective-permute-start.9 = (f32[4,64,128]{2,1,0:T(8,128)S(1)}, f32[4,64,128]{2,1,0:T(8,128)S(1)}, u32[]{:S(2)}, u32[]{:S(2)}) collective-permute-start(f32[4,64,128]{2,1,0:T(8,128)S(1)} %get-tuple-element.53), channel_id=1, source_target_pairs={{0,12},{4,8},{8,4},{12,0},{1,13},{5,9},{9,5},{13,1},{2,14},{6,10},... | collective-permute-start | bytes 393224 | tf_op jit(solution)/shard_map/ppermute | solution.py:747
  142.9 12.2 %collective-permute-start.26 = (f32[4,64,128]{2,1,0:T(8,128)S(1)}, f32[4,64,128]{2,1,0:T(8,128)S(1)}, u32[]{:S(2)}, u32[]{:S(2)}) collective-permute-start(f32[4,64,128]{2,1,0:T(8,128)S(1)} %get-tuple-element.75), channel_id=1, source_target_pairs={{0,4},{1,5},{4,0},{5,1},{8,12},{9,13},{12,8},{13,9},{2,6},{3,7},{6... | collective-permute-start | bytes 393224 | tf_op jit(solution)/shard_map/ppermute | solution.py:697
  148.9 8.7 %collective-permute-start.27 = (f32[4,64,128]{2,1,0:T(8,128)S(1)}, f32[4,64,128]{2,1,0:T(8,128)S(1)}, u32[]{:S(2)}, u32[]{:S(2)}) collective-permute-start(f32[4,64,128]{2,1,0:T(8,128)S(1)} %get-tuple-element.76), channel_id=1, source_target_pairs={{0,5},{1,4},{4,1},{5,0},{8,13},{9,12},{12,9},{13,8},{2,7},{3,6},{6... | collective-permute-start | bytes 393224 | tf_op jit(solution)/shard_map/ppermute | solution.py:697
  151.7 6.0 %collective-permute-start.28 = (f32[4,64,128]{2,1,0:T(8,128)S(1)}, f32[4,64,128]{2,1,0:T(8,128)S(1)}, u32[]{:S(2)}, u32[]{:S(2)}) collective-permute-start(f32[4,64,128]{2,1,0:T(8,128)S(1)} %get-tuple-element.77), channel_id=1, source_target_pairs={{0,1},{1,0},{4,5},{5,4},{8,9},{9,8},{12,13},{13,12},{2,3},{3,2},{6... | collective-permute-start | bytes 393224 | tf_op jit(solution)/shard_map/ppermute | solution.py:697
  152.9 7.8 %collective-permute-start.17 = (f32[4,64,128]{2,1,0:T(8,128)S(1)}, f32[4,64,128]{2,1,0:T(8,128)S(1)}, u32[]{:S(2)}, u32[]{:S(2)}) collective-permute-start(f32[4,64,128]{2,1,0:T(8,128)S(1)} %get-tuple-element.64), channel_id=1, source_target_pairs={{0,4},{1,5},{4,0},{5,1},{8,12},{9,13},{12,8},{13,9},{2,6},{3,7},{6... | collective-permute-start | bytes 393224 | tf_op jit(solution)/shard_map/ppermute | solution.py:697
  152.9 10.4 %collective-permute-start.18 = (f32[4,64,128]{2,1,0:T(8,128)S(1)}, f32[4,64,128]{2,1,0:T(8,128)S(1)}, u32[]{:S(2)}, u32[]{:S(2)}) collective-permute-start(f32[4,64,128]{2,1,0:T(8,128)S(1)} %get-tuple-element.65), channel_id=1, source_target_pairs={{0,5},{1,4},{4,1},{5,0},{8,13},{9,12},{12,9},{13,8},{2,7},{3,6},{6... | collective-permute-start | bytes 393224 | tf_op jit(solution)/shard_map/ppermute | solution.py:697
  155.1 8.2 %collective-permute-start.19 = (f32[4,64,128]{2,1,0:T(8,128)S(1)}, f32[4,64,128]{2,1,0:T(8,128)S(1)}, u32[]{:S(2)}, u32[]{:S(2)}) collective-permute-start(f32[4,64,128]{2,1,0:T(8,128)S(1)} %get-tuple-element.66), channel_id=1, source_target_pairs={{0,1},{1,0},{4,5},{5,4},{8,9},{9,8},{12,13},{13,12},{2,3},{3,2},{6... | collective-permute-start | bytes 393224 | tf_op jit(solution)/shard_map/ppermute | solution.py:697
